TPU v7x, 32 devices: a whole 2x2x4 slice. The times are simulated.
32 devices in a mesh: los: 2 (over x), sky: 16 (over z, y, core).
Axes of the slice: x: 2, y: 2, z: 4, core: 2. Of those that a mesh axis runs over, the one named last changes fastest.
Arguments:
- density: bfloat16 [16, 2048, 2048], P('los', 'sky'), may hold values from 0.1 to 10
- refine: int32 [2, 256, 256], P('los', 'sky'), may hold values from 0 to 1, as said below
- weight_low: float32 [16], P('los'), may hold values from 0.1 to 0.5
- weight_high: float32 [16], P('los'), may hold values from 0.6 to 3
Outputs:
- deflection_x: float32 [2048, 2048], P('sky', 'los')
- deflection_y: float32 [2048, 2048], P('sky', 'los')
Inputs may be any that keep to these rules, and one draw needn't show every extreme that they name: `refine`: the blocks of one slab and one sky column (one index of los and of sky) hold at most 1024 refined blocks, and in every draw some slab and column holds exactly 1024.
All inputs are finite; a program needn't handle non-finite values.
Results may differ from a plain program's by a relative error of at most 0.0003.
Values may be sent and summed in bfloat16 or wider, within the bound.
A program may use at most 128 MiB of HBM per device.

v0:
```python
import math

import jax
import jax.numpy as jnp
from jax import lax
from jax.sharding import PartitionSpec as P

highest = lax.Precision.HIGHEST


def padded(cells, sides, width):
    for axis, dim in sides:
        count = lax.axis_size(axis)
        head = lax.slice_in_dim(cells, 0, width, axis=dim)
        tail = lax.slice_in_dim(cells, cells.shape[dim] - width, cells.shape[dim], axis=dim)
        cells = jnp.concatenate(
            [
                lax.ppermute(tail, axis, [(i, (i + 1) % count) for i in range(count)]),
                cells,
                lax.ppermute(head, axis, [((i + 1) % count, i) for i in range(count)]),
            ],
            axis=dim,
        )
    return cells


def minmod(former, latter):
    return (
        0.5 * (jnp.sign(former) + jnp.sign(latter)) * jnp.minimum(jnp.abs(former), jnp.abs(latter))
    )


def spread(field, dimension):
    return 0.75 * field + 0.125 * (jnp.roll(field, 1, dimension) + jnp.roll(field, -1, dimension))


def slanted(field, dimension):
    return (jnp.roll(field, 1, dimension) - jnp.roll(field, -1, dimension)) / 32.0


def factors(length):
    return (64, length // 64)


def phases(outer, inner, length, flip):
    product = (
        jnp.arange(outer, dtype=jnp.int32)[:, None]
        * jnp.arange(inner, dtype=jnp.int32)[None, :]
        % length
    )
    angle = product.astype(jnp.float32) * (flip * 2.0 * math.pi / length)
    return (jnp.cos(angle), jnp.sin(angle))


def contract(pattern, real_part, imag_part, cosine, sine):

    def mixed(left, right):
        return jnp.einsum(pattern, left, right, precision=highest)

    return (
        mixed(real_part, cosine) - mixed(imag_part, sine),
        mixed(real_part, sine) + mixed(imag_part, cosine),
    )


def twist(real_part, imag_part, cosine, sine):
    cosine = cosine[None, :, :, None]
    sine = sine[None, :, :, None]
    return (real_part * cosine - imag_part * sine, real_part * sine + imag_part * cosine)


def transform(real_part, imag_part, dimension, inverse):
    shape = real_part.shape
    length = shape[dimension]
    before = math.prod(shape[:dimension])
    after = math.prod(shape[dimension + 1 :])
    outer, inner = factors(length)
    real_part = real_part.reshape(before, outer, inner, after)
    imag_part = imag_part.reshape(before, outer, inner, after)
    flip = 1.0 if inverse else -1.0
    cos_outer, sin_outer = phases(outer, outer, outer, flip)
    cos_inner, sin_inner = phases(inner, inner, inner, flip)
    cos_twist, sin_twist = phases(outer, inner, length, flip)
    if inverse:
        real_part, imag_part = contract("pkmq,bm->pkbq", real_part, imag_part, cos_inner, sin_inner)
        real_part, imag_part = twist(real_part, imag_part, cos_twist, sin_twist)
        real_part, imag_part = contract("pkbq,ak->pabq", real_part, imag_part, cos_outer, sin_outer)
        real_part = real_part / length
        imag_part = imag_part / length
    else:
        real_part, imag_part = contract("pabq,ak->pkbq", real_part, imag_part, cos_outer, sin_outer)
        real_part, imag_part = twist(real_part, imag_part, cos_twist, sin_twist)
        real_part, imag_part = contract("pkbq,bm->pkmq", real_part, imag_part, cos_inner, sin_inner)
    return (real_part.reshape(shape), imag_part.reshape(shape))


def wavenumbers(position, length):
    outer, inner = factors(length)
    frequency = position // inner + outer * (position % inner)
    return jnp.where(frequency < length // 2, frequency, frequency - length)


def layer_sums(ghosted, refine, weight_low, weight_high):
    layers = ghosted.shape[0] - 2
    row_count = ghosted.shape[1] - 2
    width = ghosted.shape[2]
    block_x = refine.shape[1]
    block_y = refine.shape[2]

    def step(position, totals):
        slab = lax.dynamic_slice_in_dim(ghosted, position, 3, 0).astype(jnp.float32)
        middle = slab[1, 1:-1]
        coarse = lax.dynamic_index_in_dim(refine, position // 8, 0, keepdims=False).astype(
            jnp.float32
        )
        marked = jnp.broadcast_to(coarse[:, None, :, None], (block_x, 8, block_y, 8)).reshape(
            row_count, width
        )
        low = lax.dynamic_index_in_dim(weight_low, position, 0, keepdims=False)
        high = lax.dynamic_index_in_dim(weight_high, position, 0, keepdims=False)
        average = 0.5 * (low + high)
        weighted = average * middle
        updates = [weighted, marked * weighted]
        grad_z = minmod(slab[2, 1:-1] - middle, middle - slab[0, 1:-1])
        grad_x = minmod(slab[1, 2:] - middle, middle - slab[1, :-2])
        grad_y = minmod(jnp.roll(middle, -1, 1) - middle, middle - jnp.roll(middle, 1, 1))
        updates = updates + [
            marked * (0.125 * (high - low)) * grad_z,
            marked * average * grad_x,
            marked * average * grad_y,
        ]
        return tuple((total + change for total, change in zip(totals, updates)))

    blank = jnp.zeros((row_count, width), jnp.float32)
    starting = tuple((blank for change in range(5)))
    return lax.fori_loop(0, layers, step, starting)


def body(density, refine, weight_low, weight_high):
    los_position = lax.axis_index("los")
    sky_position = lax.axis_index("sky")
    los_count = lax.axis_size("los")
    layers = density.shape[0]
    ghosted = padded(density, (("los", 0), ("sky", 1)), 1)
    ghosted = ghosted.at[0].set(jnp.where(los_position == 0, ghosted[1], ghosted[0]))
    ghosted = ghosted.at[-1].set(jnp.where(los_position == los_count - 1, ghosted[-2], ghosted[-1]))
    base, refined_base, tilt_z, tilt_x, tilt_y = layer_sums(
        ghosted, refine, weight_low, weight_high
    )
    smoothed = spread(refined_base + tilt_z, 1) + slanted(tilt_y, 1)
    sloped = spread(tilt_x, 1)
    rimmed = padded(jnp.stack([smoothed, sloped]), (("sky", 1),), 1)
    deposit = (
        base
        - refined_base
        + 0.75 * rimmed[0, 1:-1]
        + 0.125 * (rimmed[0, :-2] + rimmed[0, 2:])
        + (rimmed[1, :-2] - rimmed[1, 2:]) / 32.0
    )
    partial_columns = lax.psum_scatter(deposit, "los", scatter_dimension=1, tiled=True)
    summed = lax.all_to_all(partial_columns, "los", split_axis=0, concat_axis=1, tiled=True)
    kappa = summed / float(layers * los_count)
    spec_real, spec_imag = transform(kappa, jnp.zeros_like(kappa), 1, False)
    spec_real, spec_imag = (
        lax.all_to_all(
            lax.all_to_all(spec_real, "los", split_axis=1, concat_axis=0, tiled=True),
            "sky",
            split_axis=1,
            concat_axis=0,
            tiled=True,
        ),
        lax.all_to_all(
            lax.all_to_all(spec_imag, "los", split_axis=1, concat_axis=0, tiled=True),
            "sky",
            split_axis=1,
            concat_axis=0,
            tiled=True,
        ),
    )
    spec_real, spec_imag = transform(spec_real, spec_imag, 0, False)
    length = spec_real.shape[0]
    columns = spec_real.shape[1]
    row_modes = wavenumbers(jnp.arange(length, dtype=jnp.int32), length)
    column_start = los_position * (length // los_count) + sky_position * columns
    column_modes = wavenumbers(column_start + jnp.arange(columns, dtype=jnp.int32), length)
    squared = (
        row_modes[:, None] * row_modes[:, None] + column_modes[None, :] * column_modes[None, :]
    )
    at_anchor = squared == 0
    unit = 2.0 * math.pi / length
    factor = jnp.where(
        at_anchor, 0.0, -2.0 / (unit * unit * jnp.where(at_anchor, 1, squared).astype(jnp.float32))
    )
    wave_x = (unit * row_modes.astype(jnp.float32))[:, None] * factor
    wave_y = (unit * column_modes.astype(jnp.float32))[None, :] * factor
    field_real = jnp.stack([-wave_x * spec_imag, -wave_y * spec_imag])
    field_imag = jnp.stack([wave_x * spec_real, wave_y * spec_real])
    field_real, field_imag = transform(field_real, field_imag, 1, True)
    field_real, field_imag = (
        lax.all_to_all(
            lax.all_to_all(field_real, "sky", split_axis=1, concat_axis=2, tiled=True),
            "los",
            split_axis=1,
            concat_axis=2,
            tiled=True,
        ),
        lax.all_to_all(
            lax.all_to_all(field_imag, "sky", split_axis=1, concat_axis=2, tiled=True),
            "los",
            split_axis=1,
            concat_axis=2,
            tiled=True,
        ),
    )
    field_real, leftover = transform(field_real, field_imag, 2, True)
    deflection = lax.all_to_all(field_real, "los", split_axis=2, concat_axis=1, tiled=True)
    return (deflection[0], deflection[1])


def solution(mesh):
    placed = (P("los", "sky", None), P("los", "sky", None), P("los"), P("los"))
    return jax.shard_map(
        body,
        mesh=mesh,
        in_specs=placed,
        out_specs=(P("sky", "los"), P("sky", "los")),
        check_vma=False,
    )
```

profile of v0, /device:TPU:0, one launch (start us, length us, event | category | flops | bytes accessed | tf_op | source)
XLA Modules:
  0.0 621.0 jit_solution(5599655907658653806)
XLA Ops:
  8.5 3.0 collective-permute-start
  11.6 12.7 %collective-permute-done = bf16[1,128,2048]{2,1,0:T(8,128)(2,1)S(1)} collective-permute-done((bf16[1,128,2048]{2,1,0:T(8,128)(2,1)S(1)}, bf16[1,128,2048]{2,1,0:T(8,128)(2,1)S(1)}, u32[]{:S(2)}, u32[]{:S(2)}) %collective-permute-start) | collective-permute-done | bytes 524320 | tf_op jit(solution)/shard_map/ppermute | solution.py:18
  26.9 7.8 %collective-permute-done.1 = bf16[1,128,2048]{2,1,0:T(8,128)(2,1)S(1)} collective-permute-done((bf16[1,128,2048]{2,1,0:T(8,128)(2,1)S(1)}, bf16[1,128,2048]{2,1,0:T(8,128)(2,1)S(1)}, u32[]{:S(2)}, u32[]{:S(2)}) %collective-permute-start.1) | collective-permute-done | bytes 524320 | tf_op jit(solution)/shard_map/ppermute | solution.py:20
  37.2 3.4 collective-permute-start.3
  42.7 4.5 collective-permute-done.2
  47.2 4.4 pad_maximum_fusion
  54.7 260.7 %while.26 = (s32[]{:T(128)}, f32[128,2048]{1,0:T(8,128)}, f32[128,2048]{1,0:T(8,128)}, f32[128,2048]{1,0:T(8,128)}, f32[128,2048]{1,0:T(8,128)S(1)}, /*index=5*/...) while((s32[]{:T(128)}, f32[128,2048]{1,0:T(8,128)}, ...), condition=%wide.region_1.2_spmd.clone, body=%wide.region_0.1_spmd.clone.sunk | while | flops 13643783 | bytes 60383640 | solution.py:136
  54.9 7.9 %broadcast_in_dim.97 = f32[16,8,256,8]{3,2,1,0:T(8,128)} broadcast(f32[16,256]{1,0:T(8,128)S(1)} %bitcast.324), dimensions={0,2} | broadcast | bytes 1064960 | tf_op jit(solution)/shard_map/while/body/eval_jaxpr/broadcast_in_dim | solution.py:116
  62.8 12.6 %reshape.573 = f32[128,2048]{1,0:T(8,128)S(1)} reshape(f32[16,8,256,8]{3,2,1,0:T(8,128)} %broadcast_in_dim.97) | data formatting | bytes 2097152 | tf_op jit(solution)/shard_map/while/body/eval_jaxpr/reshape | solution.py:116
  83.5 2.9 select_add_fusion.8
  87.5 7.9 %broadcast_in_dim.97 = f32[16,8,256,8]{3,2,1,0:T(8,128)} broadcast(f32[16,256]{1,0:T(8,128)S(1)} %bitcast.324), dimensions={0,2} | broadcast | bytes 1064960 | tf_op jit(solution)/shard_map/while/body/eval_jaxpr/broadcast_in_dim | solution.py:116
  95.4 12.6 %reshape.573 = f32[128,2048]{1,0:T(8,128)S(1)} reshape(f32[16,8,256,8]{3,2,1,0:T(8,128)} %broadcast_in_dim.97) | data formatting | bytes 2097152 | tf_op jit(solution)/shard_map/while/body/eval_jaxpr/reshape | solution.py:116
  116.0 2.9 select_add_fusion.8
  120.0 7.9 %broadcast_in_dim.97 = f32[16,8,256,8]{3,2,1,0:T(8,128)} broadcast(f32[16,256]{1,0:T(8,128)S(1)} %bitcast.324), dimensions={0,2} | broadcast | bytes 1064960 | tf_op jit(solution)/shard_map/while/body/eval_jaxpr/broadcast_in_dim | solution.py:116
  127.9 12.6 %reshape.573 = f32[128,2048]{1,0:T(8,128)S(1)} reshape(f32[16,8,256,8]{3,2,1,0:T(8,128)} %broadcast_in_dim.97) | data formatting | bytes 2097152 | tf_op jit(solution)/shard_map/while/body/eval_jaxpr/reshape | solution.py:116
  148.6 2.9 select_add_fusion.8
  152.6 7.9 %broadcast_in_dim.97 = f32[16,8,256,8]{3,2,1,0:T(8,128)} broadcast(f32[16,256]{1,0:T(8,128)S(1)} %bitcast.324), dimensions={0,2} | broadcast | bytes 1064960 | tf_op jit(solution)/shard_map/while/body/eval_jaxpr/broadcast_in_dim | solution.py:116
  160.5 12.6 %reshape.573 = f32[128,2048]{1,0:T(8,128)S(1)} reshape(f32[16,8,256,8]{3,2,1,0:T(8,128)} %broadcast_in_dim.97) | data formatting | bytes 2097152 | tf_op jit(solution)/shard_map/while/body/eval_jaxpr/reshape | solution.py:116
  181.1 2.9 select_add_fusion.8
  185.1 7.9 %broadcast_in_dim.97 = f32[16,8,256,8]{3,2,1,0:T(8,128)} broadcast(f32[16,256]{1,0:T(8,128)S(1)} %bitcast.324), dimensions={0,2} | broadcast | bytes 1064960 | tf_op jit(solution)/shard_map/while/body/eval_jaxpr/broadcast_in_dim | solution.py:116
  193.0 12.6 %reshape.573 = f32[128,2048]{1,0:T(8,128)S(1)} reshape(f32[16,8,256,8]{3,2,1,0:T(8,128)} %broadcast_in_dim.97) | data formatting | bytes 2097152 | tf_op jit(solution)/shard_map/while/body/eval_jaxpr/reshape | solution.py:116
  213.7 2.9 select_add_fusion.8
  217.7 7.9 %broadcast_in_dim.97 = f32[16,8,256,8]{3,2,1,0:T(8,128)} broadcast(f32[16,256]{1,0:T(8,128)S(1)} %bitcast.324), dimensions={0,2} | broadcast | bytes 1064960 | tf_op jit(solution)/shard_map/while/body/eval_jaxpr/broadcast_in_dim | solution.py:116
  225.6 12.6 %reshape.573 = f32[128,2048]{1,0:T(8,128)S(1)} reshape(f32[16,8,256,8]{3,2,1,0:T(8,128)} %broadcast_in_dim.97) | data formatting | bytes 2097152 | tf_op jit(solution)/shard_map/while/body/eval_jaxpr/reshape | solution.py:116
  246.3 2.9 select_add_fusion.8
  250.2 7.9 %broadcast_in_dim.97 = f32[16,8,256,8]{3,2,1,0:T(8,128)} broadcast(f32[16,256]{1,0:T(8,128)S(1)} %bitcast.324), dimensions={0,2} | broadcast | bytes 1064960 | tf_op jit(solution)/shard_map/while/body/eval_jaxpr/broadcast_in_dim | solution.py:116
  258.2 12.6 %reshape.573 = f32[128,2048]{1,0:T(8,128)S(1)} reshape(f32[16,8,256,8]{3,2,1,0:T(8,128)} %broadcast_in_dim.97) | data formatting | bytes 2097152 | tf_op jit(solution)/shard_map/while/body/eval_jaxpr/reshape | solution.py:116
  278.8 2.9 select_add_fusion.8
  282.8 7.9 %broadcast_in_dim.97 = f32[16,8,256,8]{3,2,1,0:T(8,128)} broadcast(f32[16,256]{1,0:T(8,128)S(1)} %bitcast.324), dimensions={0,2} | broadcast | bytes 1064960 | tf_op jit(solution)/shard_map/while/body/eval_jaxpr/broadcast_in_dim | solution.py:116
  290.7 12.6 %reshape.573 = f32[128,2048]{1,0:T(8,128)S(1)} reshape(f32[16,8,256,8]{3,2,1,0:T(8,128)} %broadcast_in_dim.97) | data formatting | bytes 2097152 | tf_op jit(solution)/shard_map/while/body/eval_jaxpr/reshape | solution.py:116
  311.4 2.9 select_add_fusion.8
  320.2 4.5 collective-permute-done.4
  326.3 17.8 %reduce-scatter.2.cloned.1.call-done = f32[128,1024]{1,0:T(8,128)} async-done(((f32[128,2048]{1,0:T(8,128)}), f32[128,1024]{1,0:T(8,128)}) %reduce-scatter.2.cloned.1.call-update) | async-done | bytes 524304 | tf_op jit(solution)/shard_map/reduce_scatter | solution.py:160
  344.1 4.0 all-to-all-start
  348.2 8.0 %all-to-all-done = f32[2,64,1024]{2,1,0:T(8,128)S(1)} async-done(((f32[2,64,1024]{2,1,0:T(8,128)}), f32[2,64,1024]{2,1,0:T(8,128)S(1)}, u32[]{:S(2)}, u32[]{:S(2)}) %all-to-all-start) | async-done | bytes 524320 | tf_op jit(solution)/shard_map/all_to_all | solution.py:161
  357.2 3.3 fusion.80
  360.4 3.3 fusion.85
  377.3 3.5 all-to-all-start.1
  388.0 3.5 all-to-all-start.3
  393.0 5.1 all-to-all-done.3
  398.1 5.6 all-to-all-start.2
  405.4 12.5 %all-to-all-done.2 = f32[128,16,64]{0,2,1:T(8,128)S(1)} async-done(((f32[128,16,64]{0,2,1:T(8,128)}), f32[128,16,64]{0,2,1:T(8,128)S(1)}, u32[]{:S(2)}, u32[]{:S(2)}) %all-to-all-start.2) | async-done | bytes 524320 | tf_op jit(solution)/shard_map/all_to_all | solution.py:165
  418.0 4.2 all-to-all-start.4
  426.4 10.2 %all-to-all-done.4 = f32[128,16,64]{0,2,1:T(8,128)} async-done(((f32[128,16,64]{0,2,1:T(8,128)}), f32[128,16,64]{0,2,1:T(8,128)}, u32[]{:S(2)}, u32[]{:S(2)}) %all-to-all-start.4) | async-done | bytes 524320 | tf_op jit(solution)/shard_map/all_to_all | solution.py:172
  455.3 2.8 fusion.4
  458.1 3.3 fusion.8
  461.4 3.2 multiply_bitcast_fusion.1
  465.9 8.6 %copy.375 = f32[2,2048,64]{2,0,1:T(2,128)} copy(f32[2,2048,64]{2,1,0:T(8,128)S(1)} %bitcast.310) | data formatting | bytes 2097152 | tf_op jit(solution)/shard_map/reshape | solution.py:94
  474.5 4.2 reshape.564
  478.7 4.6 all-to-all-start.5
  483.3 4.6 fusion.6
  487.9 3.2 multiply_bitcast_fusion
  492.4 7.8 %copy.374 = f32[2,2048,64]{2,0,1:T(2,128)S(1)} copy(f32[2,2048,64]{2,1,0:T(8,128)S(1)} %bitcast.312) | data formatting | bytes 2097152 | tf_op jit(solution)/shard_map/reshape | solution.py:94
  500.2 3.2 reshape.566
  506.1 6.8 %all-to-all-start.7 = ((f32[16,1,16384]{2,1,0:T(1,128)}), f32[16,1,16384]{2,1,0:T(1,128)}, u32[]{:S(2)}, u32[]{:S(2)}) async-start(f32[16,1,16384]{2,1,0:T(1,128)} %reshape.566), calls=%async_computation.8 | async-start | bytes 2097152 | tf_op jit(solution)/shard_map/all_to_all | solution.py:208
  513.5 4.4 reduce.4
  521.7 14.2 %all-to-all-done.7 = f32[16,1,16384]{2,1,0:T(1,128)} async-done(((f32[16,1,16384]{2,1,0:T(1,128)}), f32[16,1,16384]{2,1,0:T(1,128)}, u32[]{:S(2)}, u32[]{:S(2)}) %all-to-all-start.7) | async-done | bytes 1048608 | tf_op jit(solution)/shard_map/all_to_all | solution.py:208
  535.9 4.4 all-to-all-start.6
  540.4 4.4 reduce.5
  548.6 6.6 %all-to-all-done.6 = f32[2,128,1024]{2,0,1:T(2,128)} async-done(((f32[2,128,1024]{2,0,1:T(2,128)}), f32[2,128,1024]{2,0,1:T(2,128)}, u32[]{:S(2)}, u32[]{:S(2)}) %all-to-all-start.6) | async-done | bytes 1048608 | tf_op jit(solution)/shard_map/all_to_all | solution.py:200
  555.2 4.6 all-to-all-start.8
  567.8 6.0 all-to-all-done.8
  589.0 15.7 %all_to_all.158 = f32[2,1,131072]{2,1,0:T(1,128)S(1)} all-to-all(f32[2,1,131072]{2,1,0:T(1,128)S(1)} %reshape.568), channel_id=1, replica_groups=mesh['los'=2,'sky'=16] {'los'}, dimensions={0} | all-to-all | bytes 2097152 | tf_op jit(solution)/shard_map/all_to_all | solution.py:216
  604.7 4.0 reduce.6
  (280 shorter events, 158.5 us)
Async XLA Ops:
  7.2 337.0 %reduce-scatter.2.cloned.1.call-start = ((), (), s32[]{:S(2)}) async-start(), calls=%async_computation.11 | async-start | bytes 1572864 | tf_op jit(solution)/shard_map/reduce_scatter | solution.py:160
  8.5 15.8 %collective-permute-start = (bf16[1,128,2048]{2,1,0:T(8,128)(2,1)S(1)}, bf16[1,128,2048]{2,1,0:T(8,128)(2,1)S(1)}, u32[]{:S(2)}, u32[]{:S(2)}) collective-permute-start(bf16[1,128,2048]{2,1,0:T(8,128)(2,1)S(1)} %get-tuple-element.335), channel_id=1, source_target_pairs={{0,16},{16,0},{1,17},{17,1},{2,18},{18,2},{3,19},{19,3},{4,20},{20... | collective-permute-start | bytes 1572872 | tf_op jit(solution)/shard_map/ppermute | solution.py:18
  11.5 23.2 %collective-permute-start.1 = (bf16[1,128,2048]{2,1,0:T(8,128)(2,1)S(1)}, bf16[1,128,2048]{2,1,0:T(8,128)(2,1)S(1)}, u32[]{:S(2)}, u32[]{:S(2)}) collective-permute-start(bf16[1,128,2048]{2,1,0:T(8,128)(2,1)S(1)} %get-tuple-element.334), channel_id=1, source_target_pairs={{16,0},{0,16},{17,1},{1,17},{18,2},{2,18},{19,3},{3,19},{20,4},{4,... | collective-permute-start | bytes 1572872 | tf_op jit(solution)/shard_map/ppermute | solution.py:20
  24.3 16.3 %copy-start.14 = (s32[1,16,256]{2,1,0:T(8,128)S(1)}, s32[1,16,256]{2,1,0:T(8,128)}, u32[]{:S(2)}) copy-start(s32[1,16,256]{2,1,0:T(8,128)} %param.11) | copy-start | bytes 49156
  34.7 2.4 copy-start.11
  37.2 5.5 collective-permute-start.3
  40.7 6.6 %collective-permute-start.2 = (bf16[10,1,2048]{2,1,0:T(2,128)(2,1)S(1)}, bf16[10,1,2048]{2,1,0:T(2,128)(2,1)S(1)}, u32[]{:S(2)}, u32[]{:S(2)}) collective-permute-start(bf16[10,1,2048]{2,1,0:T(2,128)(2,1)S(1)} %get-tuple-element.330), channel_id=1, source_target_pairs={{0,1},{1,2},{2,3},{3,4},{4,5},{5,6},{6,7},{7,8},{8,9},{9,10},{10,1... | collective-permute-start | bytes 122888 | tf_op jit(solution)/shard_map/ppermute | solution.py:18
  51.7 3.0 copy-start.15
  51.7 3.0 copy-start.16
  52.2 2.4 copy-start.3
  77.9 2.0 copy-start
  77.9 2.0 copy-start.7
  80.7 1.4 copy-start.8
  80.8 2.6 copy-start.4
  86.4 1.0 copy-start.5
  110.5 2.0 copy-start
  110.5 2.0 copy-start.7
  113.3 1.4 copy-start.8
  113.4 2.6 copy-start.4
  119.0 1.0 copy-start.5
  143.0 2.0 copy-start
  143.1 2.0 copy-start.7
  145.9 1.4 copy-start.8
  146.0 2.6 copy-start.4
  151.5 1.0 copy-start.5
  175.6 2.0 copy-start
  175.6 2.0 copy-start.7
  178.4 1.4 copy-start.8
  178.5 2.6 copy-start.4
  184.1 1.0 copy-start.5
  208.2 2.0 copy-start
  208.2 2.0 copy-start.7
  211.0 1.4 copy-start.8
  211.1 2.6 copy-start.4
  240.7 2.0 copy-start
  240.7 2.0 copy-start.7
  243.5 1.4 copy-start.8
  243.6 2.6 copy-start.4
  273.3 2.0 copy-start
  273.3 2.0 copy-start.7
  276.1 1.4 copy-start.8
  276.2 2.6 copy-start.4
  281.8 1.0 copy-start.5
  305.8 2.0 copy-start
  305.8 2.0 copy-start.7
  308.6 1.4 copy-start.8
  308.7 2.6 copy-start.4
  315.4 1.2 copy-start.2
  315.4 1.5 copy-start.6
  318.7 6.0 copy-start.9
  318.7 1.5 collective-permute-start.5
  318.8 5.9 collective-permute-start.4
  344.1 12.0 %all-to-all-start = ((f32[2,64,1024]{2,1,0:T(8,128)}), f32[2,64,1024]{2,1,0:T(8,128)S(1)}, u32[]{:S(2)}, u32[]{:S(2)}) async-start(f32[2,64,1024]{2,1,0:T(8,128)} %bitcast.325), calls=%async_computation.1 | async-start | bytes 1048576 | tf_op jit(solution)/shard_map/all_to_all | solution.py:161
  377.3 10.7 %all-to-all-start.1 = ((f32[64,2,1024]{2,0,1:T(8,128)}), f32[64,2,1024]{2,0,1:T(8,128)S(1)}, u32[]{:S(2)}, u32[]{:S(2)}) async-start(f32[64,2,1024]{2,0,1:T(8,128)} %copy.240), calls=%async_computation.2 | async-start | bytes 1048576 | tf_op jit(solution)/shard_map/all_to_all | solution.py:166
  388.0 10.1 %all-to-all-start.3 = ((f32[64,2,1024]{2,0,1:T(8,128)}), f32[64,2,1024]{2,0,1:T(8,128)S(1)}, u32[]{:S(2)}, u32[]{:S(2)}) async-start(f32[64,2,1024]{2,0,1:T(8,128)} %copy.250), calls=%async_computation.4 | async-start | bytes 1048576 | tf_op jit(solution)/shard_map/all_to_all | solution.py:173
  398.1 19.9 %all-to-all-start.2 = ((f32[128,16,64]{0,2,1:T(8,128)}), f32[128,16,64]{0,2,1:T(8,128)S(1)}, u32[]{:S(2)}, u32[]{:S(2)}) async-start(f32[128,16,64]{0,2,1:T(8,128)} %copy.241), calls=%async_computation.3 | async-start | bytes 1048576 | tf_op jit(solution)/shard_map/all_to_all | solution.py:165
  418.0 18.5 %all-to-all-start.4 = ((f32[128,16,64]{0,2,1:T(8,128)}), f32[128,16,64]{0,2,1:T(8,128)}, u32[]{:S(2)}, u32[]{:S(2)}) async-start(f32[128,16,64]{0,2,1:T(8,128)} %copy.251), calls=%async_computation.5 | async-start | bytes 1048576 | tf_op jit(solution)/shard_map/all_to_all | solution.py:172
  458.1 3.3 copy-start.10
  478.7 27.4 %all-to-all-start.5 = ((f32[16,1,16384]{2,1,0:T(1,128)}), f32[16,1,16384]{2,1,0:T(1,128)S(1)}, u32[]{:S(2)}, u32[]{:S(2)}) async-start(f32[16,1,16384]{2,1,0:T(1,128)} %reshape.564), calls=%async_computation.6 | async-start | bytes 2097152 | tf_op jit(solution)/shard_map/all_to_all | solution.py:201
  506.1 6.9 %copy-start.12 = (f32[16,1,16384]{2,1,0:T(1,128)}, f32[16,1,16384]{2,1,0:T(1,128)S(1)}, u32[]{:S(2)}) copy-start(f32[16,1,16384]{2,1,0:T(1,128)S(1)} %all-to-all-done.5) | copy-start | bytes 3145732
  506.1 29.8 %all-to-all-start.7 = ((f32[16,1,16384]{2,1,0:T(1,128)}), f32[16,1,16384]{2,1,0:T(1,128)}, u32[]{:S(2)}, u32[]{:S(2)}) async-start(f32[16,1,16384]{2,1,0:T(1,128)} %reshape.566), calls=%async_computation.8 | async-start | bytes 2097152 | tf_op jit(solution)/shard_map/all_to_all | solution.py:208
  535.9 19.3 %all-to-all-start.6 = ((f32[2,128,1024]{2,0,1:T(2,128)}), f32[2,128,1024]{2,0,1:T(2,128)}, u32[]{:S(2)}, u32[]{:S(2)}) async-start(f32[2,128,1024]{2,0,1:T(2,128)} %copy.275), calls=%async_computation.7 | async-start | bytes 2097152 | tf_op jit(solution)/shard_map/all_to_all | solution.py:200
  555.2 18.6 %all-to-all-start.8 = ((f32[2,128,1024]{2,0,1:T(2,128)}), f32[2,128,1024]{2,0,1:T(2,128)}, u32[]{:S(2)}, u32[]{:S(2)}) async-start(f32[2,128,1024]{2,0,1:T(2,128)} %copy.284), calls=%async_computation.9 | async-start | bytes 2097152 | tf_op jit(solution)/shard_map/all_to_all | solution.py:207
  577.6 2.4 copy-start.13
  (11 other events, 11.1 us)
Sparse Core Ops, SparseCore 0:
  326.4 17.6 reduce-scatter.1
where the time goes:
time: 628 us; the launch traced here: 621 us
  local copies, waits for them, and re-layouts  270 us (43%)
  waiting for transfers between devices  118 us (19%)
  other arithmetic  66.3 us (11%)
  matrix products  65.1 us (10%)
  starting transfers between devices  48.4 us (8%)
  loops' own time  21.5 us (3%)
  blocking collectives  15.7 us (2%)
  between operations  15.3 us (2%)
    reshape x8, local copies, waits for them, and re-layouts, step(): jnp.broadcast_to(coarse[:, None, :, None], (block_x, 8, block_y, 8))  101 us
    dot_general x30, matrix products, mixed(): return jnp.einsum(pattern, left, right, precision=highest)  65.1 us
    broadcast_in_dim x8, local copies, waits for them, and re-layouts, step(): jnp.broadcast_to(coarse[:, None, :, None], (block_x, 8, block_y, 8))  63.4 us
    add x16, other arithmetic, step(): return tuple((total + change for total, change in zip(totals, updates)))  29.4 us
    unnamed x30, local copies, waits for them, and re-layouts  22.7 us
    ppermute x3, waiting for transfers between devices, padded(): lax.ppermute(tail, axis, [(i, (i + 1) % count) for i in range(count)])  21.7 us
    another operation x1, loops' own time, layer_sums(): return lax.fori_loop(0, layers, step, starting)  21.5 us
    reduce_scatter x1, waiting for transfers between devices, body(): lax.psum_scatter(deposit, 'los', scatter_dimension=1, tiled=True)  17.8 us
  transfers between devices with their start and end apart: 16, of which 16 were waited for; matrix products, arithmetic and copies ran while one was open for 9% of the time, Pallas kernels for 0%

commit v1 on v0

v1 whole, which is shorter than its diff:
```python
import functools
import math

import jax
import jax.numpy as jnp
import numpy as np
from jax import lax
from jax.experimental import pallas as pl
from jax.experimental.pallas import tpu as pltpu
from jax.sharding import PartitionSpec as P

LANES = 128
SUB = 8
VMEM = pl.BlockSpec(memory_space=pltpu.VMEM)
SMEM = pl.BlockSpec(memory_space=pltpu.SMEM)


def median0(a, b):
    return jnp.maximum(jnp.minimum(a, b), jnp.minimum(jnp.maximum(a, b), 0.0))


def add(p, q):
    im = q[1] if p[1] is None else (p[1] if q[1] is None else p[1] + q[1])
    return (p[0] + q[0], im)


def sub(p, q):
    if q[1] is None:
        return (p[0] - q[0], p[1])
    return (p[0] - q[0], -q[1] if p[1] is None else p[1] - q[1])


def turn(p, angle):
    c, s = math.cos(angle), math.sin(angle)
    re, im = p
    if abs(s) < 1e-12:
        return p if c > 0 else (-re, None if im is None else -im)
    if abs(c) < 1e-12:
        sign = 1.0 if s > 0 else -1.0
        if im is None:
            return (jnp.zeros_like(re), sign * re)
        return (-im, re) if s > 0 else (im, -re)
    if im is None:
        return (c * re, s * re)
    return (c * re - s * im, s * re + c * im)


def fft_list(items, flip):
    count = len(items)
    if count == 1:
        return items
    even = fft_list(items[0::2], flip)
    odd = fft_list(items[1::2], flip)
    first, second = [], []
    for k in range(count // 2):
        w = turn(odd[k], flip * 2.0 * math.pi * k / count)
        first.append(add(even[k], w))
        second.append(sub(even[k], w))
    return first + second


def row_table(width):
    tiles = width // LANES
    classes = tiles // 2
    half = LANES // 2
    t = np.arange(LANES)
    table = np.zeros((classes, 2 * LANES, 2 * LANES))

    def angles(n):
        return 2.0 * np.pi * ((n[:, None] * t[None, :]) % width) / width

    for c in range(classes):
        if c == 0:
            j = np.arange(half)
            low = angles(tiles * j)
            high = angles(tiles * j + classes)
            table[0, :half, :LANES] = np.cos(low)
            table[0, half:LANES, LANES:] = np.cos(high)
            table[0, LANES : LANES + half, :LANES] = -np.sin(low)
            table[0, LANES, :LANES] = np.cos(np.pi * t)
            table[0, LANES + half :, LANES:] = -np.sin(high)
        else:
            a = angles(c + tiles * np.arange(LANES))
            table[c, :LANES, :LANES] = np.cos(a)
            table[c, :LANES, LANES:] = np.sin(a)
            table[c, LANES:, :LANES] = -np.sin(a)
            table[c, LANES:, LANES:] = np.cos(a)
    return jnp.asarray(table, jnp.float32)


def tile_table(width):
    tiles = width // LANES
    classes = tiles // 2
    s = np.arange(tiles)
    table = np.zeros((classes, 2 * tiles))
    for c in range(classes):
        if c == 0:
            table[c, 0::2] = 1.0
            table[c, 1::2] = np.where(s % 2 == 0, 1.0, -1.0)
        else:
            table[c, 0::2] = np.cos(2.0 * np.pi * s * c / tiles)
            table[c, 1::2] = -np.sin(2.0 * np.pi * s * c / tiles)
    return jnp.asarray(table, jnp.float32)


def column_tables(length, sky):
    rows = length // sky
    t = np.arange(rows)
    a = 2.0 * np.pi * (t[:, None] * t[None, :] % rows) / rows
    c, s = np.cos(a), np.sin(a)
    forward = np.block([[c, -s], [s, c]])
    b = 2.0 * np.pi * (np.arange(sky)[:, None] * t[None, :]) / length
    twist = np.stack([np.cos(b), np.sin(b)], axis=1)
    return jnp.asarray(forward, jnp.float32), jnp.asarray(twist, jnp.float32)


def dot(a, b, dims):
    return lax.dot_general(
        a, b, (dims, ((), ())), precision=lax.Precision.HIGHEST, preferred_element_type=jnp.float32
    )


def layer_kernel(
    density, below, above, before, after, refine, average, slope, keep, out, cells, base_s, smooth_s, tilt_s
):
    layers, rows, width = density.shape
    tiles = width // LANES
    blocks = refine.shape[0]
    coarse = refine.shape[1]
    deep = 16
    for z in range(layers):
        rims = [before[z : z + 1, :].astype(jnp.float32), after[z : z + 1, :].astype(jnp.float32)]
        cells[z + 1, SUB - 1 : SUB, :] = rims[0]
        cells[z + 1, SUB + rows : SUB + rows + 1, :] = rims[1]

    def fill(r, carry):
        start = pl.multiple_of(r * deep, deep)
        into = pl.ds(pl.multiple_of(start + SUB, SUB), deep)
        cells[0, into, :] = below[pl.ds(start, deep), :].astype(jnp.float32)
        cells[layers + 1, into, :] = above[pl.ds(start, deep), :].astype(jnp.float32)
        for z in range(layers):
            cells[z + 1, into, :] = density[z, pl.ds(start, deep), :].astype(jnp.float32)
        return carry

    lax.fori_loop(0, rows // deep, fill, 0)
    blank = jnp.zeros((2 * SUB, width), jnp.float32)
    for ref in (smooth_s, tilt_s):
        ref[0 : 2 * SUB, :] = blank
        ref[rows + 2 * SUB : rows + 4 * SUB, :] = blank
    base_s[0:SUB, :] = blank[:SUB]
    base_s[rows + SUB : rows + 2 * SUB, :] = blank[:SUB]
    column = lax.broadcasted_iota(jnp.int32, (coarse, width), 1)
    line = lax.broadcasted_iota(jnp.int32, (coarse, width), 0)
    wide = width // coarse
    inside = (column >= line * wide) & (column < line * wide + wide)
    stretch = jnp.where(inside, 1.0, 0.0).astype(jnp.bfloat16)
    marks = jnp.dot(
        refine[...].astype(jnp.float32).astype(jnp.bfloat16), stretch, preferred_element_type=jnp.float32
    )
    for r in range(blocks):
        base_s[SUB * (r + 1) : SUB * (r + 2), :] = jnp.broadcast_to(marks[r : r + 1], (SUB, width))

    def spread(field):
        return 0.75 * field + 0.125 * (pltpu.roll(field, 1, 1) + pltpu.roll(field, width - 1, 1))

    def chunk(r, carry):
        start = pl.multiple_of(r * SUB, SUB)
        here = pl.ds(pl.multiple_of(start + SUB, SUB), SUB)
        mid = cells[1, here, :]
        step_z = keep[0] * (mid - cells[0, here, :])
        base = jnp.zeros((SUB, width), jnp.float32)
        tilt_z, tilt_x, tilt_y = base, base, base
        for z in range(layers):
            above_mid = cells[z + 2, here, :]
            next_z = above_mid - mid
            if z == layers - 1:
                next_z = keep[1] * next_z
            w = cells[z + 1, pl.ds(start, 3 * SUB), :]
            up, down = w[SUB - 1 : 2 * SUB - 1], w[SUB + 1 : 2 * SUB + 1]
            step_y = pltpu.roll(mid, width - 1, 1) - mid
            back_y = pltpu.roll(step_y, 1, 1)
            base = base + average[z] * mid
            tilt_z = tilt_z + slope[z] * median0(next_z, step_z)
            tilt_x = tilt_x + average[z] * median0(down - mid, mid - up)
            tilt_y = tilt_y + average[z] * median0(step_y, back_y)
            mid, step_z = above_mid, next_z
        mark = base_s[here, :]
        refined = mark * base
        base_s[here, :] = base - refined
        tilt_y = mark * tilt_y
        into = pl.ds(pl.multiple_of(start + 2 * SUB, SUB), SUB)
        smooth_s[into, :] = spread(refined + mark * tilt_z) + (
            pltpu.roll(tilt_y, 1, 1) - pltpu.roll(tilt_y, width - 1, 1)
        ) * (1.0 / 32.0)
        tilt_s[into, :] = spread(mark * tilt_x)
        return carry

    lax.fori_loop(0, rows // SUB, chunk, 0)

    def finish(r, carry):
        start = pl.multiple_of(r * SUB, SUB)
        a = smooth_s[pl.ds(start, 3 * SUB), :]
        b = tilt_s[pl.ds(start, 3 * SUB), :]
        prior, mid, later = slice(SUB - 1, 2 * SUB - 1), slice(SUB, 2 * SUB), slice(SUB + 1, 2 * SUB + 1)
        deposit = (
            base_s[pl.ds(start, SUB), :]
            + 0.75 * a[mid]
            + 0.125 * (a[prior] + a[later])
            + (b[prior] - b[later]) * (1.0 / 32.0)
        )
        parts = [(deposit[:, LANES * s : LANES * (s + 1)], None) for s in range(tiles)]
        modes = fft_list(parts, -1.0)
        for c in range(tiles // 2):
            pair = (modes[0][0], modes[tiles // 2][0]) if c == 0 else modes[c]
            for j in range(2):
                out[c, j, pl.ds(start, SUB), :] = pair[j]
        return carry

    lax.fori_loop(0, rows // SUB + 2, finish, 0)


def row_kernel(place, tiles, table, out):
    sources, groups, pair, padded, lanes = tiles.shape
    rows = padded - 2 * SUB
    sky, part = out.shape[0], out.shape[3]
    line = lax.broadcasted_iota(jnp.int32, (rows, lanes), 0)
    for g in range(groups):
        sides = []
        for j in range(pair):
            total = tiles[0, g, j]
            for source in range(1, sources):
                total = total + tiles[source, g, j]
            side = total[SUB : SUB + rows]
            side = side + jnp.where(line == 0, total[0:1], 0.0)
            side = side + jnp.where(line == rows - 1, total[padded - 1 : padded], 0.0)
            sides.append(side)
        modes = dot(table[place[0] * groups + g], jnp.concatenate(sides, axis=1), ((1,), (1,)))
        for d in range(sky):
            for j in range(pair):
                begin = j * lanes + d * part
                out[d, g, j] = modes[begin : begin + part]


def column_kernel(length, layers, place, modes, forward, twist, out):
    sky, groups, pair, part, rows = modes.shape
    classes = length // LANES // 2
    tiles = 2 * classes
    count = groups * part
    extra = SUB
    total = count + extra
    line = lax.broadcasted_iota(jnp.int32, (total, rows), 0)
    lane = lax.broadcasted_iota(jnp.int32, (total, rows), 1)
    first = (place[0] == 0) & (place[1] == 0)
    packed = (line == 0) & first
    group = line // part
    kind = place[0] * groups + group
    j = place[1] * part + line % part
    half = LANES // 2
    n = jnp.where(kind == 0, jnp.where(j < half, tiles * j, tiles * (j - half) + classes), kind + tiles * j)
    n = jnp.where(n >= length // 2, n - length, n)
    n = jnp.where(line >= count, length // 2, n)
    ny = n.astype(jnp.float32)
    odd_y = jnp.where(n == length // 2, 0.0, ny)
    single = packed | (line >= count)
    unit = 2.0 * math.pi / length
    weight = jnp.where(single, 1.0, 2.0) * (-2.0 / (unit * float(length) * float(length) * float(layers)))
    zero = jnp.zeros((extra, rows), jnp.float32)
    items = []
    for s in range(sky):
        re = jnp.concatenate([modes[s, g, 0] for g in range(groups)], axis=0)
        im = jnp.concatenate([modes[s, g, 1] for g in range(groups)], axis=0)
        spare = jnp.broadcast_to(im[0:1], (extra, rows))
        re = jnp.concatenate([re, spare], axis=0)
        im = jnp.concatenate([im, zero], axis=0)
        items.append((re, jnp.where(packed, 0.0, im)))
    items = fft_list(items, -1.0)
    turned = []
    for k, (re, im) in enumerate(items):
        c, s = twist[k, 0:1, :], twist[k, 1:2, :]
        turned.append(jnp.concatenate([re * c + im * s, im * c - re * s], axis=1))
    spectrum = dot(jnp.concatenate(turned, axis=0), forward[...], ((1,), (0,)))
    fields = ([], [])
    for k in range(sky):
        here = spectrum[k * total : (k + 1) * total]
        re, im = here[:, :rows], here[:, rows:]
        nx = k + sky * lane
        nx = jnp.where(nx >= length // 2, nx - length, nx)
        odd_x = jnp.where(nx == -(length // 2), 0, nx).astype(jnp.float32)
        square = nx.astype(jnp.float32) * nx.astype(jnp.float32) + ny * ny
        factor = jnp.where(square == 0.0, 0.0, weight / jnp.where(square == 0.0, 1.0, square))
        for field, odd in ((0, odd_x), (1, odd_y)):
            scale = odd * factor
            fields[field].append(jnp.concatenate([-scale * im, scale * re], axis=1))
    for field in range(2):
        values = dot(jnp.concatenate(fields[field], axis=0), forward[...], ((1,), (1,)))
        items = []
        for k in range(sky):
            here = values[k * total : (k + 1) * total]
            re, im = here[:, :rows], here[:, rows:]
            c, s = twist[k, 0:1, :], twist[k, 1:2, :]
            items.append((re * c - im * s, im * c + re * s))
        items = fft_list(items, 1.0)
        for s in range(sky):
            re, im = items[s]
            im = jnp.where(packed, jnp.broadcast_to(re[count : count + 1], (total, rows)), im)
            for g in range(groups):
                out[s, field, g, 0] = re[g * part : (g + 1) * part]
                out[s, field, g, 1] = im[g * part : (g + 1) * part]


def plane_kernel(place, modes, table, mix, out):
    sky, fields, groups, pair, part, rows = modes.shape
    parts, width = out.shape[0], out.shape[3]
    tiles = parts * width // LANES
    for field in range(fields):
        pieces = []
        for g in range(groups):
            z = jnp.concatenate([modes[d, field, g, j] for j in range(pair) for d in range(sky)], axis=0)
            both = dot(z, table[place[0] * groups + g], ((0,), (0,)))
            pieces.append((both[:, :LANES], both[:, LANES:]))
        for s in range(tiles):
            total = None
            for g in range(groups):
                kind = place[0] * groups + g
                term = mix[kind, 2 * s] * pieces[g][0] + mix[kind, 2 * s + 1] * pieces[g][1]
                total = term if total is None else total + term
            at = s * LANES
            out[at // width, field, :, at % width : at % width + LANES] = total


def call(kernel, shape, specs, scratch=()):
    return pl.pallas_call(
        kernel,
        out_shape=jax.ShapeDtypeStruct(shape, jnp.float32),
        in_specs=specs,
        out_specs=VMEM,
        scratch_shapes=list(scratch),
        compiler_params=pltpu.CompilerParams(vmem_limit_bytes=60 * 1024 * 1024),
    )


def body(density, refine, weight_low, weight_high):
    los_count = lax.axis_size("los")
    sky_count = lax.axis_size("sky")
    los = lax.axis_index("los")
    sky = lax.axis_index("sky")
    layers, rows, width = density.shape
    length = rows * sky_count
    tiles = width // LANES
    classes = tiles // 2
    groups = classes // los_count
    part = LANES // sky_count
    place = jnp.stack([los, sky]).astype(jnp.int32)
    onward = [(i, i + 1) for i in range(los_count - 1)]
    back = [(i + 1, i) for i in range(los_count - 1)]
    ring = [(i, (i + 1) % sky_count) for i in range(sky_count)]
    gnir = [((i + 1) % sky_count, i) for i in range(sky_count)]
    below = lax.ppermute(density[layers - 1], "los", onward)
    above = lax.ppermute(density[0], "los", back)
    before = lax.ppermute(density[:, rows - 1, :], "sky", ring)
    after = lax.ppermute(density[:, 0, :], "sky", gnir)
    average = 0.5 * (weight_low + weight_high)
    slope = 0.125 * (weight_high - weight_low)
    keep = jnp.stack([los > 0, los < los_count - 1]).astype(jnp.float32)
    padded = rows + 2 * SUB
    folded = call(
        layer_kernel,
        (classes, 2, padded, LANES),
        [VMEM] * 6 + [SMEM] * 3,
        [
            pltpu.VMEM((layers + 2, padded, width), jnp.float32),
            pltpu.VMEM((padded, width), jnp.float32),
            pltpu.VMEM((rows + 4 * SUB, width), jnp.float32),
            pltpu.VMEM((rows + 4 * SUB, width), jnp.float32),
        ],
    )(density, below, above, before, after, refine[0], average, slope, keep)
    to_before = folded[:, :, SUB - 1 : SUB]
    to_after = folded[:, :, rows + SUB : rows + SUB + 1]
    from_before = lax.ppermute(to_after, "sky", ring)
    from_after = lax.ppermute(to_before, "sky", gnir)
    folded = lax.dynamic_update_slice(folded, from_before, (0, 0, 0, 0))
    folded = lax.dynamic_update_slice(folded, from_after, (0, 0, padded - 1, 0))
    folded = folded.reshape(los_count, groups, 2, padded, LANES)
    folded = lax.all_to_all(folded, "los", split_axis=0, concat_axis=0, tiled=True)
    table = row_table(width)
    modes = call(row_kernel, (sky_count, groups, 2, part, rows), [SMEM, VMEM, VMEM])(place, folded, table)
    modes = lax.all_to_all(modes, "sky", split_axis=0, concat_axis=0, tiled=True)
    forward, twist = column_tables(length, sky_count)
    fields = call(
        functools.partial(column_kernel, length, layers * los_count),
        (sky_count, 2, groups, 2, part, rows),
        [SMEM, VMEM, VMEM, VMEM],
    )(place, modes, forward, twist)
    fields = lax.all_to_all(fields, "sky", split_axis=0, concat_axis=0, tiled=True)
    plane = call(plane_kernel, (los_count, 2, rows, width // los_count), [SMEM, VMEM, VMEM, SMEM])(
        place, fields, table, tile_table(width)
    )
    plane = lax.all_to_all(plane, "los", split_axis=0, concat_axis=0, tiled=True)
    plane = jnp.sum(plane, axis=0)
    return (plane[0], plane[1])


def solution(mesh):
    placed = (P("los", "sky", None), P("los", "sky", None), P("los"), P("los"))
    return jax.shard_map(
        body,
        mesh=mesh,
        in_specs=placed,
        out_specs=(P("sky", "los"), P("sky", "los")),
        check_vma=False,
    )
```

time: 628 us -> 168 us (0.27)
  local copies, waits for them, and re-layouts: 270 us -> 9.23 us
  waiting for transfers between devices: 118 us -> 19.4 us
  matrix products: 65.1 us -> 0 us
  other arithmetic: 66.3 us -> 2.02 us
  blocking collectives: 15.7 us -> 79.5 us
  Pallas kernels: 0 us -> 36.7 us
  starting transfers between devices: 48.4 us -> 19.2 us
  loops' own time: 21.5 us -> 0 us
  between operations: 15.3 us -> 0.73 us
    reshape x11 -> x0, local copies, waits for them, and re-layouts: 118 us -> none  [the longest x8 101 us: step(): jnp.broadcast_to(coarse[:, None, :, None], (block_x, 8, block_y, 8))]
    dot_general x30 -> x0, matrix products: 65.1 us -> none  [mixed(): return jnp.einsum(pattern, left, right, precision=highest)]
    all_to_all x1 -> x3, blocking collectives: 15.7 us -> 79.5 us  [the longest x1 30 us: body(): lax.all_to_all(plane, 'los', split_axis=0, concat_axis=0, tiled=True)]
    broadcast_in_dim x8 -> x0, local copies, waits for them, and re-layouts: 63.4 us -> none  [step(): jnp.broadcast_to(coarse[:, None, :, None], (block_x, 8, block_y, 8))]
    all_to_all x9 -> x1, waiting for transfers between devices: 68.2 us -> 14 us  [body(): lax.all_to_all(folded, 'los', split_axis=0, concat_axis=0, tiled=True)]
    all_to_all x9 -> x1, starting transfers between devices: 41.3 us -> 3.75 us  [body(): lax.all_to_all(folded, 'los', split_axis=0, concat_axis=0, tiled=True)]
    pallas_call x0 -> x4, Pallas kernels: none -> 36.7 us  [the longest x1 23.1 us: body(): call(layer_kernel, (classes, 2, padded, LANES), [VMEM] * 6 + [SMEM] * 3,...]
    add x19 -> x0, other arithmetic: 31.9 us -> none  [the longest x16 29.4 us: step(): return tuple((total + change for total, change in zip(totals, updates)))]
  transfers between devices with their start and end apart: 16 -> 7, of which waited for: 16 -> 6; matrix products, arithmetic and copies ran while one was open for 9% -> 3% of each run, Pallas kernels for 0% -> 0%
where the time goes in v1:
time: 168 us; the launch traced here: 167 us
  blocking collectives  79.5 us (47%)
  Pallas kernels  36.7 us (22%)
  waiting for transfers between devices  19.4 us (12%)
  starting transfers between devices  19.2 us (11%)
  local copies, waits for them, and re-layouts  9.23 us (5%)
  other arithmetic  2.02 us (1%)
    all_to_all x1, blocking collectives, body(): lax.all_to_all(plane, 'los', split_axis=0, concat_axis=0, tiled=True)  30 us
    all_to_all x1, blocking collectives, body(): lax.all_to_all(fields, 'sky', split_axis=0, concat_axis=0, tiled=True)  29 us
    pallas_call x1, Pallas kernels, body(): call(layer_kernel, (classes, 2, padded, LANES), [VMEM] * 6 + [SMEM] * 3,...  23.1 us
    all_to_all x1, blocking collectives, body(): lax.all_to_all(modes, 'sky', split_axis=0, concat_axis=0, tiled=True)  20.5 us
    all_to_all x1, waiting for transfers between devices, body(): lax.all_to_all(folded, 'los', split_axis=0, concat_axis=0, tiled=True)  14 us
    pallas_call x1, Pallas kernels, body(): call(plane_kernel, (los_count, 2, rows, width // los_count), [SMEM, VMEM,...  5.39 us
    ppermute x1, starting transfers between devices, body(): below = lax.ppermute(density[layers - 1], 'los', onward)  4.93 us
    ppermute x1, starting transfers between devices, body(): after = lax.ppermute(density[:, 0, :], 'sky', gnir)  4.64 us
  transfers between devices with their start and end apart: 7, of which 6 were waited for; matrix products, arithmetic and copies ran while one was open for 3% of the time, Pallas kernels for 0%

profile of v1, /device:TPU:0, one launch (start us, length us, event | category | flops | bytes accessed | tf_op | source)
XLA Modules:
  0.0 166.8 jit_solution(10228253741598202199)
XLA Ops:
  0.6 0.0 copy-start.5
  0.6 0.0 copy-start.6
  0.6 1.3 slice_bitcast_fusion.2
  1.9 1.3 collective-permute-start.1
  3.2 4.9 %collective-permute-start = (bf16[128,2048]{1,0:T(8,128)(2,1)S(1)}, bf16[128,2048]{1,0:T(8,128)(2,1)S(1)}, u32[]{:S(2)}, u32[]{:S(2)}) collective-permute-start(bf16[128,2048]{1,0:T(8,128)(2,1)S(1)} %get-tuple-element.5), channel_id=1, source_target_pairs={{0,16},{1,17},{2,18},{3,19},{4,20},{5,21},{6,22},{7,23},{8,24},{9,... | collective-permute-start | bytes 1572872 | tf_op jit(solution)/shard_map/ppermute | solution.py:358
  8.2 1.1 fusion
  9.3 0.1 collective-permute-start.2
  9.4 4.6 %collective-permute-start.3 = (bf16[8,2048]{1,0:T(8,128)(2,1)S(1)}, bf16[8,2048]{1,0:T(8,128)(2,1)S(1)}, u32[]{:S(2)}, u32[]{:S(2)}) collective-permute-start(bf16[8,2048]{1,0:T(8,128)(2,1)S(1)} %bitcast.22), channel_id=1, source_target_pairs={{1,0},{2,1},{3,2},{4,3},{5,4},{6,5},{7,6},{8,7},{9,8},{10,9},{11,1... | collective-permute-start | bytes 98312 | tf_op jit(solution)/shard_map/ppermute | solution.py:361
  14.1 0.0 copy-done.5
  14.1 0.0 copy-done.6
  14.1 0.5 subtract_multiply_fusion
  14.6 0.7 add_convert_fusion.keep
  15.3 0.3 collective-permute-done.2.before
  15.6 0.0 copy-start.3
  15.6 0.1 collective-permute-done.3.after
  15.7 0.0 copy-start.4
  15.7 2.5 %collective-permute-done.1.above = bf16[128,2048]{1,0:T(8,128)(2,1)S(1)} collective-permute-done((bf16[128,2048]{1,0:T(8,128)(2,1)S(1)}, bf16[128,2048]{1,0:T(8,128)(2,1)S(1)}, u32[]{:S(2)}, u32[]{:S(2)}) %collective-permute-start.1) | collective-permute-done | bytes 524320 | tf_op jit(solution)/shard_map/ppermute | solution.py:359
  18.1 0.0 copy-start.1
  18.1 1.2 collective-permute-done.below
  19.4 0.0 copy-start.2
  19.4 0.0 copy-done.3
  19.4 0.0 copy-done.4
  19.4 0.0 copy-done.1
  19.4 0.8 copy-done.2
  20.2 23.1 %shard_map.95 = f32[8,2,144,128]{3,2,1,0:T(8,128)} custom-call(bf16[8,128,2048]{2,1,0:T(8,128)(2,1)} %density.1, bf16[128,2048]{1,0:T(8,128)(2,1)} %copy-done.2, bf16[128,2048]{1,0:T(8,128)(2,1)} %copy-done.1, bf16[8,2048]{1,0:T(8,128)(2,1)} %copy-done.3, bf16[8,2048]{1,0:T(8,128)(2,1)} %copy-done.4, s32[16,256]{1,0:T(8,128)} %bitcast.23, ...), custom_call_target="tpu_custom_call" | custom-call | tf_op jit(solution)/shard_map/pallas_call | solution.py:366
  43.2 0.9 fusion.1
  44.1 0.1 collective-permute-start.4
  44.2 4.4 %collective-permute-start.5 = (f32[8,2,1,128]{3,2,1,0:T(1,128)S(1)}, f32[8,2,1,128]{3,2,1,0:T(1,128)S(1)}, u32[]{:S(2)}, u32[]{:S(2)}) collective-permute-start(f32[8,2,1,128]{3,2,1,0:T(1,128)S(1)} %get-tuple-element.6), channel_id=1, source_target_pairs={{1,0},{2,1},{3,2},{4,3},{5,4},{6,5},{7,6},{8,7},{9,8},{10,9},{11,1... | collective-permute-start | bytes 24584 | tf_op jit(solution)/shard_map/ppermute | solution.py:380
  48.6 1.4 collective-permute-done.4
  50.0 1.5 dynamic_update_slice.6
  51.5 0.0 collective-permute-done.5
  51.5 1.5 dynamic_update_slice.7
  53.0 3.7 %all-to-all-start = ((f32[2,4,2,144,128]{4,3,2,1,0:T(8,128)}), f32[2,4,2,144,128]{4,3,2,1,0:T(8,128)S(1)}, u32[]{:S(2)}, u32[]{:S(2)}) async-start(f32[2,4,2,144,128]{4,3,2,1,0:T(8,128)} %bitcast.20), calls=%async_computation | async-start | bytes 2359296 | tf_op jit(solution)/shard_map/all_to_all | solution.py:384
  56.7 0.6 pad_add_fusion.place
  57.3 14.0 %all-to-all-done.tiles = f32[2,4,2,144,128]{4,3,2,1,0:T(8,128)S(1)} async-done(((f32[2,4,2,144,128]{4,3,2,1,0:T(8,128)}), f32[2,4,2,144,128]{4,3,2,1,0:T(8,128)S(1)}, u32[]{:S(2)}, u32[]{:S(2)}) %all-to-all-start) | async-done | bytes 1179680 | tf_op jit(solution)/shard_map/all_to_all | solution.py:384
  71.3 0.0 copy-start
  71.3 1.0 copy-done
  72.3 3.8 %shard_map.96 = f32[16,4,2,8,128]{4,3,2,1,0:T(8,128)} custom-call(s32[2]{0:T(128)} %pad_add_fusion.place, f32[2,4,2,144,128]{4,3,2,1,0:T(8,128)} %copy-done, f32[8,256,256]{2,1,0:T(8,128)} %constant.29.clone.table), custom_call_target="tpu_custom_call" | custom-call | tf_op jit(solution)/shard_map/pallas_call | solution.py:386
  76.1 20.5 %all_to_all.20.modes = f32[16,4,2,8,128]{4,3,2,1,0:T(8,128)} all-to-all(f32[16,4,2,8,128]{4,3,2,1,0:T(8,128)} %shard_map.96), channel_id=1, replica_groups=mesh['los'=2,'sky'=16] {'sky'}, dimensions={0} | all-to-all | bytes 1048576 | tf_op jit(solution)/shard_map/all_to_all | solution.py:387
  96.7 4.5 %shard_map.97 = f32[16,2,4,2,8,128]{5,4,3,2,1,0:T(8,128)} custom-call(s32[2]{0:T(128)} %pad_add_fusion.place, f32[16,4,2,8,128]{4,3,2,1,0:T(8,128)} %all_to_all.20.modes, f32[256,256]{1,0:T(8,128)} %constant.30.clone.forward, f32[16,2,128]{2,1,0:T(2,128)} %constant.31.clone.twist), custom_call_target="tpu_custom_call" | custom-call | tf_op jit(solution)/shard_map/pallas_call | solution.py:389
  101.1 29.0 %all_to_all.21.modes = f32[16,2,4,2,8,128]{5,4,3,2,1,0:T(8,128)} all-to-all(f32[16,2,4,2,8,128]{5,4,3,2,1,0:T(8,128)} %shard_map.97), channel_id=1, replica_groups=mesh['los'=2,'sky'=16] {'sky'}, dimensions={0} | all-to-all | bytes 2097152 | tf_op jit(solution)/shard_map/all_to_all | solution.py:394
  130.1 5.4 %shard_map.98 = f32[2,2,128,1024]{3,2,1,0:T(8,128)} custom-call(s32[2]{0:T(128)} %pad_add_fusion.place, f32[16,2,4,2,8,128]{5,4,3,2,1,0:T(8,128)} %all_to_all.21.modes, f32[8,256,256]{2,1,0:T(8,128)} %constant.29.clone.table, f32[8,32]{1,0:T(8,128)} %constant.32.clone.mix), custom_call_target="tpu_custom_call" | custom-call | tf_op jit(solution)/shard_map/pallas_call | solution.py:395
  135.5 30.0 %all_to_all.22 = f32[2,2,128,1024]{3,2,1,0:T(8,128)S(1)} all-to-all(f32[2,2,128,1024]{3,2,1,0:T(8,128)} %shard_map.98), channel_id=1, replica_groups=mesh['los'=2,'sky'=16] {'los'}, dimensions={0} | all-to-all | bytes 4194304 | tf_op jit(solution)/shard_map/all_to_all | solution.py:398
  165.5 0.2 reduce_sum.9
  165.8 1.0 slice_bitcast_fusion
  (2 shorter events, 0.0 us)
Async XLA Ops:
  0.6 13.5 %copy-start.5 = (f32[8]{0:T(128)S(1)}, f32[8]{0:T(128)}, u32[]{:S(2)}) copy-start(f32[8]{0:T(128)} %param.11) | copy-start | bytes 100
  0.6 13.4 %copy-start.6 = (f32[8]{0:T(128)S(1)}, f32[8]{0:T(128)}, u32[]{:S(2)}) copy-start(f32[8]{0:T(128)} %param.10) | copy-start | bytes 100
  1.9 16.2 %collective-permute-start.1 = (bf16[128,2048]{1,0:T(8,128)(2,1)S(1)}, bf16[128,2048]{1,0:T(8,128)(2,1)S(1)}, u32[]{:S(2)}, u32[]{:S(2)}) collective-permute-start(bf16[128,2048]{1,0:T(8,128)(2,1)S(1)} %get-tuple-element.4), channel_id=1, source_target_pairs={{16,0},{17,1},{18,2},{19,3},{20,4},{21,5},{22,6},{23,7},{24,8},{25... | collective-permute-start | bytes 1572872 | tf_op jit(solution)/shard_map/ppermute | solution.py:359
  3.2 16.1 %collective-permute-start = (bf16[128,2048]{1,0:T(8,128)(2,1)S(1)}, bf16[128,2048]{1,0:T(8,128)(2,1)S(1)}, u32[]{:S(2)}, u32[]{:S(2)}) collective-permute-start(bf16[128,2048]{1,0:T(8,128)(2,1)S(1)} %get-tuple-element.5), channel_id=1, source_target_pairs={{0,16},{1,17},{2,18},{3,19},{4,20},{5,21},{6,22},{7,23},{8,24},{9,... | collective-permute-start | bytes 1572872 | tf_op jit(solution)/shard_map/ppermute | solution.py:358
  9.3 6.2 %collective-permute-start.2 = (bf16[8,2048]{1,0:T(8,128)(2,1)S(1)}, bf16[8,2048]{1,0:T(8,128)(2,1)S(1)}, u32[]{:S(2)}, u32[]{:S(2)}) collective-permute-start(bf16[8,2048]{1,0:T(8,128)(2,1)S(1)} %bitcast.21), channel_id=1, source_target_pairs={{0,1},{1,2},{2,3},{3,4},{4,5},{5,6},{6,7},{7,8},{8,9},{9,10},{10,1... | collective-permute-start | bytes 98312 | tf_op jit(solution)/shard_map/ppermute | solution.py:360
  9.4 6.2 %collective-permute-start.3 = (bf16[8,2048]{1,0:T(8,128)(2,1)S(1)}, bf16[8,2048]{1,0:T(8,128)(2,1)S(1)}, u32[]{:S(2)}, u32[]{:S(2)}) collective-permute-start(bf16[8,2048]{1,0:T(8,128)(2,1)S(1)} %bitcast.22), channel_id=1, source_target_pairs={{1,0},{2,1},{3,2},{4,3},{5,4},{6,5},{7,6},{8,7},{9,8},{10,9},{11,1... | collective-permute-start | bytes 98312 | tf_op jit(solution)/shard_map/ppermute | solution.py:361
  15.6 3.8 %copy-start.3 = (bf16[8,2048]{1,0:T(8,128)(2,1)}, bf16[8,2048]{1,0:T(8,128)(2,1)S(1)}, u32[]{:S(2)}) copy-start(bf16[8,2048]{1,0:T(8,128)(2,1)S(1)} %collective-permute-done.2.before) | copy-start | bytes 98308
  15.7 3.7 %copy-start.4 = (bf16[8,2048]{1,0:T(8,128)(2,1)}, bf16[8,2048]{1,0:T(8,128)(2,1)S(1)}, u32[]{:S(2)}) copy-start(bf16[8,2048]{1,0:T(8,128)(2,1)S(1)} %collective-permute-done.3.after) | copy-start | bytes 98308
  18.1 1.2 copy-start.1
  19.4 0.8 copy-start.2
  44.1 5.8 %collective-permute-start.4 = (f32[8,2,1,128]{3,2,1,0:T(1,128)S(1)}, f32[8,2,1,128]{3,2,1,0:T(1,128)S(1)}, u32[]{:S(2)}, u32[]{:S(2)}) collective-permute-start(f32[8,2,1,128]{3,2,1,0:T(1,128)S(1)} %get-tuple-element.7), channel_id=1, source_target_pairs={{0,1},{1,2},{2,3},{3,4},{4,5},{5,6},{6,7},{7,8},{8,9},{9,10},{10,1... | collective-permute-start | bytes 24584 | tf_op jit(solution)/shard_map/ppermute | solution.py:379
  44.2 7.3 %collective-permute-start.5 = (f32[8,2,1,128]{3,2,1,0:T(1,128)S(1)}, f32[8,2,1,128]{3,2,1,0:T(1,128)S(1)}, u32[]{:S(2)}, u32[]{:S(2)}) collective-permute-start(f32[8,2,1,128]{3,2,1,0:T(1,128)S(1)} %get-tuple-element.6), channel_id=1, source_target_pairs={{1,0},{2,1},{3,2},{4,3},{5,4},{6,5},{7,6},{8,7},{9,8},{10,9},{11,1... | collective-permute-start | bytes 24584 | tf_op jit(solution)/shard_map/ppermute | solution.py:380
  53.0 18.3 %all-to-all-start = ((f32[2,4,2,144,128]{4,3,2,1,0:T(8,128)}), f32[2,4,2,144,128]{4,3,2,1,0:T(8,128)S(1)}, u32[]{:S(2)}, u32[]{:S(2)}) async-start(f32[2,4,2,144,128]{4,3,2,1,0:T(8,128)} %bitcast.20), calls=%async_computation | async-start | bytes 2359296 | tf_op jit(solution)/shard_map/all_to_all | solution.py:384
  71.3 1.0 copy-start

commit v2 on v1

--- a/solution.py
+++ b/solution.py
@@ -120,29 +120,72 @@
     )
 
 
-def layer_kernel(
-    density, below, above, before, after, refine, average, slope, keep, out, cells, base_s, smooth_s, tilt_s
-):
+def sums_kernel(density, average, slope, out, cells):
     layers, rows, width = density.shape
-    tiles = width // LANES
-    blocks = refine.shape[0]
-    coarse = refine.shape[1]
     deep = 16
+    last = density[:, rows - deep : rows, :]
+    head = density[:, 0:deep, :]
     for z in range(layers):
-        rims = [before[z : z + 1, :].astype(jnp.float32), after[z : z + 1, :].astype(jnp.float32)]
-        cells[z + 1, SUB - 1 : SUB, :] = rims[0]
-        cells[z + 1, SUB + rows : SUB + rows + 1, :] = rims[1]
+        cells[z, SUB - 1 : SUB, :] = head[z].astype(jnp.float32)[0:1]
+        cells[z, SUB + rows : SUB + rows + 1, :] = last[z].astype(jnp.float32)[deep - 1 : deep]
 
     def fill(r, carry):
         start = pl.multiple_of(r * deep, deep)
         into = pl.ds(pl.multiple_of(start + SUB, SUB), deep)
-        cells[0, into, :] = below[pl.ds(start, deep), :].astype(jnp.float32)
-        cells[layers + 1, into, :] = above[pl.ds(start, deep), :].astype(jnp.float32)
         for z in range(layers):
-            cells[z + 1, into, :] = density[z, pl.ds(start, deep), :].astype(jnp.float32)
+            cells[z, into, :] = density[z, pl.ds(start, deep), :].astype(jnp.float32)
         return carry
 
     lax.fori_loop(0, rows // deep, fill, 0)
+
+    def chunk(r, carry):
+        start = pl.multiple_of(r * SUB, SUB)
+        here = pl.ds(pl.multiple_of(start + SUB, SUB), SUB)
+        mid = cells[0, here, :]
+        step_z = None
+        base = jnp.zeros((SUB, width), jnp.float32)
+        tilt_z, tilt_x, tilt_y = base, base, base
+        for z in range(layers):
+            w = cells[z, pl.ds(start, 3 * SUB), :]
+            up, down = w[SUB - 1 : 2 * SUB - 1], w[SUB + 1 : 2 * SUB + 1]
+            step_y = pltpu.roll(mid, width - 1, 1) - mid
+            back_y = pltpu.roll(step_y, 1, 1)
+            base = base + average[z] * mid
+            tilt_x = tilt_x + average[z] * median0(down - mid, mid - up)
+            tilt_y = tilt_y + average[z] * median0(step_y, back_y)
+            if z < layers - 1:
+                above = cells[z + 1, here, :]
+                next_z = above - mid
+                if z > 0:
+                    tilt_z = tilt_z + slope[z] * median0(next_z, step_z)
+                mid, step_z = above, next_z
+        rows_at = pl.ds(start, SUB)
+        out[0, rows_at, :] = base
+        out[1, rows_at, :] = tilt_z
+        out[2, rows_at, :] = tilt_x
+        out[3, rows_at, :] = tilt_y
+        return carry
+
+    lax.fori_loop(0, rows // SUB, chunk, 0)
+
+
+def edge_kernel(
+    sums, low, high, below, above, before, first, second, former, final, after, refine, column_average, slope, keep,
+    place, out, rims, base_s, smooth_s, tilt_s
+):
+    rows, width = below.shape
+    tiles = width // LANES
+    los_count, groups = out.shape[0], out.shape[1]
+    blocks, coarse = refine.shape
+    deep = 16
+    weight = column_average[...]
+
+    def rim_slope(one, two, three):
+        one, two, three = [ref[...].astype(jnp.float32) for ref in (one, two, three)]
+        return jnp.sum(weight * median0(three - two, two - one), axis=0, keepdims=True)
+
+    fix_first = rim_slope(before, first, second)
+    fix_last = rim_slope(former, final, after)
     blank = jnp.zeros((2 * SUB, width), jnp.float32)
     for ref in (smooth_s, tilt_s):
         ref[0 : 2 * SUB, :] = blank
@@ -163,42 +206,34 @@
     def spread(field):
         return 0.75 * field + 0.125 * (pltpu.roll(field, 1, 1) + pltpu.roll(field, width - 1, 1))
 
+    end = low.shape[0]
+
     def chunk(r, carry):
-        start = pl.multiple_of(r * SUB, SUB)
-        here = pl.ds(pl.multiple_of(start + SUB, SUB), SUB)
-        mid = cells[1, here, :]
-        step_z = keep[0] * (mid - cells[0, here, :])
-        base = jnp.zeros((SUB, width), jnp.float32)
-        tilt_z, tilt_x, tilt_y = base, base, base
-        for z in range(layers):
-            above_mid = cells[z + 2, here, :]
-            next_z = above_mid - mid
-            if z == layers - 1:
-                next_z = keep[1] * next_z
-            w = cells[z + 1, pl.ds(start, 3 * SUB), :]
-            up, down = w[SUB - 1 : 2 * SUB - 1], w[SUB + 1 : 2 * SUB + 1]
-            step_y = pltpu.roll(mid, width - 1, 1) - mid
-            back_y = pltpu.roll(step_y, 1, 1)
-            base = base + average[z] * mid
-            tilt_z = tilt_z + slope[z] * median0(next_z, step_z)
-            tilt_x = tilt_x + average[z] * median0(down - mid, mid - up)
-            tilt_y = tilt_y + average[z] * median0(step_y, back_y)
-            mid, step_z = above_mid, next_z
-        mark = base_s[here, :]
+        start = pl.multiple_of(r * deep, deep)
+        here = pl.ds(start, deep)
+        base, tilt_z, tilt_x, tilt_y = [sums[i, here, :] for i in range(4)]
+        v0, v1 = [low[i, here, :].astype(jnp.float32) for i in range(2)]
+        v6, v7 = [high[i, here, :].astype(jnp.float32) for i in range(2)]
+        under, over = below[here, :].astype(jnp.float32), above[here, :].astype(jnp.float32)
+        tilt_z = tilt_z + slope[0] * median0(v1 - v0, keep[0] * (v0 - under))
+        tilt_z = tilt_z + slope[slope.shape[0] - 1] * median0(keep[1] * (over - v7), v7 - v6)
+        at = lax.broadcasted_iota(jnp.int32, (deep, width), 0) + start
+        tilt_x = tilt_x + jnp.where(at == 0, fix_first, 0.0) + jnp.where(at == rows - 1, fix_last, 0.0)
+        ours = pl.ds(pl.multiple_of(start + SUB, SUB), deep)
+        mark = base_s[ours, :]
         refined = mark * base
-        base_s[here, :] = base - refined
+        base_s[ours, :] = base - refined
         tilt_y = mark * tilt_y
-        into = pl.ds(pl.multiple_of(start + 2 * SUB, SUB), SUB)
+        into = pl.ds(pl.multiple_of(start + 2 * SUB, SUB), deep)
         smooth_s[into, :] = spread(refined + mark * tilt_z) + (
             pltpu.roll(tilt_y, 1, 1) - pltpu.roll(tilt_y, width - 1, 1)
         ) * (1.0 / 32.0)
         tilt_s[into, :] = spread(mark * tilt_x)
         return carry
 
-    lax.fori_loop(0, rows // SUB, chunk, 0)
-
-    def finish(r, carry):
-        start = pl.multiple_of(r * SUB, SUB)
+    lax.fori_loop(0, rows // deep, chunk, 0)
+
+    def pairs(start):
         a = smooth_s[pl.ds(start, 3 * SUB), :]
         b = tilt_s[pl.ds(start, 3 * SUB), :]
         prior, mid, later = slice(SUB - 1, 2 * SUB - 1), slice(SUB, 2 * SUB), slice(SUB + 1, 2 * SUB + 1)
@@ -210,29 +245,36 @@
         )
         parts = [(deposit[:, LANES * s : LANES * (s + 1)], None) for s in range(tiles)]
         modes = fft_list(parts, -1.0)
-        for c in range(tiles // 2):
-            pair = (modes[0][0], modes[tiles // 2][0]) if c == 0 else modes[c]
+        return [(modes[0][0], modes[tiles // 2][0])] + modes[1 : tiles // 2]
+
+    def finish(r, carry):
+        into = pl.ds(pl.multiple_of(r * SUB, SUB), SUB)
+        for c, pair in enumerate(pairs(pl.multiple_of((r + 1) * SUB, SUB))):
+            relative = lax.rem(c // groups - place[0] + los_count, los_count)
             for j in range(2):
-                out[c, j, pl.ds(start, SUB), :] = pair[j]
+                out[relative, c % groups, j, into, :] = pair[j]
         return carry
 
-    lax.fori_loop(0, rows // SUB + 2, finish, 0)
-
-
-def row_kernel(place, tiles, table, out):
-    sources, groups, pair, padded, lanes = tiles.shape
-    rows = padded - 2 * SUB
+    lax.fori_loop(0, rows // SUB, finish, 0)
+    for edge, (start, row) in enumerate(((0, SUB - 1), (rows + SUB, 0))):
+        for c, pair in enumerate(pairs(start)):
+            for j in range(2):
+                rims[edge, c, j : j + 1, :] = pair[j][row : row + 1]
+
+
+def row_kernel(place, own, *refs):
+    *others, rims, table, out = refs
+    groups, pair, rows, lanes = own.shape
     sky, part = out.shape[0], out.shape[3]
     line = lax.broadcasted_iota(jnp.int32, (rows, lanes), 0)
     for g in range(groups):
         sides = []
         for j in range(pair):
-            total = tiles[0, g, j]
-            for source in range(1, sources):
-                total = total + tiles[source, g, j]
-            side = total[SUB : SUB + rows]
-            side = side + jnp.where(line == 0, total[0:1], 0.0)
-            side = side + jnp.where(line == rows - 1, total[padded - 1 : padded], 0.0)
+            side = own[g, j]
+            for other in others:
+                side = side + other[g, j]
+            side = side + jnp.where(line == 0, rims[0, g, j : j + 1, :], 0.0)
+            side = side + jnp.where(line == rows - 1, rims[1, g, j : j + 1, :], 0.0)
             sides.append(side)
         modes = dot(table[place[0] * groups + g], jnp.concatenate(sides, axis=1), ((1,), (1,)))
         for d in range(sky):
@@ -241,7 +283,7 @@
                 out[d, g, j] = modes[begin : begin + part]
 
 
-def column_kernel(length, layers, place, modes, forward, twist, out):
+def column_kernel(length, layers, place, modes, forward, twist, *outs):
     sky, groups, pair, part, rows = modes.shape
     classes = length // LANES // 2
     tiles = 2 * classes
@@ -304,37 +346,41 @@
             re, im = items[s]
             im = jnp.where(packed, jnp.broadcast_to(re[count : count + 1], (total, rows)), im)
             for g in range(groups):
-                out[s, field, g, 0] = re[g * part : (g + 1) * part]
-                out[s, field, g, 1] = im[g * part : (g + 1) * part]
+                outs[field][s, g, 0] = re[g * part : (g + 1) * part]
+                outs[field][s, g, 1] = im[g * part : (g + 1) * part]
 
 
 def plane_kernel(place, modes, table, mix, out):
-    sky, fields, groups, pair, part, rows = modes.shape
-    parts, width = out.shape[0], out.shape[3]
+    sky, groups, pair, part, rows = modes.shape
+    parts, _, width = out.shape
     tiles = parts * width // LANES
-    for field in range(fields):
-        pieces = []
+    pieces = []
+    for g in range(groups):
+        z = jnp.concatenate([modes[d, g, j] for j in range(pair) for d in range(sky)], axis=0)
+        both = dot(z, table[place[0] * groups + g], ((0,), (0,)))
+        pieces.append((both[:, :LANES], both[:, LANES:]))
+    for s in range(tiles):
+        total = None
         for g in range(groups):
-            z = jnp.concatenate([modes[d, field, g, j] for j in range(pair) for d in range(sky)], axis=0)
-            both = dot(z, table[place[0] * groups + g], ((0,), (0,)))
-            pieces.append((both[:, :LANES], both[:, LANES:]))
-        for s in range(tiles):
-            total = None
-            for g in range(groups):
-                kind = place[0] * groups + g
-                term = mix[kind, 2 * s] * pieces[g][0] + mix[kind, 2 * s + 1] * pieces[g][1]
-                total = term if total is None else total + term
-            at = s * LANES
-            out[at // width, field, :, at % width : at % width + LANES] = total
-
-
-def call(kernel, shape, specs, scratch=()):
+            kind = place[0] * groups + g
+            term = mix[kind, 2 * s] * pieces[g][0] + mix[kind, 2 * s + 1] * pieces[g][1]
+            total = term if total is None else total + term
+        at = s * LANES
+        relative = lax.rem(at // width - place[0] + parts, parts)
+        out[relative, :, at % width : at % width + LANES] = total
+
+
+def call(kernel, shapes, specs, scratch=(), work=1, grid=()):
     return pl.pallas_call(
         kernel,
-        out_shape=jax.ShapeDtypeStruct(shape, jnp.float32),
+        grid=grid,
+        out_shape=jax.tree.map(
+            lambda shape: jax.ShapeDtypeStruct(shape, jnp.float32), shapes, is_leaf=lambda s: isinstance(s[0], int)
+        ),
         in_specs=specs,
-        out_specs=VMEM,
+        out_specs=jax.tree.map(lambda shape: VMEM, shapes, is_leaf=lambda s: isinstance(s[0], int)),
         scratch_shapes=list(scratch),
+        cost_estimate=pl.CostEstimate(flops=work, bytes_accessed=work, transcendentals=0),
         compiler_params=pltpu.CompilerParams(vmem_limit_bytes=60 * 1024 * 1024),
     )
 
@@ -355,49 +401,86 @@
     back = [(i + 1, i) for i in range(los_count - 1)]
     ring = [(i, (i + 1) % sky_count) for i in range(sky_count)]
     gnir = [((i + 1) % sky_count, i) for i in range(sky_count)]
+
+    def to_shift(values, shift):
+        return lax.ppermute(values, "los", [(i, (i + shift) % los_count) for i in range(los_count)])
+
     below = lax.ppermute(density[layers - 1], "los", onward)
     above = lax.ppermute(density[0], "los", back)
-    before = lax.ppermute(density[:, rows - 1, :], "sky", ring)
-    after = lax.ppermute(density[:, 0, :], "sky", gnir)
+    first, second = density[:, 0, :], density[:, 1, :]
+    former, final = density[:, rows - 2, :], density[:, rows - 1, :]
+    before = lax.ppermute(final, "sky", ring)
+    after = lax.ppermute(first, "sky", gnir)
     average = 0.5 * (weight_low + weight_high)
     slope = 0.125 * (weight_high - weight_low)
     keep = jnp.stack([los > 0, los < los_count - 1]).astype(jnp.float32)
-    padded = rows + 2 * SUB
-    folded = call(
-        layer_kernel,
-        (classes, 2, padded, LANES),
-        [VMEM] * 6 + [SMEM] * 3,
+    sums = call(
+        sums_kernel,
+        (4, rows, width),
+        [VMEM, SMEM, SMEM],
+        [pltpu.VMEM((layers, rows + 2 * SUB, width), jnp.float32)],
+        work=40_000_000,
+    )(density, average, slope)
+    two = (2, rows, width)
+    folded, rims = call(
+        edge_kernel,
+        ((los_count, groups, 2, rows, LANES), (2, classes, 2, LANES)),
         [
-            pltpu.VMEM((layers + 2, padded, width), jnp.float32),
-            pltpu.VMEM((padded, width), jnp.float32),
+            VMEM,
+            pl.BlockSpec(two, lambda i: (0, 0, 0), memory_space=pltpu.VMEM),
+            pl.BlockSpec(two, lambda i: (layers // 2 - 1, 0, 0), memory_space=pltpu.VMEM),
+        ]
+        + [VMEM] * 10
+        + [SMEM] * 3,
+        [
+            pltpu.VMEM((rows + 2 * SUB, width), jnp.float32),
             pltpu.VMEM((rows + 4 * SUB, width), jnp.float32),
             pltpu.VMEM((rows + 4 * SUB, width), jnp.float32),
         ],
-    )(density, below, above, before, after, refine[0], average, slope, keep)
-    to_before = folded[:, :, SUB - 1 : SUB]
-    to_after = folded[:, :, rows + SUB : rows + SUB + 1]
-    from_before = lax.ppermute(to_after, "sky", ring)
-    from_after = lax.ppermute(to_before, "sky", gnir)
-    folded = lax.dynamic_update_slice(folded, from_before, (0, 0, 0, 0))
-    folded = lax.dynamic_update_slice(folded, from_after, (0, 0, padded - 1, 0))
-    folded = folded.reshape(los_count, groups, 2, padded, LANES)
-    folded = lax.all_to_all(folded, "los", split_axis=0, concat_axis=0, tiled=True)
+        grid=(1,),
+    )(
+        sums, density, density, below, above, before, first, second, former, final, after, refine[0],
+        average[:, None], slope, keep, place,
+    )
+    others = [to_shift(folded[shift], shift) for shift in range(1, los_count)]
+    from_before = lax.ppermute(rims[1], "sky", ring)
+    from_after = lax.ppermute(rims[0], "sky", gnir)
+    rims = jnp.stack([from_before, from_after])
+
+    def rims_of(shift):
+        return lax.dynamic_slice_in_dim(rims, (los + shift) % los_count * groups, groups, 1)
+
+    gathered = rims_of(0)
+    for shift in range(1, los_count):
+        gathered = gathered + to_shift(rims_of(shift), shift)
     table = row_table(width)
-    modes = call(row_kernel, (sky_count, groups, 2, part, rows), [SMEM, VMEM, VMEM])(place, folded, table)
+    block = (sky_count, groups, 2, part, rows)
+    modes = call(row_kernel, block, [SMEM] + [VMEM] * (los_count + 2))(place, folded[0], *others, gathered, table)
     modes = lax.all_to_all(modes, "sky", split_axis=0, concat_axis=0, tiled=True)
     forward, twist = column_tables(length, sky_count)
     fields = call(
         functools.partial(column_kernel, length, layers * los_count),
-        (sky_count, 2, groups, 2, part, rows),
+        (block, block),
         [SMEM, VMEM, VMEM, VMEM],
     )(place, modes, forward, twist)
-    fields = lax.all_to_all(fields, "sky", split_axis=0, concat_axis=0, tiled=True)
-    plane = call(plane_kernel, (los_count, 2, rows, width // los_count), [SMEM, VMEM, VMEM, SMEM])(
-        place, fields, table, tile_table(width)
-    )
-    plane = lax.all_to_all(plane, "los", split_axis=0, concat_axis=0, tiled=True)
-    plane = jnp.sum(plane, axis=0)
-    return (plane[0], plane[1])
+    mix = tile_table(width)
+    results = []
+    for field in fields:
+        if results:
+            field, results[0] = lax.optimization_barrier((field, results[0]))
+        field = lax.all_to_all(field, "sky", split_axis=0, concat_axis=0, tiled=True)
+        results.append(
+            call(plane_kernel, (los_count, rows, width // los_count), [SMEM, VMEM, VMEM, SMEM])(
+                place, field, table, mix
+            )
+        )
+    planes = []
+    for result in results:
+        plane = result[0]
+        for shift in range(1, los_count):
+            plane = plane + to_shift(result[shift], shift)
+        planes.append(plane)
+    return tuple(planes)
 
 
 def solution(mesh):

time: 168 us -> 151 us (0.90)
  blocking collectives: 79.5 us -> 37.5 us
  waiting for transfers between devices: 19.4 us -> 28.5 us
  starting transfers between devices: 19.2 us -> 25.1 us
  other arithmetic: 2.02 us -> 5.84 us
  Pallas kernels: 36.7 us -> 40.4 us
  local copies, waits for them, and re-layouts: 9.23 us -> 11.6 us
    all_to_all x2 -> x1, blocking collectives: 59 us -> 18.5 us  [body(): lax.all_to_all(field, 'sky', split_axis=0, concat_axis=0, tiled=True)]
    ppermute x4 -> x8, waiting for transfers between devices: 1.74 us -> 16.7 us  [the longest x4 15.4 us: to_shift(): lax.ppermute(values, 'los', [(i, (i + shift) % los_count) for i in range(...]
    ppermute x4 -> x8, starting transfers between devices: 9.18 us -> 14.6 us  [the longest x4 5.61 us: to_shift(): lax.ppermute(values, 'los', [(i, (i + shift) % los_count) for i in range(...]
    squeeze x1 -> x5, local copies, waits for them, and re-layouts: 1.04 us -> 5.61 us  [the longest x2 2.15 us: body(): plane = plane + to_shift(result[shift], shift)]
    pallas_call x4 -> x6, Pallas kernels: 36.7 us -> 40.4 us  [the longest x1 15.5 us: body(): call(sums_kernel, (4, rows, width), [VMEM, SMEM, SMEM], [pltpu.VMEM((laye...]
    add x0 -> x3, other arithmetic: none -> 3.36 us  [the longest x2 2.75 us: body(): plane = plane + to_shift(result[shift], shift)]
    dynamic_update_slice x2 -> x0, local copies, waits for them, and re-layouts: 3 us -> none  [the longest x1 1.5 us: body(): folded = lax.dynamic_update_slice(folded, from_before, (0, 0, 0, 0))]
    ppermute x1, waiting for transfers between devices: 2.46 us -> 0.01 us  [body(): above = lax.ppermute(density[0], 'los', back)]
  transfers between devices with their start and end apart: 7 -> 11, of which waited for: 6 -> 4; matrix products, arithmetic and copies ran while one was open for 3% -> 6% of each run, Pallas kernels for 0% -> 13%
where the time goes in v2:
time: 151 us; the launch traced here: 150 us
  Pallas kernels  40.4 us (27%)
  blocking collectives  37.5 us (25%)
  waiting for transfers between devices  28.5 us (19%)
  starting transfers between devices  25.1 us (17%)
  local copies, waits for them, and re-layouts  11.6 us (8%)
  other arithmetic  5.84 us (4%)
    all_to_all x1, blocking collectives, body(): lax.all_to_all(modes, 'sky', split_axis=0, concat_axis=0, tiled=True)  19 us
    all_to_all x1, blocking collectives, body(): lax.all_to_all(field, 'sky', split_axis=0, concat_axis=0, tiled=True)  18.5 us
    pallas_call x1, Pallas kernels, body(): call(sums_kernel, (4, rows, width), [VMEM, SMEM, SMEM], [pltpu.VMEM((laye...  15.5 us
    ppermute x4, waiting for transfers between devices, to_shift(): lax.ppermute(values, 'los', [(i, (i + shift) % los_count) for i in range(...  15.4 us
    all_to_all x1, waiting for transfers between devices, body(): lax.all_to_all(field, 'sky', split_axis=0, concat_axis=0, tiled=True)  11.7 us
    pallas_call x1, Pallas kernels, body(): call(edge_kernel, ((los_count, groups, 2, rows, LANES), (2, classes, 2, L...  8.9 us
    pallas_call x2, Pallas kernels, body(): call(plane_kernel, (los_count, rows, width // los_count), [SMEM, VMEM, VM...  7.79 us
    ppermute x4, starting transfers between devices, to_shift(): lax.ppermute(values, 'los', [(i, (i + shift) % los_count) for i in range(...  5.61 us
  transfers between devices with their start and end apart: 11, of which 4 were waited for; matrix products, arithmetic and copies ran while one was open for 6% of the time, Pallas kernels for 13%

profile of v2, /device:TPU:0, one launch (start us, length us, event | category | flops | bytes accessed | tf_op | source)
XLA Modules:
  0.0 149.7 jit_solution(10797450285779343762)
XLA Ops:
  0.6 1.3 slice_bitcast_fusion.5
  1.9 4.9 %collective-permute-start = (bf16[128,2048]{1,0:T(8,128)(2,1)S(1)}, bf16[128,2048]{1,0:T(8,128)(2,1)S(1)}, u32[]{:S(2)}, u32[]{:S(2)}) collective-permute-start(bf16[128,2048]{1,0:T(8,128)(2,1)S(1)} %get-tuple-element.19), channel_id=1, source_target_pairs={{0,16},{1,17},{2,18},{3,19},{4,20},{5,21},{6,22},{7,23},{8,24},{9,... | collective-permute-start | bytes 1572872 | tf_op jit(solution)/shard_map/ppermute | solution.py:408
  6.8 1.3 collective-permute-start.1
  8.1 1.4 fusion.4
  9.6 0.0 copy-start.5
  9.6 0.1 collective-permute-start.2
  9.7 0.0 copy-start.6
  9.7 4.5 %collective-permute-start.3 = (bf16[8,2048]{1,0:T(8,128)(2,1)S(1)}, bf16[8,2048]{1,0:T(8,128)(2,1)S(1)}, u32[]{:S(2)}, u32[]{:S(2)}) collective-permute-start(bf16[8,2048]{1,0:T(8,128)(2,1)S(1)} %bitcast.42), channel_id=1, source_target_pairs={{1,0},{2,1},{3,2},{4,3},{5,4},{6,5},{7,6},{8,7},{9,8},{10,9},{11,1... | collective-permute-start | bytes 98312 | tf_op jit(solution)/shard_map/ppermute | solution.py:413
  14.2 0.7 pad_add_fusion.place
  14.8 1.2 subtract_multiply_fusion
  16.0 0.0 copy-start.9
  16.0 0.7 copy_bitcast_fusion
  16.7 0.6 add_convert_fusion.keep
  17.3 0.7 copy.14.column_average
  18.0 0.0 copy-done.9
  18.0 15.5 %shard_map.95.sums = f32[4,128,2048]{2,1,0:T(8,128)} custom-call(bf16[8,128,2048]{2,1,0:T(8,128)(2,1)} %high.1, f32[8]{0:T(128)} %copy-done.9, f32[8]{0:T(128)} %get-tuple-element.24.slope), custom_call_target="tpu_custom_call" | custom-call | flops 40000000 | bytes 40000000 | tf_op jit(solution)/shard_map/pallas_call | solution.py:417
  33.5 0.0 copy-done.5
  33.5 0.0 copy-done.6
  33.5 0.0 collective-permute-done.2.before
  33.5 0.0 copy-start.7
  33.5 0.0 collective-permute-done.3.after
  33.5 0.0 copy-start.8
  33.5 0.0 collective-permute-done.below
  33.5 0.0 copy-start.3
  33.5 0.0 collective-permute-done.1.above
  33.6 0.0 copy-start.4
  33.6 0.5 copy-done.7
  34.1 0.0 copy-done.8
  34.1 0.2 copy-done.3
  34.3 0.2 copy-done.4
  34.5 8.9 %shard_map.96 = (f32[2,4,2,128,128]{4,3,2,1,0:T(8,128)}, f32[2,8,2,128]{3,2,1,0:T(2,128)}) custom-call(f32[4,128,2048]{2,1,0:T(8,128)} %shard_map.95.sums, bf16[8,128,2048]{2,1,0:T(8,128)(2,1)} %high.1, bf16[8,128,2048]{2,1,0:T(8,128)(2,1)} %high.1, bf16[128,2048]{1,0:T(8,128)(2,1)} %copy-done.3, bf16[128,2048]{1,0:T(8,128)(2,1)} %copy-done.4, ...), custom_call_target="tpu_custom_call" | custom-call | flops 1 | bytes 1 | tf_op jit(solution)/shard_map/pallas_call | solution.py:425
  43.4 2.1 %slice_bitcast_fusion.3 = (f32[4,2,128,128]{3,2,1,0:T(8,128)S(1)}, f32[4,2,128,128]{3,2,1,0:T(8,128)}) fusion(f32[2,4,2,128,128]{4,3,2,1,0:T(8,128)} %get-tuple-element.8), kind=kLoop, calls=%fused_computation.5 | loop fusion | bytes 2097152 | tf_op jit(solution)/shard_map/squeeze | solution.py:445
  45.5 2.7 %collective-permute-start.4 = (f32[4,2,128,128]{3,2,1,0:T(8,128)S(1)}, f32[4,2,128,128]{3,2,1,0:T(8,128)S(1)}, u32[]{:S(2)}, u32[]{:S(2)}) collective-permute-start(f32[4,2,128,128]{3,2,1,0:T(8,128)S(1)} %get-tuple-element.20), channel_id=1, source_target_pairs={{0,16},{16,0},{1,17},{17,1},{2,18},{18,2},{3,19},{19,3},{4,20},{20... | collective-permute-start | bytes 1572872 | tf_op jit(solution)/shard_map/ppermute | solution.py:406
  48.2 0.7 slice_bitcast_fusion.7
  48.9 0.0 collective-permute-start.5
  48.9 4.4 %collective-permute-start.6 = (f32[8,2,128]{2,1,0:T(2,128)S(1)}, f32[8,2,128]{2,1,0:T(2,128)S(1)}, u32[]{:S(2)}, u32[]{:S(2)}) collective-permute-start(f32[8,2,128]{2,1,0:T(2,128)S(1)} %get-tuple-element.22), channel_id=1, source_target_pairs={{1,0},{2,1},{3,2},{4,3},{5,4},{6,5},{7,6},{8,7},{9,8},{10,9},{11,1... | collective-permute-start | bytes 24584 | tf_op jit(solution)/shard_map/ppermute | solution.py:447
  53.3 1.3 collective-permute-done.5
  54.6 0.0 collective-permute-done.6
  54.7 0.0 collective-permute-start.7
  54.8 3.6 %collective-permute-done.7 = f32[2,4,2,128]{3,2,1,0:T(2,128)S(1)} collective-permute-done((f32[2,4,2,128]{3,2,1,0:T(2,128)S(1)}, f32[2,4,2,128]{3,2,1,0:T(2,128)S(1)}, u32[]{:S(2)}, u32[]{:S(2)}) %collective-permute-start.7) | collective-permute-done | bytes 8224 | tf_op jit(solution)/shard_map/ppermute | solution.py:406
  58.4 0.6 fusion.3.refs_1_
  59.0 0.0 collective-permute-done.4.refs_0_
  59.0 0.0 copy-start.2
  59.0 0.8 copy-done.2
  59.8 3.8 %shard_map.97 = f32[16,4,2,8,128]{4,3,2,1,0:T(8,128)} custom-call(s32[2]{0:T(128)} %pad_add_fusion.place, f32[4,2,128,128]{3,2,1,0:T(8,128)} %get-tuple-element.21.own, f32[4,2,128,128]{3,2,1,0:T(8,128)} %copy-done.2, f32[2,4,2,128]{3,2,1,0:T(2,128)} %fusion.3.refs_1_, f32[8,256,256]{2,1,0:T(8,128)} %constant.44.clone.refs_2_.table), custom_call_target="tpu_custom_call" | custom-call | flops 1 | bytes 1 | tf_op jit(solution)/shard_map/pallas_call | solution.py:458
  63.6 19.0 %all_to_all.15.modes = f32[16,4,2,8,128]{4,3,2,1,0:T(8,128)} all-to-all(f32[16,4,2,8,128]{4,3,2,1,0:T(8,128)} %shard_map.97), channel_id=1, replica_groups=mesh['los'=2,'sky'=16] {'sky'}, dimensions={0} | all-to-all | bytes 1048576 | tf_op jit(solution)/shard_map/all_to_all | solution.py:459
  82.6 4.4 %shard_map.98 = (f32[16,4,2,8,128]{4,3,2,1,0:T(8,128)}, f32[16,4,2,8,128]{4,3,2,1,0:T(8,128)}) custom-call(s32[2]{0:T(128)} %pad_add_fusion.place, f32[16,4,2,8,128]{4,3,2,1,0:T(8,128)} %all_to_all.15.modes, f32[256,256]{1,0:T(8,128)} %constant.45.clone.forward, f32[16,2,128]{2,1,0:T(2,128)} %constant.46.clone.twist), custom_call_target="tpu_custom_call" | custom-call | flops 1 | bytes 1 | tf_op jit(solution)/shard_map/pallas_call | solution.py:461
  87.0 18.5 %all_to_all.16.modes = f32[16,4,2,8,128]{4,3,2,1,0:T(8,128)} all-to-all(f32[16,4,2,8,128]{4,3,2,1,0:T(8,128)} %get-tuple-element.11), channel_id=1, replica_groups=mesh['los'=2,'sky'=16] {'sky'}, dimensions={0} | all-to-all | bytes 1048576 | tf_op jit(solution)/shard_map/all_to_all | solution.py:471
  105.5 3.9 %shard_map.99 = f32[2,128,1024]{2,1,0:T(8,128)} custom-call(s32[2]{0:T(128)} %pad_add_fusion.place, f32[16,4,2,8,128]{4,3,2,1,0:T(8,128)} %all_to_all.16.modes, f32[8,256,256]{2,1,0:T(8,128)} %constant.44.clone.refs_2_.table, f32[8,32]{1,0:T(8,128)} %constant.47.clone.mix), custom_call_target="tpu_custom_call" | custom-call | flops 1 | bytes 1 | tf_op jit(solution)/shard_map/pallas_call | solution.py:473
  109.5 0.0 copy-start
  109.5 4.3 %all-to-all-start.2 = ((f32[16,4,2,8,128]{4,3,2,1,0:T(8,128)}), f32[16,4,2,8,128]{4,3,2,1,0:T(8,128)S(1)}, u32[]{:S(2)}, u32[]{:S(2)}) async-start(f32[16,4,2,8,128]{4,3,2,1,0:T(8,128)} %get-tuple-element.13), calls=%async_computation.2 | async-start | bytes 1048576 | tf_op jit(solution)/shard_map/all_to_all | solution.py:471
  113.8 1.1 slice_bitcast_fusion.2
  114.8 1.4 collective-permute-start.8
  116.3 11.7 %all-to-all-done.2.modes = f32[16,4,2,8,128]{4,3,2,1,0:T(8,128)S(1)} async-done(((f32[16,4,2,8,128]{4,3,2,1,0:T(8,128)}), f32[16,4,2,8,128]{4,3,2,1,0:T(8,128)S(1)}, u32[]{:S(2)}, u32[]{:S(2)}) %all-to-all-start.2) | async-done | bytes 524320 | tf_op jit(solution)/shard_map/all_to_all | solution.py:471
  128.0 0.0 copy-start.1
  128.0 0.8 copy-done.1
  128.8 3.9 %shard_map.100 = f32[2,128,1024]{2,1,0:T(8,128)} custom-call(s32[2]{0:T(128)} %pad_add_fusion.place, f32[16,4,2,8,128]{4,3,2,1,0:T(8,128)} %copy-done.1, f32[8,256,256]{2,1,0:T(8,128)} %constant.44.clone.refs_2_.table, f32[8,32]{1,0:T(8,128)} %constant.47.clone.mix), custom_call_target="tpu_custom_call" | custom-call | flops 1 | bytes 1 | tf_op jit(solution)/shard_map/pallas_call | solution.py:473
  132.7 1.1 slice_bitcast_fusion
  133.8 1.4 collective-permute-start.9
  135.2 0.0 collective-permute-done.8
  135.2 0.0 copy-done
  135.2 0.9 bitcast_add_fusion
  136.1 11.7 %collective-permute-done.9 = f32[128,1024]{1,0:T(8,128)S(1)} collective-permute-done((f32[128,1024]{1,0:T(8,128)S(1)}, f32[128,1024]{1,0:T(8,128)S(1)}, u32[]{:S(2)}, u32[]{:S(2)}) %collective-permute-start.9) | collective-permute-done | bytes 524320 | tf_op jit(solution)/shard_map/ppermute | solution.py:406
  147.8 1.9 %fusion = f32[128,1024]{1,0:T(8,128)} fusion(f32[128,1024]{1,0:T(8,128)S(1)} %collective-permute-done.9, f32[2,128,1024]{2,1,0:T(8,128)} %shard_map.100), kind=kLoop, calls=%fused_computation.2 | loop fusion | flops 131072 | bytes 1572864 | tf_op jit(solution)/shard_map/add | solution.py:481
  (3 shorter events, 0.1 us)
Async XLA Ops:
  1.9 31.6 %collective-permute-start = (bf16[128,2048]{1,0:T(8,128)(2,1)S(1)}, bf16[128,2048]{1,0:T(8,128)(2,1)S(1)}, u32[]{:S(2)}, u32[]{:S(2)}) collective-permute-start(bf16[128,2048]{1,0:T(8,128)(2,1)S(1)} %get-tuple-element.19), channel_id=1, source_target_pairs={{0,16},{1,17},{2,18},{3,19},{4,20},{5,21},{6,22},{7,23},{8,24},{9,... | collective-permute-start | bytes 1572872 | tf_op jit(solution)/shard_map/ppermute | solution.py:408
  6.8 26.7 %collective-permute-start.1 = (bf16[128,2048]{1,0:T(8,128)(2,1)S(1)}, bf16[128,2048]{1,0:T(8,128)(2,1)S(1)}, u32[]{:S(2)}, u32[]{:S(2)}) collective-permute-start(bf16[128,2048]{1,0:T(8,128)(2,1)S(1)} %get-tuple-element.18), channel_id=1, source_target_pairs={{16,0},{17,1},{18,2},{19,3},{20,4},{21,5},{22,6},{23,7},{24,8},{25... | collective-permute-start | bytes 1572872 | tf_op jit(solution)/shard_map/ppermute | solution.py:409
  9.6 23.9 %copy-start.5 = (bf16[8,1,2048]{2,0,1:T(8,128)(2,1)}, bf16[8,1,2048]{2,0,1:T(8,128)(2,1)S(1)}, u32[]{:S(2)}) copy-start(bf16[8,1,2048]{2,0,1:T(8,128)(2,1)S(1)} %copy.24) | copy-start | bytes 98308
  9.6 23.9 %collective-permute-start.2 = (bf16[8,2048]{1,0:T(8,128)(2,1)S(1)}, bf16[8,2048]{1,0:T(8,128)(2,1)S(1)}, u32[]{:S(2)}, u32[]{:S(2)}) collective-permute-start(bf16[8,2048]{1,0:T(8,128)(2,1)S(1)} %bitcast.40), channel_id=1, source_target_pairs={{0,1},{1,2},{2,3},{3,4},{4,5},{5,6},{6,7},{7,8},{8,9},{9,10},{10,1... | collective-permute-start | bytes 98312 | tf_op jit(solution)/shard_map/ppermute | solution.py:412
  9.7 23.8 %copy-start.6 = (bf16[8,1,2048]{2,0,1:T(8,128)(2,1)}, bf16[8,1,2048]{2,0,1:T(8,128)(2,1)S(1)}, u32[]{:S(2)}) copy-start(bf16[8,1,2048]{2,0,1:T(8,128)(2,1)S(1)} %copy.23) | copy-start | bytes 98308
  9.7 23.8 %collective-permute-start.3 = (bf16[8,2048]{1,0:T(8,128)(2,1)S(1)}, bf16[8,2048]{1,0:T(8,128)(2,1)S(1)}, u32[]{:S(2)}, u32[]{:S(2)}) collective-permute-start(bf16[8,2048]{1,0:T(8,128)(2,1)S(1)} %bitcast.42), channel_id=1, source_target_pairs={{1,0},{2,1},{3,2},{4,3},{5,4},{6,5},{7,6},{8,7},{9,8},{10,9},{11,1... | collective-permute-start | bytes 98312 | tf_op jit(solution)/shard_map/ppermute | solution.py:413
  16.0 2.0 %copy-start.9 = (f32[8]{0:T(128)}, f32[8]{0:T(128)S(1)}, u32[]{:S(2)}) copy-start(f32[8]{0:T(128)S(1)} %get-tuple-element.25.average) | copy-start | bytes 100
  33.5 0.6 copy-start.7
  33.5 0.6 copy-start.8
  33.5 0.8 copy-start.3
  33.6 0.9 copy-start.4
  45.5 13.5 %collective-permute-start.4 = (f32[4,2,128,128]{3,2,1,0:T(8,128)S(1)}, f32[4,2,128,128]{3,2,1,0:T(8,128)S(1)}, u32[]{:S(2)}, u32[]{:S(2)}) collective-permute-start(f32[4,2,128,128]{3,2,1,0:T(8,128)S(1)} %get-tuple-element.20), channel_id=1, source_target_pairs={{0,16},{16,0},{1,17},{17,1},{2,18},{18,2},{3,19},{19,3},{4,20},{20... | collective-permute-start | bytes 1572872 | tf_op jit(solution)/shard_map/ppermute | solution.py:406
  48.9 5.8 %collective-permute-start.5 = (f32[8,2,128]{2,1,0:T(2,128)S(1)}, f32[8,2,128]{2,1,0:T(2,128)S(1)}, u32[]{:S(2)}, u32[]{:S(2)}) collective-permute-start(f32[8,2,128]{2,1,0:T(2,128)S(1)} %get-tuple-element.23), channel_id=1, source_target_pairs={{0,1},{1,2},{2,3},{3,4},{4,5},{5,6},{6,7},{7,8},{8,9},{9,10},{10,1... | collective-permute-start | bytes 24584 | tf_op jit(solution)/shard_map/ppermute | solution.py:446
  48.9 5.8 %collective-permute-start.6 = (f32[8,2,128]{2,1,0:T(2,128)S(1)}, f32[8,2,128]{2,1,0:T(2,128)S(1)}, u32[]{:S(2)}, u32[]{:S(2)}) collective-permute-start(f32[8,2,128]{2,1,0:T(2,128)S(1)} %get-tuple-element.22), channel_id=1, source_target_pairs={{1,0},{2,1},{3,2},{4,3},{5,4},{6,5},{7,6},{8,7},{9,8},{10,9},{11,1... | collective-permute-start | bytes 24584 | tf_op jit(solution)/shard_map/ppermute | solution.py:447
  54.7 3.7 %collective-permute-start.7 = (f32[2,4,2,128]{3,2,1,0:T(2,128)S(1)}, f32[2,4,2,128]{3,2,1,0:T(2,128)S(1)}, u32[]{:S(2)}, u32[]{:S(2)}) collective-permute-start(f32[2,4,2,128]{3,2,1,0:T(2,128)S(1)} %fusion.1), channel_id=1, source_target_pairs={{0,16},{16,0},{1,17},{17,1},{2,18},{18,2},{3,19},{19,3},{4,20},{20... | collective-permute-start | bytes 24584 | tf_op jit(solution)/shard_map/ppermute | solution.py:406
  59.0 0.8 copy-start.2
  109.5 25.8 %copy-start = (f32[2,128,1024]{2,1,0:T(8,128)S(1)}, f32[2,128,1024]{2,1,0:T(8,128)}, u32[]{:S(2)}) copy-start(f32[2,128,1024]{2,1,0:T(8,128)} %shard_map.99) | copy-start | bytes 3145732
  109.5 18.6 %all-to-all-start.2 = ((f32[16,4,2,8,128]{4,3,2,1,0:T(8,128)}), f32[16,4,2,8,128]{4,3,2,1,0:T(8,128)S(1)}, u32[]{:S(2)}, u32[]{:S(2)}) async-start(f32[16,4,2,8,128]{4,3,2,1,0:T(8,128)} %get-tuple-element.13), calls=%async_computation.2 | async-start | bytes 1048576 | tf_op jit(solution)/shard_map/all_to_all | solution.py:471
  114.8 20.4 %collective-permute-start.8 = (f32[128,1024]{1,0:T(8,128)S(1)}, f32[128,1024]{1,0:T(8,128)S(1)}, u32[]{:S(2)}, u32[]{:S(2)}) collective-permute-start(f32[128,1024]{1,0:T(8,128)S(1)} %slice_bitcast_fusion.2), channel_id=1, source_target_pairs={{0,16},{16,0},{1,17},{17,1},{2,18},{18,2},{3,19},{19,3},{4,20},{20... | collective-permute-start | bytes 1572872 | tf_op jit(solution)/shard_map/ppermute | solution.py:406
  128.0 0.8 copy-start.1
  133.8 14.0 %collective-permute-start.9 = (f32[128,1024]{1,0:T(8,128)S(1)}, f32[128,1024]{1,0:T(8,128)S(1)}, u32[]{:S(2)}, u32[]{:S(2)}) collective-permute-start(f32[128,1024]{1,0:T(8,128)S(1)} %slice_bitcast_fusion), channel_id=1, source_target_pairs={{0,16},{16,0},{1,17},{17,1},{2,18},{18,2},{3,19},{19,3},{4,20},{20... | collective-permute-start | bytes 1572872 | tf_op jit(solution)/shard_map/ppermute | solution.py:406

commit v3 on v2

--- a/solution.py
+++ b/solution.py
@@ -262,11 +262,80 @@
                 rims[edge, c, j : j + 1, :] = pair[j][row : row + 1]
 
 
+def reach(values):
+    return jnp.max(values, axis=1, keepdims=True), jnp.min(values, axis=1, keepdims=True)
+
+
+def encode(first, second):
+    top, low = zip(reach(first), reach(second))
+    span = jnp.maximum(top[0] - low[0], top[1] - low[1])
+    size = jnp.maximum(
+        jnp.maximum(jnp.abs(top[0]), jnp.abs(low[0])), jnp.maximum(jnp.abs(top[1]), jnp.abs(low[1]))
+    )
+    span = jnp.maximum(jnp.maximum(span, size * (1.0 / 64.0)), 1e-25)
+    power = jnp.ceil(jnp.log2(span * (1.0 / 65000.0)))
+    inverse = jnp.exp2(-power)
+    codes, offsets = [], []
+    for values, t, l in ((first, top[0], low[0]), (second, top[1], low[1])):
+        offset = jnp.floor(0.5 * (t + l) * inverse + 0.5)
+        codes.append(jnp.floor(values * inverse - offset + 0.5).astype(jnp.int32))
+        offsets.append(offset)
+    return lax.shift_left(codes[0], jnp.full_like(codes[0], 16)) + (codes[1] & 65535), [power] + offsets
+
+
+def decode(words, notes):
+    power, one, two = notes
+    step = jnp.exp2(power)
+    shift = jnp.full_like(words, 16)
+    first = lax.shift_right_arithmetic(words, shift).astype(jnp.float32)
+    second = lax.shift_right_arithmetic(lax.shift_left(words, shift), shift).astype(jnp.float32)
+    return (first + one) * step, (second + two) * step
+
+
+def note_masks(count, lanes, shift):
+    line = lax.broadcasted_iota(jnp.int32, (count, lanes), 0)
+    lane = lax.broadcasted_iota(jnp.int32, (count, lanes), 1)
+    return lane == line + shift
+
+
+def pack_notes(notes, lanes):
+    count = notes[0].shape[0]
+    total = None
+    for i, note in enumerate(notes):
+        term = jnp.where(note_masks(count, lanes, i * count), note, 0.0)
+        total = term if total is None else total + term
+    row = jnp.sum(total, axis=0, keepdims=True)
+    return jnp.broadcast_to(row, (SUB, lanes)).astype(jnp.int32)
+
+
+def unpack_notes(row, count, number):
+    lanes = row.shape[1]
+    row = row.astype(jnp.float32)
+    return [
+        jnp.sum(jnp.where(note_masks(count, lanes, i * count), row, 0.0), axis=1, keepdims=True)
+        for i in range(number)
+    ]
+
+
+def put(out, d, re, im):
+    count, lanes = re.shape
+    words, notes = encode(re, im)
+    out[d, :count] = words
+    out[d, count:] = pack_notes(notes, lanes)
+
+
+def take(ref, d):
+    count = ref.shape[1] - SUB
+    return decode(ref[d, :count], unpack_notes(ref[d, count:][0:1], count, 3))
+
+
 def row_kernel(place, own, *refs):
     *others, rims, table, out = refs
     groups, pair, rows, lanes = own.shape
-    sky, part = out.shape[0], out.shape[3]
+    sky = out.shape[0]
+    part = lanes // sky
     line = lax.broadcasted_iota(jnp.int32, (rows, lanes), 0)
+    spectra = []
     for g in range(groups):
         sides = []
         for j in range(pair):
@@ -276,15 +345,18 @@
             side = side + jnp.where(line == 0, rims[0, g, j : j + 1, :], 0.0)
             side = side + jnp.where(line == rows - 1, rims[1, g, j : j + 1, :], 0.0)
             sides.append(side)
-        modes = dot(table[place[0] * groups + g], jnp.concatenate(sides, axis=1), ((1,), (1,)))
-        for d in range(sky):
-            for j in range(pair):
-                begin = j * lanes + d * part
-                out[d, g, j] = modes[begin : begin + part]
-
-
-def column_kernel(length, layers, place, modes, forward, twist, *outs):
-    sky, groups, pair, part, rows = modes.shape
+        spectra.append(dot(table[place[0] * groups + g], jnp.concatenate(sides, axis=1), ((1,), (1,))))
+    for d in range(sky):
+        re, im = [
+            jnp.concatenate([z[j * lanes + d * part : j * lanes + (d + 1) * part] for z in spectra], axis=0)
+            for j in range(pair)
+        ]
+        put(out, d, re, im)
+
+
+def column_kernel(length, layers, groups, place, modes, forward, twist, *outs):
+    sky, _, rows = modes.shape
+    part = LANES // sky
     classes = length // LANES // 2
     tiles = 2 * classes
     count = groups * part
@@ -309,8 +381,7 @@
     zero = jnp.zeros((extra, rows), jnp.float32)
     items = []
     for s in range(sky):
-        re = jnp.concatenate([modes[s, g, 0] for g in range(groups)], axis=0)
-        im = jnp.concatenate([modes[s, g, 1] for g in range(groups)], axis=0)
+        re, im = take(modes, s)
         spare = jnp.broadcast_to(im[0:1], (extra, rows))
         re = jnp.concatenate([re, spare], axis=0)
         im = jnp.concatenate([im, zero], axis=0)
@@ -345,37 +416,70 @@
         for s in range(sky):
             re, im = items[s]
             im = jnp.where(packed, jnp.broadcast_to(re[count : count + 1], (total, rows)), im)
-            for g in range(groups):
-                outs[field][s, g, 0] = re[g * part : (g + 1) * part]
-                outs[field][s, g, 1] = im[g * part : (g + 1) * part]
-
-
-def plane_kernel(place, modes, table, mix, out):
-    sky, groups, pair, part, rows = modes.shape
-    parts, _, width = out.shape
-    tiles = parts * width // LANES
+            put(outs[field], s, re[:count], im[:count])
+
+
+def plane_kernel(groups, place, modes, table, mix, own, *outs):
+    sky, _, rows = modes.shape
+    part = LANES // sky
+    width = own.shape[1]
+    parts = len(outs) + 1
+    inner = width // LANES
+    halves = inner // 2
+    blocks = [take(modes, d) for d in range(sky)]
     pieces = []
     for g in range(groups):
-        z = jnp.concatenate([modes[d, g, j] for j in range(pair) for d in range(sky)], axis=0)
+        z = jnp.concatenate([block[j][g * part : (g + 1) * part] for j in range(2) for block in blocks], axis=0)
         both = dot(z, table[place[0] * groups + g], ((0,), (0,)))
         pieces.append((both[:, :LANES], both[:, LANES:]))
-    for s in range(tiles):
-        total = None
-        for g in range(groups):
-            kind = place[0] * groups + g
-            term = mix[kind, 2 * s] * pieces[g][0] + mix[kind, 2 * s + 1] * pieces[g][1]
-            total = term if total is None else total + term
-        at = s * LANES
-        relative = lax.rem(at // width - place[0] + parts, parts)
-        out[relative, :, at % width : at % width + LANES] = total
-
-
-def call(kernel, shapes, specs, scratch=(), work=1, grid=()):
+    for relative in range(parts):
+        owner = lax.rem(place[0] + relative, parts)
+        sums = []
+        for i in range(inner):
+            total = None
+            for g in range(groups):
+                kind = place[0] * groups + g
+                at = 2 * (owner * inner + i)
+                term = mix[kind, at] * pieces[g][0] + mix[kind, at + 1] * pieces[g][1]
+                total = term if total is None else total + term
+            sums.append(total)
+        if relative == 0:
+            for i in range(inner):
+                own[:, i * LANES : (i + 1) * LANES] = sums[i]
+        else:
+            out = outs[relative - 1]
+            words, notes = encode(
+                jnp.concatenate(sums[:halves], axis=1), jnp.concatenate(sums[halves:], axis=1)
+            )
+            out[:rows] = words
+            for i, note in enumerate(notes):
+                out[rows + i * SUB : rows + (i + 1) * SUB, :LANES] = pack_notes([note], LANES)
+                for tile in range(1, halves):
+                    out[rows + i * SUB : rows + (i + 1) * SUB, tile * LANES : (tile + 1) * LANES] = jnp.zeros(
+                        (SUB, LANES), jnp.int32
+                    )
+
+
+def join_kernel(own, *refs):
+    *others, out = refs
+    rows, width = own.shape
+    totals = [own[:, : width // 2], own[:, width // 2 :]]
+    for other in others:
+        notes = [unpack_notes(other[rows + i * SUB : rows + i * SUB + 1, :LANES], rows, 1)[0] for i in range(3)]
+        for half, values in enumerate(decode(other[:rows], notes)):
+            totals[half] = totals[half] + values
+    out[:, : width // 2] = totals[0]
+    out[:, width // 2 :] = totals[1]
+
+
+def call(kernel, shapes, specs, scratch=(), work=1, grid=(), types=jnp.float32):
+    if not isinstance(types, tuple):
+        types = jax.tree.map(lambda shape: types, shapes, is_leaf=lambda s: isinstance(s[0], int))
     return pl.pallas_call(
         kernel,
         grid=grid,
         out_shape=jax.tree.map(
-            lambda shape: jax.ShapeDtypeStruct(shape, jnp.float32), shapes, is_leaf=lambda s: isinstance(s[0], int)
+            jax.ShapeDtypeStruct, shapes, types, is_leaf=lambda s: isinstance(s[0], int)
         ),
         in_specs=specs,
         out_specs=jax.tree.map(lambda shape: VMEM, shapes, is_leaf=lambda s: isinstance(s[0], int)),
@@ -454,32 +558,38 @@
     for shift in range(1, los_count):
         gathered = gathered + to_shift(rims_of(shift), shift)
     table = row_table(width)
-    block = (sky_count, groups, 2, part, rows)
-    modes = call(row_kernel, block, [SMEM] + [VMEM] * (los_count + 2))(place, folded[0], *others, gathered, table)
+    block = (sky_count, groups * part + SUB, rows)
+    modes = call(row_kernel, block, [SMEM] + [VMEM] * (los_count + 2), types=jnp.int32)(
+        place, folded[0], *others, gathered, table
+    )
     modes = lax.all_to_all(modes, "sky", split_axis=0, concat_axis=0, tiled=True)
     forward, twist = column_tables(length, sky_count)
     fields = call(
-        functools.partial(column_kernel, length, layers * los_count),
+        functools.partial(column_kernel, length, layers * los_count, groups),
         (block, block),
         [SMEM, VMEM, VMEM, VMEM],
+        types=jnp.int32,
     )(place, modes, forward, twist)
     mix = tile_table(width)
+    out_width = width // los_count
+    shapes = ((rows, out_width),) + ((rows + 3 * SUB, out_width // 2),) * (los_count - 1)
     results = []
     for field in fields:
         if results:
             field, results[0] = lax.optimization_barrier((field, results[0]))
         field = lax.all_to_all(field, "sky", split_axis=0, concat_axis=0, tiled=True)
         results.append(
-            call(plane_kernel, (los_count, rows, width // los_count), [SMEM, VMEM, VMEM, SMEM])(
-                place, field, table, mix
-            )
+            call(
+                functools.partial(plane_kernel, groups),
+                shapes,
+                [SMEM, VMEM, VMEM, SMEM],
+                types=(jnp.float32,) + (jnp.int32,) * (los_count - 1),
+            )(place, field, table, mix)
         )
     planes = []
-    for result in results:
-        plane = result[0]
-        for shift in range(1, los_count):
-            plane = plane + to_shift(result[shift], shift)
-        planes.append(plane)
+    for own, *sent in results:
+        got = [to_shift(words, shift) for shift, words in enumerate(sent, 1)]
+        planes.append(call(join_kernel, (rows, out_width), [VMEM] * los_count)(own, *got))
     return tuple(planes)
 
 

time: 151 us -> 137 us (0.907)
  waiting for transfers between devices: 28.5 us -> 20 us
  blocking collectives: 37.5 us -> 31 us
  Pallas kernels: 40.4 us -> 46 us
  other arithmetic: 5.84 us -> 3.01 us
    ppermute x4, waiting for transfers between devices: 15.4 us -> 9.04 us  [to_shift(): lax.ppermute(values, 'los', [(i, (i + shift) % los_count) for i in range(...]
    pallas_call x4 -> x6, Pallas kernels: 16 us -> 21.5 us  [the longest x2 7.92 us: body(): call(functools.partial(plane_kernel, groups), shapes, [SMEM, VMEM, VMEM,...]
    all_to_all x1, blocking collectives: 18.5 us -> 15.3 us  [body(): lax.all_to_all(field, 'sky', split_axis=0, concat_axis=0, tiled=True)]
    all_to_all x1, blocking collectives: 19 us -> 15.8 us  [body(): lax.all_to_all(modes, 'sky', split_axis=0, concat_axis=0, tiled=True)]
    add x2 -> x0, other arithmetic: 2.75 us -> none  [body(): plane = plane + to_shift(result[shift], shift)]
    squeeze x2 -> x0, local copies, waits for them, and re-layouts: 2.15 us -> none  [body(): plane = plane + to_shift(result[shift], shift)]
    all_to_all x1, waiting for transfers between devices: 11.7 us -> 9.59 us  [body(): lax.all_to_all(field, 'sky', split_axis=0, concat_axis=0, tiled=True)]
    unnamed x22 -> x24, local copies, waits for them, and re-layouts: 2.6 us -> 3.96 us
  transfers between devices with their start and end apart: 11 -> 11, of which waited for: 4 -> 4; matrix products, arithmetic and copies ran while one was open for 6% -> 5% of each run, Pallas kernels for 13% -> 16%
where the time goes in v3:
time: 137 us; the launch traced here: 136 us
  Pallas kernels  46 us (34%)
  blocking collectives  31 us (23%)
  starting transfers between devices  24.2 us (18%)
  waiting for transfers between devices  20 us (15%)
  local copies, waits for them, and re-layouts  10.8 us (8%)
  other arithmetic  3.01 us (2%)
    all_to_all x1, blocking collectives, body(): lax.all_to_all(modes, 'sky', split_axis=0, concat_axis=0, tiled=True)  15.8 us
    pallas_call x1, Pallas kernels, body(): call(sums_kernel, (4, rows, width), [VMEM, SMEM, SMEM], [pltpu.VMEM((laye...  15.5 us
    all_to_all x1, blocking collectives, body(): lax.all_to_all(field, 'sky', split_axis=0, concat_axis=0, tiled=True)  15.3 us
    all_to_all x1, waiting for transfers between devices, body(): lax.all_to_all(field, 'sky', split_axis=0, concat_axis=0, tiled=True)  9.59 us
    ppermute x4, waiting for transfers between devices, to_shift(): lax.ppermute(values, 'los', [(i, (i + shift) % los_count) for i in range(...  9.04 us
    pallas_call x1, Pallas kernels, body(): call(edge_kernel, ((los_count, groups, 2, rows, LANES), (2, classes, 2, L...  8.92 us
    pallas_call x2, Pallas kernels, body(): call(functools.partial(plane_kernel, groups), shapes, [SMEM, VMEM, VMEM,...  7.92 us
    ppermute x4, starting transfers between devices, to_shift(): lax.ppermute(values, 'los', [(i, (i + shift) % los_count) for i in range(...  5.53 us
  transfers between devices with their start and end apart: 11, of which 4 were waited for; matrix products, arithmetic and copies ran while one was open for 5% of the time, Pallas kernels for 16%

profile of v3, /device:TPU:0, one launch (start us, length us, event | category | flops | bytes accessed | tf_op | source)
XLA Modules:
  0.0 135.9 jit_solution(177031727542755959)
XLA Ops:
  0.6 1.3 slice_bitcast_fusion.2
  1.9 4.9 %collective-permute-start = (bf16[128,2048]{1,0:T(8,128)(2,1)S(1)}, bf16[128,2048]{1,0:T(8,128)(2,1)S(1)}, u32[]{:S(2)}, u32[]{:S(2)}) collective-permute-start(bf16[128,2048]{1,0:T(8,128)(2,1)S(1)} %get-tuple-element.29), channel_id=1, source_target_pairs={{0,16},{1,17},{2,18},{3,19},{4,20},{5,21},{6,22},{7,23},{8,24},{9,... | collective-permute-start | bytes 1572872 | tf_op jit(solution)/shard_map/ppermute | solution.py:512
  6.8 1.3 collective-permute-start.1
  8.1 1.4 %fusion.3 = (bf16[8,1,2048]{2,1,0:T(2,128)(2,1)S(1)}, bf16[8,1,2048]{2,1,0:T(2,128)(2,1)S(1)}, bf16[8,1,2048]{2,1,0:T(2,128)(2,1)S(1)}, bf16[8,1,2048]{2,1,0:T(2,128)(2,1)S(1)}) fusion(bf16[8,128,2048]{2,1,0:T(8,128)(2,1)} %high.1), kind=kLoop, calls=%fused_computation.21 | loop fusion | bytes 262144 | tf_op jit(solution)/shard_map/slice | solution.py:515
  9.6 0.0 copy-start.6
  9.6 0.1 collective-permute-start.2
  9.7 0.0 copy-start.7
  9.7 4.5 %collective-permute-start.3 = (bf16[8,2048]{1,0:T(8,128)(2,1)S(1)}, bf16[8,2048]{1,0:T(8,128)(2,1)S(1)}, u32[]{:S(2)}, u32[]{:S(2)}) collective-permute-start(bf16[8,2048]{1,0:T(8,128)(2,1)S(1)} %bitcast.32), channel_id=1, source_target_pairs={{1,0},{2,1},{3,2},{4,3},{5,4},{6,5},{7,6},{8,7},{9,8},{10,9},{11,1... | collective-permute-start | bytes 98312 | tf_op jit(solution)/shard_map/ppermute | solution.py:517
  14.2 0.6 pad_add_fusion.place
  14.8 1.2 subtract_multiply_fusion
  16.0 0.0 copy-start.10
  16.0 0.7 copy_bitcast_fusion
  16.7 0.6 add_convert_fusion.keep
  17.3 0.7 copy.14.column_average
  17.9 0.0 copy-done.10
  17.9 15.5 %shard_map.95.sums = f32[4,128,2048]{2,1,0:T(8,128)} custom-call(bf16[8,128,2048]{2,1,0:T(8,128)(2,1)} %high.1, f32[8]{0:T(128)} %copy-done.10, f32[8]{0:T(128)} %get-tuple-element.34.slope), custom_call_target="tpu_custom_call" | custom-call | flops 40000000 | bytes 40000000 | tf_op jit(solution)/shard_map/pallas_call | solution.py:521
  33.4 0.0 copy-done.6
  33.4 0.0 copy-done.7
  33.4 0.0 collective-permute-done.2.before
  33.4 0.0 copy-start.8
  33.5 0.0 collective-permute-done.3.after
  33.5 0.0 copy-start.9
  33.5 0.0 collective-permute-done.below
  33.5 0.0 copy-start.2
  33.5 0.0 collective-permute-done.1.above
  33.5 0.0 copy-start.3
  33.5 0.5 copy-done.8
  34.1 0.0 copy-done.9
  34.1 0.2 copy-done.2
  34.3 0.2 copy-done.3
  34.5 8.9 %shard_map.96 = (f32[2,4,2,128,128]{4,3,2,1,0:T(8,128)}, f32[2,8,2,128]{3,2,1,0:T(2,128)}) custom-call(f32[4,128,2048]{2,1,0:T(8,128)} %shard_map.95.sums, bf16[8,128,2048]{2,1,0:T(8,128)(2,1)} %high.1, bf16[8,128,2048]{2,1,0:T(8,128)(2,1)} %high.1, bf16[128,2048]{1,0:T(8,128)(2,1)} %copy-done.2, bf16[128,2048]{1,0:T(8,128)(2,1)} %copy-done.3, ...), custom_call_target="tpu_custom_call" | custom-call | flops 1 | bytes 1 | tf_op jit(solution)/shard_map/pallas_call | solution.py:529
  43.4 2.1 %slice_bitcast_fusion = (f32[4,2,128,128]{3,2,1,0:T(8,128)S(1)}, f32[4,2,128,128]{3,2,1,0:T(8,128)}) fusion(f32[2,4,2,128,128]{4,3,2,1,0:T(8,128)} %get-tuple-element.13), kind=kLoop, calls=%fused_computation | loop fusion | bytes 2097152 | tf_op jit(solution)/shard_map/squeeze | solution.py:549
  45.5 2.7 %collective-permute-start.4 = (f32[4,2,128,128]{3,2,1,0:T(8,128)S(1)}, f32[4,2,128,128]{3,2,1,0:T(8,128)S(1)}, u32[]{:S(2)}, u32[]{:S(2)}) collective-permute-start(f32[4,2,128,128]{3,2,1,0:T(8,128)S(1)} %get-tuple-element.30), channel_id=1, source_target_pairs={{0,16},{16,0},{1,17},{17,1},{2,18},{18,2},{3,19},{19,3},{4,20},{20... | collective-permute-start | bytes 1572872 | tf_op jit(solution)/shard_map/ppermute | solution.py:510
  48.1 0.7 slice_bitcast_fusion.4
  48.8 0.0 collective-permute-start.5
  48.8 4.4 %collective-permute-start.6 = (f32[8,2,128]{2,1,0:T(2,128)S(1)}, f32[8,2,128]{2,1,0:T(2,128)S(1)}, u32[]{:S(2)}, u32[]{:S(2)}) collective-permute-start(f32[8,2,128]{2,1,0:T(2,128)S(1)} %get-tuple-element.32), channel_id=1, source_target_pairs={{1,0},{2,1},{3,2},{4,3},{5,4},{6,5},{7,6},{8,7},{9,8},{10,9},{11,1... | collective-permute-start | bytes 24584 | tf_op jit(solution)/shard_map/ppermute | solution.py:551
  53.3 1.3 collective-permute-done.5
  54.6 0.0 collective-permute-done.6
  54.7 0.0 collective-permute-start.7
  54.7 3.6 %collective-permute-done.7 = f32[2,4,2,128]{3,2,1,0:T(2,128)S(1)} collective-permute-done((f32[2,4,2,128]{3,2,1,0:T(2,128)S(1)}, f32[2,4,2,128]{3,2,1,0:T(2,128)S(1)}, u32[]{:S(2)}, u32[]{:S(2)}) %collective-permute-start.7) | collective-permute-done | bytes 8224 | tf_op jit(solution)/shard_map/ppermute | solution.py:510
  58.4 0.6 fusion.2.refs_1_
  59.0 0.0 collective-permute-done.4.refs_0_
  59.0 0.0 copy-start.1
  59.0 0.8 copy-done.1
  59.8 4.2 %shard_map.97 = s32[16,40,128]{2,1,0:T(8,128)} custom-call(s32[2]{0:T(128)} %pad_add_fusion.place, f32[4,2,128,128]{3,2,1,0:T(8,128)} %get-tuple-element.31.own, f32[4,2,128,128]{3,2,1,0:T(8,128)} %copy-done.1, f32[2,4,2,128]{3,2,1,0:T(2,128)} %fusion.2.refs_1_, f32[8,256,256]{2,1,0:T(8,128)} %constant.44.clone.refs_2_.table), custom_call_target="tpu_custom_call" | custom-call | flops 1 | bytes 1 | tf_op jit(solution)/shard_map/pallas_call | solution.py:562
  63.9 15.8 %all_to_all.15.modes = s32[16,40,128]{2,1,0:T(8,128)} all-to-all(s32[16,40,128]{2,1,0:T(8,128)} %shard_map.97), channel_id=1, replica_groups=mesh['los'=2,'sky'=16] {'sky'}, dimensions={0} | all-to-all | bytes 655360 | tf_op jit(solution)/shard_map/all_to_all | solution.py:565
  79.7 5.3 %shard_map.98 = (s32[16,40,128]{2,1,0:T(8,128)}, s32[16,40,128]{2,1,0:T(8,128)}) custom-call(s32[2]{0:T(128)} %pad_add_fusion.place, s32[16,40,128]{2,1,0:T(8,128)} %all_to_all.15.modes, f32[256,256]{1,0:T(8,128)} %constant.45.clone.forward, f32[16,2,128]{2,1,0:T(2,128)} %constant.46.clone.twist), custom_call_target="tpu_custom_call" | custom-call | flops 1 | bytes 1 | tf_op jit(solution)/shard_map/pallas_call | solution.py:567
  85.0 15.3 %all_to_all.16.modes = s32[16,40,128]{2,1,0:T(8,128)} all-to-all(s32[16,40,128]{2,1,0:T(8,128)} %get-tuple-element.16), channel_id=1, replica_groups=mesh['los'=2,'sky'=16] {'sky'}, dimensions={0} | all-to-all | bytes 655360 | tf_op jit(solution)/shard_map/all_to_all | solution.py:580
  100.3 4.0 %shard_map.99 = (f32[128,1024]{1,0:T(8,128)}, s32[152,512]{1,0:T(8,128)}) custom-call(s32[2]{0:T(128)} %pad_add_fusion.place, s32[16,40,128]{2,1,0:T(8,128)} %all_to_all.16.modes, f32[8,256,256]{2,1,0:T(8,128)} %constant.44.clone.refs_2_.table, f32[8,32]{1,0:T(8,128)} %constant.47.clone.mix), custom_call_target="tpu_custom_call" | custom-call | flops 1 | bytes 1 | tf_op jit(solution)/shard_map/pallas_call | solution.py:582
  104.2 3.5 %all-to-all-start.2 = ((s32[16,40,128]{2,1,0:T(8,128)}), s32[16,40,128]{2,1,0:T(8,128)S(1)}, u32[]{:S(2)}, u32[]{:S(2)}) async-start(s32[16,40,128]{2,1,0:T(8,128)} %get-tuple-element.21), calls=%async_computation.2 | async-start | bytes 655360 | tf_op jit(solution)/shard_map/all_to_all | solution.py:580
  107.8 1.4 %collective-permute-start.8 = (s32[152,512]{1,0:T(8,128)}, s32[152,512]{1,0:T(8,128)S(1)}, u32[]{:S(2)}, u32[]{:S(2)}) collective-permute-start(s32[152,512]{1,0:T(8,128)} %get-tuple-element.20), channel_id=1, source_target_pairs={{0,16},{16,0},{1,17},{17,1},{2,18},{18,2},{3,19},{19,3},{4,20},{20... | collective-permute-start | bytes 933896 | tf_op jit(solution)/shard_map/ppermute | solution.py:510
  109.2 9.6 %all-to-all-done.2.modes = s32[16,40,128]{2,1,0:T(8,128)S(1)} async-done(((s32[16,40,128]{2,1,0:T(8,128)}), s32[16,40,128]{2,1,0:T(8,128)S(1)}, u32[]{:S(2)}, u32[]{:S(2)}) %all-to-all-start.2) | async-done | bytes 327712 | tf_op jit(solution)/shard_map/all_to_all | solution.py:580
  118.8 0.0 copy-start
  118.8 0.7 copy-done
  119.5 4.0 %shard_map.101 = (f32[128,1024]{1,0:T(8,128)}, s32[152,512]{1,0:T(8,128)}) custom-call(s32[2]{0:T(128)} %pad_add_fusion.place, s32[16,40,128]{2,1,0:T(8,128)} %copy-done, f32[8,256,256]{2,1,0:T(8,128)} %constant.44.clone.refs_2_.table, f32[8,32]{1,0:T(8,128)} %constant.47.clone.mix), custom_call_target="tpu_custom_call" | custom-call | flops 1 | bytes 1 | tf_op jit(solution)/shard_map/pallas_call | solution.py:582
  123.5 1.4 %collective-permute-start.9 = (s32[152,512]{1,0:T(8,128)}, s32[152,512]{1,0:T(8,128)S(1)}, u32[]{:S(2)}, u32[]{:S(2)}) collective-permute-start(s32[152,512]{1,0:T(8,128)} %get-tuple-element.23), channel_id=1, source_target_pairs={{0,16},{16,0},{1,17},{17,1},{2,18},{18,2},{3,19},{19,3},{4,20},{20... | collective-permute-start | bytes 933896 | tf_op jit(solution)/shard_map/ppermute | solution.py:510
  124.9 0.0 collective-permute-done.8.refs_0_
  124.9 0.0 copy-start.4
  124.9 0.7 copy-done.4
  125.6 2.1 %shard_map.100 = f32[128,1024]{1,0:T(8,128)} custom-call(f32[128,1024]{1,0:T(8,128)} %get-tuple-element.19.own, s32[152,512]{1,0:T(8,128)} %copy-done.4), custom_call_target="tpu_custom_call" | custom-call | flops 1 | bytes 1 | tf_op jit(solution)/shard_map/pallas_call | solution.py:592
  127.7 5.4 %collective-permute-done.9.refs_0_ = s32[152,512]{1,0:T(8,128)S(1)} collective-permute-done((s32[152,512]{1,0:T(8,128)}, s32[152,512]{1,0:T(8,128)S(1)}, u32[]{:S(2)}, u32[]{:S(2)}) %collective-permute-start.9) | collective-permute-done | bytes 311328 | tf_op jit(solution)/shard_map/ppermute | solution.py:510
  133.1 0.0 copy-start.5
  133.1 0.7 copy-done.5
  133.8 2.1 %shard_map.102 = f32[128,1024]{1,0:T(8,128)} custom-call(f32[128,1024]{1,0:T(8,128)} %get-tuple-element.22.own, s32[152,512]{1,0:T(8,128)} %copy-done.5), custom_call_target="tpu_custom_call" | custom-call | flops 1 | bytes 1 | tf_op jit(solution)/shard_map/pallas_call | solution.py:592
  (3 shorter events, 0.1 us)
Async XLA Ops:
  1.9 31.6 %collective-permute-start = (bf16[128,2048]{1,0:T(8,128)(2,1)S(1)}, bf16[128,2048]{1,0:T(8,128)(2,1)S(1)}, u32[]{:S(2)}, u32[]{:S(2)}) collective-permute-start(bf16[128,2048]{1,0:T(8,128)(2,1)S(1)} %get-tuple-element.29), channel_id=1, source_target_pairs={{0,16},{1,17},{2,18},{3,19},{4,20},{5,21},{6,22},{7,23},{8,24},{9,... | collective-permute-start | bytes 1572872 | tf_op jit(solution)/shard_map/ppermute | solution.py:512
  6.8 26.7 %collective-permute-start.1 = (bf16[128,2048]{1,0:T(8,128)(2,1)S(1)}, bf16[128,2048]{1,0:T(8,128)(2,1)S(1)}, u32[]{:S(2)}, u32[]{:S(2)}) collective-permute-start(bf16[128,2048]{1,0:T(8,128)(2,1)S(1)} %get-tuple-element.28), channel_id=1, source_target_pairs={{16,0},{17,1},{18,2},{19,3},{20,4},{21,5},{22,6},{23,7},{24,8},{25... | collective-permute-start | bytes 1572872 | tf_op jit(solution)/shard_map/ppermute | solution.py:513
  9.6 23.9 %copy-start.6 = (bf16[8,1,2048]{2,0,1:T(8,128)(2,1)}, bf16[8,1,2048]{2,0,1:T(8,128)(2,1)S(1)}, u32[]{:S(2)}) copy-start(bf16[8,1,2048]{2,0,1:T(8,128)(2,1)S(1)} %copy.24) | copy-start | bytes 98308
  9.6 23.8 %collective-permute-start.2 = (bf16[8,2048]{1,0:T(8,128)(2,1)S(1)}, bf16[8,2048]{1,0:T(8,128)(2,1)S(1)}, u32[]{:S(2)}, u32[]{:S(2)}) collective-permute-start(bf16[8,2048]{1,0:T(8,128)(2,1)S(1)} %bitcast.30), channel_id=1, source_target_pairs={{0,1},{1,2},{2,3},{3,4},{4,5},{5,6},{6,7},{7,8},{8,9},{9,10},{10,1... | collective-permute-start | bytes 98312 | tf_op jit(solution)/shard_map/ppermute | solution.py:516
  9.7 23.7 %copy-start.7 = (bf16[8,1,2048]{2,0,1:T(8,128)(2,1)}, bf16[8,1,2048]{2,0,1:T(8,128)(2,1)S(1)}, u32[]{:S(2)}) copy-start(bf16[8,1,2048]{2,0,1:T(8,128)(2,1)S(1)} %copy.23) | copy-start | bytes 98308
  9.7 23.8 %collective-permute-start.3 = (bf16[8,2048]{1,0:T(8,128)(2,1)S(1)}, bf16[8,2048]{1,0:T(8,128)(2,1)S(1)}, u32[]{:S(2)}, u32[]{:S(2)}) collective-permute-start(bf16[8,2048]{1,0:T(8,128)(2,1)S(1)} %bitcast.32), channel_id=1, source_target_pairs={{1,0},{2,1},{3,2},{4,3},{5,4},{6,5},{7,6},{8,7},{9,8},{10,9},{11,1... | collective-permute-start | bytes 98312 | tf_op jit(solution)/shard_map/ppermute | solution.py:517
  16.0 1.9 %copy-start.10 = (f32[8]{0:T(128)}, f32[8]{0:T(128)S(1)}, u32[]{:S(2)}) copy-start(f32[8]{0:T(128)S(1)} %get-tuple-element.35.average) | copy-start | bytes 100
  33.4 0.6 copy-start.8
  33.5 0.6 copy-start.9
  33.5 0.8 copy-start.2
  33.5 0.9 copy-start.3
  45.5 13.5 %collective-permute-start.4 = (f32[4,2,128,128]{3,2,1,0:T(8,128)S(1)}, f32[4,2,128,128]{3,2,1,0:T(8,128)S(1)}, u32[]{:S(2)}, u32[]{:S(2)}) collective-permute-start(f32[4,2,128,128]{3,2,1,0:T(8,128)S(1)} %get-tuple-element.30), channel_id=1, source_target_pairs={{0,16},{16,0},{1,17},{17,1},{2,18},{18,2},{3,19},{19,3},{4,20},{20... | collective-permute-start | bytes 1572872 | tf_op jit(solution)/shard_map/ppermute | solution.py:510
  48.8 5.8 %collective-permute-start.5 = (f32[8,2,128]{2,1,0:T(2,128)S(1)}, f32[8,2,128]{2,1,0:T(2,128)S(1)}, u32[]{:S(2)}, u32[]{:S(2)}) collective-permute-start(f32[8,2,128]{2,1,0:T(2,128)S(1)} %get-tuple-element.33), channel_id=1, source_target_pairs={{0,1},{1,2},{2,3},{3,4},{4,5},{5,6},{6,7},{7,8},{8,9},{9,10},{10,1... | collective-permute-start | bytes 24584 | tf_op jit(solution)/shard_map/ppermute | solution.py:550
  48.8 5.8 %collective-permute-start.6 = (f32[8,2,128]{2,1,0:T(2,128)S(1)}, f32[8,2,128]{2,1,0:T(2,128)S(1)}, u32[]{:S(2)}, u32[]{:S(2)}) collective-permute-start(f32[8,2,128]{2,1,0:T(2,128)S(1)} %get-tuple-element.32), channel_id=1, source_target_pairs={{1,0},{2,1},{3,2},{4,3},{5,4},{6,5},{7,6},{8,7},{9,8},{10,9},{11,1... | collective-permute-start | bytes 24584 | tf_op jit(solution)/shard_map/ppermute | solution.py:551
  54.7 3.7 %collective-permute-start.7 = (f32[2,4,2,128]{3,2,1,0:T(2,128)S(1)}, f32[2,4,2,128]{3,2,1,0:T(2,128)S(1)}, u32[]{:S(2)}, u32[]{:S(2)}) collective-permute-start(f32[2,4,2,128]{3,2,1,0:T(2,128)S(1)} %fusion), channel_id=1, source_target_pairs={{0,16},{16,0},{1,17},{17,1},{2,18},{18,2},{3,19},{19,3},{4,20},{20... | collective-permute-start | bytes 24584 | tf_op jit(solution)/shard_map/ppermute | solution.py:510
  59.0 0.8 copy-start.1
  104.2 14.6 %all-to-all-start.2 = ((s32[16,40,128]{2,1,0:T(8,128)}), s32[16,40,128]{2,1,0:T(8,128)S(1)}, u32[]{:S(2)}, u32[]{:S(2)}) async-start(s32[16,40,128]{2,1,0:T(8,128)} %get-tuple-element.21), calls=%async_computation.2 | async-start | bytes 655360 | tf_op jit(solution)/shard_map/all_to_all | solution.py:580
  107.8 17.1 %collective-permute-start.8 = (s32[152,512]{1,0:T(8,128)}, s32[152,512]{1,0:T(8,128)S(1)}, u32[]{:S(2)}, u32[]{:S(2)}) collective-permute-start(s32[152,512]{1,0:T(8,128)} %get-tuple-element.20), channel_id=1, source_target_pairs={{0,16},{16,0},{1,17},{17,1},{2,18},{18,2},{3,19},{19,3},{4,20},{20... | collective-permute-start | bytes 933896 | tf_op jit(solution)/shard_map/ppermute | solution.py:510
  118.8 0.7 copy-start
  123.5 9.6 %collective-permute-start.9 = (s32[152,512]{1,0:T(8,128)}, s32[152,512]{1,0:T(8,128)S(1)}, u32[]{:S(2)}, u32[]{:S(2)}) collective-permute-start(s32[152,512]{1,0:T(8,128)} %get-tuple-element.23), channel_id=1, source_target_pairs={{0,16},{16,0},{1,17},{17,1},{2,18},{18,2},{3,19},{19,3},{4,20},{20... | collective-permute-start | bytes 933896 | tf_op jit(solution)/shard_map/ppermute | solution.py:510
  124.9 0.7 copy-start.4
  133.1 0.7 copy-start.5

commit v4 on v3

--- a/solution.py
+++ b/solution.py
@@ -460,6 +460,52 @@
                     )
 
 
+def exchange_kernel(source, target, send, receive, local):
+    me = lax.axis_index("sky")
+    count = source.shape[0]
+    barrier = pltpu.get_barrier_semaphore()
+    for i in range(1, count):
+        pl.semaphore_signal(
+            barrier, inc=1, device_id={"sky": lax.rem(me + i, count)}, device_id_type=pl.DeviceIdType.MESH
+        )
+    own = pltpu.make_async_copy(source.at[me], target.at[me], local)
+    own.start()
+    pl.semaphore_wait(barrier, count - 1)
+    copies = []
+    for i in range(1, count):
+        peer = lax.rem(me + i, count)
+        copies.append(
+            pltpu.make_async_remote_copy(
+                src_ref=source.at[peer],
+                dst_ref=target.at[me],
+                send_sem=send.at[i],
+                recv_sem=receive.at[i],
+                device_id={"sky": peer},
+                device_id_type=pl.DeviceIdType.MESH,
+            )
+        )
+        copies[-1].start()
+    own.wait()
+    for copy in copies:
+        copy.wait()
+
+
+def exchange(values, number):
+    count = values.shape[0]
+    return pl.pallas_call(
+        exchange_kernel,
+        out_shape=jax.ShapeDtypeStruct(values.shape, values.dtype),
+        in_specs=[VMEM],
+        out_specs=VMEM,
+        scratch_shapes=[
+            pltpu.SemaphoreType.DMA((count,)),
+            pltpu.SemaphoreType.DMA((count,)),
+            pltpu.SemaphoreType.DMA,
+        ],
+        compiler_params=pltpu.CompilerParams(collective_id=number, has_side_effects=True),
+    )(values)
+
+
 def join_kernel(own, *refs):
     *others, out = refs
     rows, width = own.shape
@@ -562,7 +608,7 @@
     modes = call(row_kernel, block, [SMEM] + [VMEM] * (los_count + 2), types=jnp.int32)(
         place, folded[0], *others, gathered, table
     )
-    modes = lax.all_to_all(modes, "sky", split_axis=0, concat_axis=0, tiled=True)
+    modes = exchange(modes, 0)
     forward, twist = column_tables(length, sky_count)
     fields = call(
         functools.partial(column_kernel, length, layers * los_count, groups),
@@ -574,10 +620,10 @@
     out_width = width // los_count
     shapes = ((rows, out_width),) + ((rows + 3 * SUB, out_width // 2),) * (los_count - 1)
     results = []
-    for field in fields:
+    for number, field in enumerate(fields, 1):
         if results:
             field, results[0] = lax.optimization_barrier((field, results[0]))
-        field = lax.all_to_all(field, "sky", split_axis=0, concat_axis=0, tiled=True)
+        field = exchange(field, number)
         results.append(
             call(
                 functools.partial(plane_kernel, groups),

time: 137 us -> 130 us (0.949)
  Pallas kernels: 46 us -> 84.2 us
  blocking collectives: 31 us -> 0 us
  waiting for transfers between devices: 20 us -> 11 us
  starting transfers between devices: 24.2 us -> 19.9 us
    pallas_call x0 -> x3, Pallas kernels: none -> 38.2 us  [exchange(): pl.pallas_call(exchange_kernel, out_shape=jax.ShapeDtypeStruct(values.sha...]
    all_to_all x2 -> x0, blocking collectives: 31 us -> none  [the longest x1 15.8 us: body(): lax.all_to_all(modes, 'sky', split_axis=0, concat_axis=0, tiled=True)]
    all_to_all x1 -> x0, waiting for transfers between devices: 9.59 us -> none  [body(): lax.all_to_all(field, 'sky', split_axis=0, concat_axis=0, tiled=True)]
    all_to_all x1 -> x0, starting transfers between devices: 3.54 us -> none  [body(): lax.all_to_all(field, 'sky', split_axis=0, concat_axis=0, tiled=True)]
    unnamed x24 -> x22, local copies, waits for them, and re-layouts: 3.96 us -> 3.26 us
  transfers between devices with their start and end apart: 11 -> 10, of which waited for: 4 -> 3; matrix products, arithmetic and copies ran while one was open for 5% -> 5% of each run, Pallas kernels for 16% -> 27%
where the time goes in v4:
time: 130 us; the launch traced here: 129 us
  Pallas kernels  84.2 us (65%)
  starting transfers between devices  19.9 us (15%)
  waiting for transfers between devices  11 us (8%)
  local copies, waits for them, and re-layouts  10.1 us (8%)
  other arithmetic  3.08 us (2%)
    pallas_call x3, Pallas kernels, exchange(): pl.pallas_call(exchange_kernel, out_shape=jax.ShapeDtypeStruct(values.sha...  38.2 us
    pallas_call x1, Pallas kernels, body(): call(sums_kernel, (4, rows, width), [VMEM, SMEM, SMEM], [pltpu.VMEM((laye...  15.5 us
    ppermute x4, waiting for transfers between devices, to_shift(): lax.ppermute(values, 'los', [(i, (i + shift) % los_count) for i in range(...  9.64 us
    pallas_call x1, Pallas kernels, body(): call(edge_kernel, ((los_count, groups, 2, rows, LANES), (2, classes, 2, L...  8.9 us
    pallas_call x2, Pallas kernels, body(): call(functools.partial(plane_kernel, groups), shapes, [SMEM, VMEM, VMEM,...  7.94 us
    pallas_call x1, Pallas kernels, body(): call(functools.partial(column_kernel, length, layers * los_count, groups)...  5.32 us
    ppermute x1, starting transfers between devices, body(): below = lax.ppermute(density[layers - 1], 'los', onward)  4.9 us
    ppermute x4, starting transfers between devices, to_shift(): lax.ppermute(values, 'los', [(i, (i + shift) % los_count) for i in range(...  4.74 us
  transfers between devices with their start and end apart: 10, of which 3 were waited for; matrix products, arithmetic and copies ran while one was open for 5% of the time, Pallas kernels for 27%

profile of v4, /device:TPU:0, one launch (start us, length us, event | category | flops | bytes accessed | tf_op | source)
XLA Modules:
  0.0 129.1 jit_solution(14147833219012770301)
XLA Ops:
  0.6 1.3 slice_bitcast_fusion.2
  1.9 4.9 %collective-permute-start = (bf16[128,2048]{1,0:T(8,128)(2,1)S(1)}, bf16[128,2048]{1,0:T(8,128)(2,1)S(1)}, u32[]{:S(2)}, u32[]{:S(2)}) collective-permute-start(bf16[128,2048]{1,0:T(8,128)(2,1)S(1)} %get-tuple-element.29), channel_id=1, source_target_pairs={{0,16},{1,17},{2,18},{3,19},{4,20},{5,21},{6,22},{7,23},{8,24},{9,... | collective-permute-start | bytes 1572872 | tf_op jit(solution)/shard_map/ppermute | solution.py:558
  6.8 1.3 %collective-permute-start.1 = (bf16[128,2048]{1,0:T(8,128)(2,1)S(1)}, bf16[128,2048]{1,0:T(8,128)(2,1)S(1)}, u32[]{:S(2)}, u32[]{:S(2)}) collective-permute-start(bf16[128,2048]{1,0:T(8,128)(2,1)S(1)} %get-tuple-element.28), channel_id=1, source_target_pairs={{16,0},{17,1},{18,2},{19,3},{20,4},{21,5},{22,6},{23,7},{24,8},{25... | collective-permute-start | bytes 1572872 | tf_op jit(solution)/shard_map/ppermute | solution.py:559
  8.1 1.4 %fusion.3 = (bf16[8,1,2048]{2,1,0:T(2,128)(2,1)S(1)}, bf16[8,1,2048]{2,1,0:T(2,128)(2,1)S(1)}, bf16[8,1,2048]{2,1,0:T(2,128)(2,1)S(1)}, bf16[8,1,2048]{2,1,0:T(2,128)(2,1)S(1)}) fusion(bf16[8,128,2048]{2,1,0:T(8,128)(2,1)} %high.1), kind=kLoop, calls=%fused_computation.21 | loop fusion | bytes 262144 | tf_op jit(solution)/shard_map/slice | solution.py:561
  9.6 0.0 copy-start.5
  9.6 0.1 collective-permute-start.2
  9.7 0.0 copy-start.6
  9.7 4.5 %collective-permute-start.3 = (bf16[8,2048]{1,0:T(8,128)(2,1)S(1)}, bf16[8,2048]{1,0:T(8,128)(2,1)S(1)}, u32[]{:S(2)}, u32[]{:S(2)}) collective-permute-start(bf16[8,2048]{1,0:T(8,128)(2,1)S(1)} %bitcast.32), channel_id=1, source_target_pairs={{1,0},{2,1},{3,2},{4,3},{5,4},{6,5},{7,6},{8,7},{9,8},{10,9},{11,1... | collective-permute-start | bytes 98312 | tf_op jit(solution)/shard_map/ppermute | solution.py:563
  14.2 0.7 pad_add_fusion.place
  14.8 1.2 subtract_multiply_fusion
  16.0 0.0 copy-start.9
  16.0 0.7 copy_bitcast_fusion
  16.7 0.6 add_convert_fusion.keep
  17.3 0.7 copy.14.column_average
  18.0 0.0 copy-done.9
  18.0 15.5 %shard_map.95.sums = f32[4,128,2048]{2,1,0:T(8,128)} custom-call(bf16[8,128,2048]{2,1,0:T(8,128)(2,1)} %high.1, f32[8]{0:T(128)} %copy-done.9, f32[8]{0:T(128)} %get-tuple-element.34.slope), custom_call_target="tpu_custom_call" | custom-call | flops 40000000 | bytes 40000000 | tf_op jit(solution)/shard_map/pallas_call | solution.py:567
  33.5 0.0 copy-done.5
  33.5 0.0 copy-done.6
  33.5 0.0 collective-permute-done.2.before
  33.5 0.0 copy-start.7
  33.5 0.0 collective-permute-done.3.after
  33.5 0.0 copy-start.8
  33.5 0.0 collective-permute-done.below
  33.5 0.0 copy-start.1
  33.5 0.0 collective-permute-done.1.above
  33.6 0.0 copy-start.2
  33.6 0.5 copy-done.7
  34.1 0.0 copy-done.8
  34.1 0.2 copy-done.1
  34.3 0.2 copy-done.2
  34.5 8.9 %shard_map.96 = (f32[2,4,2,128,128]{4,3,2,1,0:T(8,128)}, f32[2,8,2,128]{3,2,1,0:T(2,128)}) custom-call(f32[4,128,2048]{2,1,0:T(8,128)} %shard_map.95.sums, bf16[8,128,2048]{2,1,0:T(8,128)(2,1)} %high.1, bf16[8,128,2048]{2,1,0:T(8,128)(2,1)} %high.1, bf16[128,2048]{1,0:T(8,128)(2,1)} %copy-done.1, bf16[128,2048]{1,0:T(8,128)(2,1)} %copy-done.2, ...), custom_call_target="tpu_custom_call" | custom-call | flops 1 | bytes 1 | tf_op jit(solution)/shard_map/pallas_call | solution.py:575
  43.4 2.1 %slice_bitcast_fusion = (f32[4,2,128,128]{3,2,1,0:T(8,128)S(1)}, f32[4,2,128,128]{3,2,1,0:T(8,128)}) fusion(f32[2,4,2,128,128]{4,3,2,1,0:T(8,128)} %get-tuple-element.13), kind=kLoop, calls=%fused_computation | loop fusion | bytes 2097152 | tf_op jit(solution)/shard_map/squeeze | solution.py:595
  45.5 2.7 %collective-permute-start.4 = (f32[4,2,128,128]{3,2,1,0:T(8,128)S(1)}, f32[4,2,128,128]{3,2,1,0:T(8,128)S(1)}, u32[]{:S(2)}, u32[]{:S(2)}) collective-permute-start(f32[4,2,128,128]{3,2,1,0:T(8,128)S(1)} %get-tuple-element.30), channel_id=1, source_target_pairs={{0,16},{16,0},{1,17},{17,1},{2,18},{18,2},{3,19},{19,3},{4,20},{20... | collective-permute-start | bytes 1572872 | tf_op jit(solution)/shard_map/ppermute | solution.py:556
  48.2 0.7 slice_bitcast_fusion.4
  48.9 0.0 collective-permute-start.5
  48.9 4.4 %collective-permute-start.6 = (f32[8,2,128]{2,1,0:T(2,128)S(1)}, f32[8,2,128]{2,1,0:T(2,128)S(1)}, u32[]{:S(2)}, u32[]{:S(2)}) collective-permute-start(f32[8,2,128]{2,1,0:T(2,128)S(1)} %get-tuple-element.32), channel_id=1, source_target_pairs={{1,0},{2,1},{3,2},{4,3},{5,4},{6,5},{7,6},{8,7},{9,8},{10,9},{11,1... | collective-permute-start | bytes 24584 | tf_op jit(solution)/shard_map/ppermute | solution.py:597
  53.3 1.3 %collective-permute-done.5 = f32[8,2,128]{2,1,0:T(2,128)S(1)} collective-permute-done((f32[8,2,128]{2,1,0:T(2,128)S(1)}, f32[8,2,128]{2,1,0:T(2,128)S(1)}, u32[]{:S(2)}, u32[]{:S(2)}) %collective-permute-start.5) | collective-permute-done | bytes 8224 | tf_op jit(solution)/shard_map/ppermute | solution.py:596
  54.6 0.0 collective-permute-done.6
  54.7 0.0 collective-permute-start.7
  54.8 3.6 %collective-permute-done.7 = f32[2,4,2,128]{3,2,1,0:T(2,128)S(1)} collective-permute-done((f32[2,4,2,128]{3,2,1,0:T(2,128)S(1)}, f32[2,4,2,128]{3,2,1,0:T(2,128)S(1)}, u32[]{:S(2)}, u32[]{:S(2)}) %collective-permute-start.7) | collective-permute-done | bytes 8224 | tf_op jit(solution)/shard_map/ppermute | solution.py:556
  58.4 0.6 fusion.2.refs_1_
  59.0 0.0 collective-permute-done.4.refs_0_
  59.0 0.0 copy-start
  59.0 0.8 copy-done
  59.8 4.1 %shard_map.97.source = s32[16,40,128]{2,1,0:T(8,128)} custom-call(s32[2]{0:T(128)} %pad_add_fusion.place, f32[4,2,128,128]{3,2,1,0:T(8,128)} %get-tuple-element.31.own, f32[4,2,128,128]{3,2,1,0:T(8,128)} %copy-done, f32[2,4,2,128]{3,2,1,0:T(2,128)} %fusion.2.refs_1_, f32[8,256,256]{2,1,0:T(8,128)} %constant.44.clone.refs_2_.table), custom_call_target="tpu_custom_call" | custom-call | flops 1 | bytes 1 | tf_op jit(solution)/shard_map/pallas_call | solution.py:608
  63.9 11.7 %shard_map.98.modes = s32[16,40,128]{2,1,0:T(8,128)} custom-call(s32[16,40,128]{2,1,0:T(8,128)} %shard_map.97.source), custom_call_target="tpu_custom_call" | custom-call | tf_op jit(solution)/shard_map/pallas_call | solution.py:495
  75.6 5.3 %shard_map.99 = (s32[16,40,128]{2,1,0:T(8,128)}, s32[16,40,128]{2,1,0:T(8,128)}) custom-call(s32[2]{0:T(128)} %pad_add_fusion.place, s32[16,40,128]{2,1,0:T(8,128)} %shard_map.98.modes, f32[256,256]{1,0:T(8,128)} %constant.45.clone.forward, f32[16,2,128]{2,1,0:T(2,128)} %constant.46.clone.twist), custom_call_target="tpu_custom_call" | custom-call | flops 1 | bytes 1 | tf_op jit(solution)/shard_map/pallas_call | solution.py:613
  80.9 12.9 %shard_map.100.modes = s32[16,40,128]{2,1,0:T(8,128)} custom-call(s32[16,40,128]{2,1,0:T(8,128)} %get-tuple-element.16.source), custom_call_target="tpu_custom_call" | custom-call | tf_op jit(solution)/shard_map/pallas_call | solution.py:495
  93.9 4.0 %shard_map.101 = (f32[128,1024]{1,0:T(8,128)}, s32[152,512]{1,0:T(8,128)}) custom-call(s32[2]{0:T(128)} %pad_add_fusion.place, s32[16,40,128]{2,1,0:T(8,128)} %shard_map.100.modes, f32[8,256,256]{2,1,0:T(8,128)} %constant.44.clone.refs_2_.table, f32[8,32]{1,0:T(8,128)} %constant.47.clone.mix), custom_call_target="tpu_custom_call" | custom-call | flops 1 | bytes 1 | tf_op jit(solution)/shard_map/pallas_call | solution.py:628
  97.9 1.4 %collective-permute-start.8 = (s32[152,512]{1,0:T(8,128)}, s32[152,512]{1,0:T(8,128)S(1)}, u32[]{:S(2)}, u32[]{:S(2)}) collective-permute-start(s32[152,512]{1,0:T(8,128)} %get-tuple-element.20), channel_id=1, source_target_pairs={{0,16},{16,0},{1,17},{17,1},{2,18},{18,2},{3,19},{19,3},{4,20},{20... | collective-permute-start | bytes 933896 | tf_op jit(solution)/shard_map/ppermute | solution.py:556
  99.3 13.6 %shard_map.103.modes = s32[16,40,128]{2,1,0:T(8,128)} custom-call(s32[16,40,128]{2,1,0:T(8,128)} %get-tuple-element.21.source), custom_call_target="tpu_custom_call" | custom-call | tf_op jit(solution)/shard_map/pallas_call | solution.py:495
  112.9 4.0 %shard_map.104 = (f32[128,1024]{1,0:T(8,128)}, s32[152,512]{1,0:T(8,128)}) custom-call(s32[2]{0:T(128)} %pad_add_fusion.place, s32[16,40,128]{2,1,0:T(8,128)} %shard_map.103.modes, f32[8,256,256]{2,1,0:T(8,128)} %constant.44.clone.refs_2_.table, f32[8,32]{1,0:T(8,128)} %constant.47.clone.mix), custom_call_target="tpu_custom_call" | custom-call | flops 1 | bytes 1 | tf_op jit(solution)/shard_map/pallas_call | solution.py:628
  116.8 0.6 collective-permute-start.9
  117.5 0.0 collective-permute-done.8.refs_0_
  117.5 0.0 copy-start.3
  117.5 0.7 copy-done.3
  118.2 2.1 %shard_map.102 = f32[128,1024]{1,0:T(8,128)} custom-call(f32[128,1024]{1,0:T(8,128)} %get-tuple-element.19.own, s32[152,512]{1,0:T(8,128)} %copy-done.3), custom_call_target="tpu_custom_call" | custom-call | flops 1 | bytes 1 | tf_op jit(solution)/shard_map/pallas_call | solution.py:638
  120.3 6.0 %collective-permute-done.9.refs_0_ = s32[152,512]{1,0:T(8,128)S(1)} collective-permute-done((s32[152,512]{1,0:T(8,128)}, s32[152,512]{1,0:T(8,128)S(1)}, u32[]{:S(2)}, u32[]{:S(2)}) %collective-permute-start.9) | collective-permute-done | bytes 311328 | tf_op jit(solution)/shard_map/ppermute | solution.py:556
  126.3 0.0 copy-start.4
  126.3 0.7 copy-done.4
  127.0 2.1 %shard_map.105 = f32[128,1024]{1,0:T(8,128)} custom-call(f32[128,1024]{1,0:T(8,128)} %get-tuple-element.22.own, s32[152,512]{1,0:T(8,128)} %copy-done.4), custom_call_target="tpu_custom_call" | custom-call | flops 1 | bytes 1 | tf_op jit(solution)/shard_map/pallas_call | solution.py:638
  (3 shorter events, 0.1 us)
Async XLA Ops:
  1.9 31.6 %collective-permute-start = (bf16[128,2048]{1,0:T(8,128)(2,1)S(1)}, bf16[128,2048]{1,0:T(8,128)(2,1)S(1)}, u32[]{:S(2)}, u32[]{:S(2)}) collective-permute-start(bf16[128,2048]{1,0:T(8,128)(2,1)S(1)} %get-tuple-element.29), channel_id=1, source_target_pairs={{0,16},{1,17},{2,18},{3,19},{4,20},{5,21},{6,22},{7,23},{8,24},{9,... | collective-permute-start | bytes 1572872 | tf_op jit(solution)/shard_map/ppermute | solution.py:558
  6.8 26.7 %collective-permute-start.1 = (bf16[128,2048]{1,0:T(8,128)(2,1)S(1)}, bf16[128,2048]{1,0:T(8,128)(2,1)S(1)}, u32[]{:S(2)}, u32[]{:S(2)}) collective-permute-start(bf16[128,2048]{1,0:T(8,128)(2,1)S(1)} %get-tuple-element.28), channel_id=1, source_target_pairs={{16,0},{17,1},{18,2},{19,3},{20,4},{21,5},{22,6},{23,7},{24,8},{25... | collective-permute-start | bytes 1572872 | tf_op jit(solution)/shard_map/ppermute | solution.py:559
  9.6 23.9 %copy-start.5 = (bf16[8,1,2048]{2,0,1:T(8,128)(2,1)}, bf16[8,1,2048]{2,0,1:T(8,128)(2,1)S(1)}, u32[]{:S(2)}) copy-start(bf16[8,1,2048]{2,0,1:T(8,128)(2,1)S(1)} %copy.24) | copy-start | bytes 98308
  9.6 23.9 %collective-permute-start.2 = (bf16[8,2048]{1,0:T(8,128)(2,1)S(1)}, bf16[8,2048]{1,0:T(8,128)(2,1)S(1)}, u32[]{:S(2)}, u32[]{:S(2)}) collective-permute-start(bf16[8,2048]{1,0:T(8,128)(2,1)S(1)} %bitcast.30), channel_id=1, source_target_pairs={{0,1},{1,2},{2,3},{3,4},{4,5},{5,6},{6,7},{7,8},{8,9},{9,10},{10,1... | collective-permute-start | bytes 98312 | tf_op jit(solution)/shard_map/ppermute | solution.py:562
  9.7 23.8 %copy-start.6 = (bf16[8,1,2048]{2,0,1:T(8,128)(2,1)}, bf16[8,1,2048]{2,0,1:T(8,128)(2,1)S(1)}, u32[]{:S(2)}) copy-start(bf16[8,1,2048]{2,0,1:T(8,128)(2,1)S(1)} %copy.23) | copy-start | bytes 98308
  9.7 23.8 %collective-permute-start.3 = (bf16[8,2048]{1,0:T(8,128)(2,1)S(1)}, bf16[8,2048]{1,0:T(8,128)(2,1)S(1)}, u32[]{:S(2)}, u32[]{:S(2)}) collective-permute-start(bf16[8,2048]{1,0:T(8,128)(2,1)S(1)} %bitcast.32), channel_id=1, source_target_pairs={{1,0},{2,1},{3,2},{4,3},{5,4},{6,5},{7,6},{8,7},{9,8},{10,9},{11,1... | collective-permute-start | bytes 98312 | tf_op jit(solution)/shard_map/ppermute | solution.py:563
  16.0 2.0 %copy-start.9 = (f32[8]{0:T(128)}, f32[8]{0:T(128)S(1)}, u32[]{:S(2)}) copy-start(f32[8]{0:T(128)S(1)} %get-tuple-element.35.average) | copy-start | bytes 100
  33.5 0.6 copy-start.7
  33.5 0.6 copy-start.8
  33.5 0.8 copy-start.1
  33.6 0.9 copy-start.2
  45.5 13.5 %collective-permute-start.4 = (f32[4,2,128,128]{3,2,1,0:T(8,128)S(1)}, f32[4,2,128,128]{3,2,1,0:T(8,128)S(1)}, u32[]{:S(2)}, u32[]{:S(2)}) collective-permute-start(f32[4,2,128,128]{3,2,1,0:T(8,128)S(1)} %get-tuple-element.30), channel_id=1, source_target_pairs={{0,16},{16,0},{1,17},{17,1},{2,18},{18,2},{3,19},{19,3},{4,20},{20... | collective-permute-start | bytes 1572872 | tf_op jit(solution)/shard_map/ppermute | solution.py:556
  48.9 5.8 %collective-permute-start.5 = (f32[8,2,128]{2,1,0:T(2,128)S(1)}, f32[8,2,128]{2,1,0:T(2,128)S(1)}, u32[]{:S(2)}, u32[]{:S(2)}) collective-permute-start(f32[8,2,128]{2,1,0:T(2,128)S(1)} %get-tuple-element.33), channel_id=1, source_target_pairs={{0,1},{1,2},{2,3},{3,4},{4,5},{5,6},{6,7},{7,8},{8,9},{9,10},{10,1... | collective-permute-start | bytes 24584 | tf_op jit(solution)/shard_map/ppermute | solution.py:596
  48.9 5.8 %collective-permute-start.6 = (f32[8,2,128]{2,1,0:T(2,128)S(1)}, f32[8,2,128]{2,1,0:T(2,128)S(1)}, u32[]{:S(2)}, u32[]{:S(2)}) collective-permute-start(f32[8,2,128]{2,1,0:T(2,128)S(1)} %get-tuple-element.32), channel_id=1, source_target_pairs={{1,0},{2,1},{3,2},{4,3},{5,4},{6,5},{7,6},{8,7},{9,8},{10,9},{11,1... | collective-permute-start | bytes 24584 | tf_op jit(solution)/shard_map/ppermute | solution.py:597
  54.7 3.7 %collective-permute-start.7 = (f32[2,4,2,128]{3,2,1,0:T(2,128)S(1)}, f32[2,4,2,128]{3,2,1,0:T(2,128)S(1)}, u32[]{:S(2)}, u32[]{:S(2)}) collective-permute-start(f32[2,4,2,128]{3,2,1,0:T(2,128)S(1)} %fusion), channel_id=1, source_target_pairs={{0,16},{16,0},{1,17},{17,1},{2,18},{18,2},{3,19},{19,3},{4,20},{20... | collective-permute-start | bytes 24584 | tf_op jit(solution)/shard_map/ppermute | solution.py:556
  59.0 0.8 copy-start
  97.9 19.6 %collective-permute-start.8 = (s32[152,512]{1,0:T(8,128)}, s32[152,512]{1,0:T(8,128)S(1)}, u32[]{:S(2)}, u32[]{:S(2)}) collective-permute-start(s32[152,512]{1,0:T(8,128)} %get-tuple-element.20), channel_id=1, source_target_pairs={{0,16},{16,0},{1,17},{17,1},{2,18},{18,2},{3,19},{19,3},{4,20},{20... | collective-permute-start | bytes 933896 | tf_op jit(solution)/shard_map/ppermute | solution.py:556
  116.8 9.5 %collective-permute-start.9 = (s32[152,512]{1,0:T(8,128)}, s32[152,512]{1,0:T(8,128)S(1)}, u32[]{:S(2)}, u32[]{:S(2)}) collective-permute-start(s32[152,512]{1,0:T(8,128)} %get-tuple-element.23), channel_id=1, source_target_pairs={{0,16},{16,0},{1,17},{17,1},{2,18},{18,2},{3,19},{19,3},{4,20},{20... | collective-permute-start | bytes 933896 | tf_op jit(solution)/shard_map/ppermute | solution.py:556
  117.5 0.7 copy-start.3
  126.3 0.7 copy-start.4

commit v5 on v4

--- a/solution.py
+++ b/solution.py
@@ -120,8 +120,38 @@
     )
 
 
-def sums_kernel(density, average, slope, out, cells):
+def sums_kernel(
+    average, slope, density, first, final, out, below, above, before, after, cells, send, receive
+):
     layers, rows, width = density.shape
+    los, sky = lax.axis_index("los"), lax.axis_index("sky")
+    los_count, sky_count = lax.axis_size("los"), lax.axis_size("sky")
+    barrier = pltpu.get_barrier_semaphore()
+    mesh = pl.DeviceIdType.MESH
+    for axis, me, count in (("los", los, los_count), ("sky", sky, sky_count)):
+        for shift in (1, count - 1):
+            pl.semaphore_signal(barrier, inc=1, device_id={axis: lax.rem(me + shift, count)}, device_id_type=mesh)
+    pl.semaphore_wait(barrier, 4)
+
+    def hop(source, target, i, axis, me, count, shift):
+        return pltpu.make_async_remote_copy(
+            src_ref=source,
+            dst_ref=target,
+            send_sem=send.at[i],
+            recv_sem=receive.at[i],
+            device_id={axis: lax.rem(me + shift, count)},
+            device_id_type=mesh,
+        )
+
+    onward = hop(density.at[layers - 1], below, 0, "los", los, los_count, 1)
+    back = hop(density.at[0], above, 1, "los", los, los_count, los_count - 1)
+    forth = hop(final, before, 2, "sky", sky, sky_count, 1)
+    prior = hop(first, after, 3, "sky", sky, sky_count, sky_count - 1)
+    has_next, has_prior = los < los_count - 1, los > 0
+    pl.when(has_next)(onward.start)
+    pl.when(has_prior)(back.start)
+    forth.start()
+    prior.start()
     deep = 16
     last = density[:, rows - deep : rows, :]
     head = density[:, 0:deep, :]
@@ -167,6 +197,12 @@
         return carry
 
     lax.fori_loop(0, rows // SUB, chunk, 0)
+    forth.wait()
+    prior.wait()
+    pl.when(has_next)(onward.wait_send)
+    pl.when(has_prior)(onward.wait_recv)
+    pl.when(has_prior)(back.wait_send)
+    pl.when(has_next)(back.wait_recv)
 
 
 def edge_kernel(
@@ -215,8 +251,8 @@
         v0, v1 = [low[i, here, :].astype(jnp.float32) for i in range(2)]
         v6, v7 = [high[i, here, :].astype(jnp.float32) for i in range(2)]
         under, over = below[here, :].astype(jnp.float32), above[here, :].astype(jnp.float32)
-        tilt_z = tilt_z + slope[0] * median0(v1 - v0, keep[0] * (v0 - under))
-        tilt_z = tilt_z + slope[slope.shape[0] - 1] * median0(keep[1] * (over - v7), v7 - v6)
+        tilt_z = tilt_z + slope[0] * median0(v1 - v0, jnp.where(keep[0] > 0.0, v0 - under, 0.0))
+        tilt_z = tilt_z + slope[slope.shape[0] - 1] * median0(jnp.where(keep[1] > 0.0, over - v7, 0.0), v7 - v6)
         at = lax.broadcasted_iota(jnp.int32, (deep, width), 0) + start
         tilt_x = tilt_x + jnp.where(at == 0, fix_first, 0.0) + jnp.where(at == rows - 1, fix_last, 0.0)
         ours = pl.ds(pl.multiple_of(start + SUB, SUB), deep)
@@ -518,7 +554,7 @@
     out[:, width // 2 :] = totals[1]
 
 
-def call(kernel, shapes, specs, scratch=(), work=1, grid=(), types=jnp.float32):
+def call(kernel, shapes, specs, scratch=(), work=1, grid=(), types=jnp.float32, number=None):
     if not isinstance(types, tuple):
         types = jax.tree.map(lambda shape: types, shapes, is_leaf=lambda s: isinstance(s[0], int))
     return pl.pallas_call(
@@ -531,7 +567,9 @@
         out_specs=jax.tree.map(lambda shape: VMEM, shapes, is_leaf=lambda s: isinstance(s[0], int)),
         scratch_shapes=list(scratch),
         cost_estimate=pl.CostEstimate(flops=work, bytes_accessed=work, transcendentals=0),
-        compiler_params=pltpu.CompilerParams(vmem_limit_bytes=60 * 1024 * 1024),
+        compiler_params=pltpu.CompilerParams(
+            vmem_limit_bytes=60 * 1024 * 1024, collective_id=number, has_side_effects=number is not None
+        ),
     )
 
 
@@ -547,30 +585,31 @@
     groups = classes // los_count
     part = LANES // sky_count
     place = jnp.stack([los, sky]).astype(jnp.int32)
-    onward = [(i, i + 1) for i in range(los_count - 1)]
-    back = [(i + 1, i) for i in range(los_count - 1)]
     ring = [(i, (i + 1) % sky_count) for i in range(sky_count)]
     gnir = [((i + 1) % sky_count, i) for i in range(sky_count)]
 
     def to_shift(values, shift):
         return lax.ppermute(values, "los", [(i, (i + shift) % los_count) for i in range(los_count)])
 
-    below = lax.ppermute(density[layers - 1], "los", onward)
-    above = lax.ppermute(density[0], "los", back)
     first, second = density[:, 0, :], density[:, 1, :]
     former, final = density[:, rows - 2, :], density[:, rows - 1, :]
-    before = lax.ppermute(final, "sky", ring)
-    after = lax.ppermute(first, "sky", gnir)
     average = 0.5 * (weight_low + weight_high)
     slope = 0.125 * (weight_high - weight_low)
     keep = jnp.stack([los > 0, los < los_count - 1]).astype(jnp.float32)
-    sums = call(
+    half = jnp.bfloat16
+    sums, below, above, before, after = call(
         sums_kernel,
-        (4, rows, width),
-        [VMEM, SMEM, SMEM],
-        [pltpu.VMEM((layers, rows + 2 * SUB, width), jnp.float32)],
+        ((4, rows, width), (rows, width), (rows, width), (layers, width), (layers, width)),
+        [SMEM, SMEM] + [VMEM] * 3,
+        [
+            pltpu.VMEM((layers, rows + 2 * SUB, width), jnp.float32),
+            pltpu.SemaphoreType.DMA((4,)),
+            pltpu.SemaphoreType.DMA((4,)),
+        ],
         work=40_000_000,
-    )(density, average, slope)
+        types=(jnp.float32, half, half, half, half),
+        number=3,
+    )(average, slope, density, first, final)
     two = (2, rows, width)
     folded, rims = call(
         edge_kernel,

time: 130 us -> 130 us (level)
  starting transfers between devices: 19.9 us -> 8.53 us
  Pallas kernels: 84.2 us -> 92.6 us
  waiting for transfers between devices: 11 us -> 15.8 us
  local copies, waits for them, and re-layouts: 10.1 us -> 8.45 us
    ppermute x4 -> x0, starting transfers between devices: 10.7 us -> none  [the longest x1 4.9 us: body(): below = lax.ppermute(density[layers - 1], 'los', onward)]
    pallas_call x1, Pallas kernels: 15.5 us -> 21.4 us  [body(): call(sums_kernel, ((4, rows, width), (rows, width), (rows, width), (layer...]
    ppermute x4, waiting for transfers between devices: 9.64 us -> 14.4 us  [to_shift(): lax.ppermute(values, 'los', [(i, (i + shift) % los_count) for i in range(...]
    pallas_call x3, Pallas kernels: 38.2 us -> 40.7 us  [exchange(): pl.pallas_call(exchange_kernel, out_shape=jax.ShapeDtypeStruct(values.sha...]
    unnamed x22 -> x8, local copies, waits for them, and re-layouts: 3.26 us -> 2.21 us
  transfers between devices with their start and end apart: 10 -> 6, of which waited for: 3 -> 4; matrix products, arithmetic and copies ran while one was open for 5% -> 1% of each run, Pallas kernels for 27% -> 2%
where the time goes in v5:
time: 130 us; the launch traced here: 129 us
  Pallas kernels  92.6 us (71%)
  waiting for transfers between devices  15.8 us (12%)
  starting transfers between devices  8.53 us (7%)
  local copies, waits for them, and re-layouts  8.45 us (6%)
  other arithmetic  3.04 us (2%)
    pallas_call x3, Pallas kernels, exchange(): pl.pallas_call(exchange_kernel, out_shape=jax.ShapeDtypeStruct(values.sha...  40.7 us
    pallas_call x1, Pallas kernels, body(): call(sums_kernel, ((4, rows, width), (rows, width), (rows, width), (layer...  21.4 us
    ppermute x4, waiting for transfers between devices, to_shift(): lax.ppermute(values, 'los', [(i, (i + shift) % los_count) for i in range(...  14.4 us
    pallas_call x1, Pallas kernels, body(): call(edge_kernel, ((los_count, groups, 2, rows, LANES), (2, classes, 2, L...  8.88 us
    pallas_call x2, Pallas kernels, body(): call(functools.partial(plane_kernel, groups), shapes, [SMEM, VMEM, VMEM,...  7.95 us
    pallas_call x1, Pallas kernels, body(): call(functools.partial(column_kernel, length, layers * los_count, groups)...  5.32 us
    ppermute x1, starting transfers between devices, body(): from_after = lax.ppermute(rims[0], 'sky', gnir)  4.44 us
    pallas_call x1, Pallas kernels, body(): call(row_kernel, block, [SMEM] + [VMEM] * (los_count + 2), types=jnp.int32)  4.16 us
  transfers between devices with their start and end apart: 6, of which 4 were waited for; matrix products, arithmetic and copies ran while one was open for 1% of the time, Pallas kernels for 2%

profile of v5, /device:TPU:0, one launch (start us, length us, event | category | flops | bytes accessed | tf_op | source)
XLA Modules:
  0.0 129.1 jit_solution(1177355187116399524)
XLA Ops:
  0.6 1.4 %fusion.3 = (bf16[8,1,2048]{2,1,0:T(2,128)(2,1)S(1)}, bf16[8,1,2048]{2,1,0:T(2,128)(2,1)S(1)}, bf16[8,1,2048]{2,1,0:T(2,128)(2,1)S(1)}, bf16[8,1,2048]{2,1,0:T(2,128)(2,1)S(1)}) fusion(bf16[8,128,2048]{2,1,0:T(8,128)(2,1)} %high.1), kind=kLoop, calls=%fused_computation.19 | loop fusion | bytes 262144 | tf_op jit(solution)/shard_map/slice | solution.py:595
  2.1 1.2 subtract_multiply_fusion
  3.3 0.0 copy-start.3
  3.3 0.7 copy.14.column_average
  3.9 0.7 copy_bitcast_fusion.2
  4.6 0.6 add_convert_fusion.keep
  5.3 0.6 pad_add_fusion.place
  5.9 0.7 copy_bitcast_fusion
  6.5 0.0 copy-done.3
  6.5 21.4 %shard_map.95 = (f32[4,128,2048]{2,1,0:T(8,128)}, bf16[128,2048]{1,0:T(8,128)(2,1)}, bf16[128,2048]{1,0:T(8,128)(2,1)}, bf16[8,2048]{1,0:T(8,128)(2,1)}, bf16[8,2048]{1,0:T(8,128)(2,1)}) custom-call(f32[8]{0:T(128)} %copy-done.3, f32[8]{0:T(128)} %get-tuple-element.42.slope, bf16[8,128,2048]{2,1,0:T(8,128)(2,1)} %high.1, ...), custom_call_target="tpu_custom_call" | custom-call | flops 40000000 | bytes 40000000 | tf_op jit(solution)/shard_map/pallas_call | solution.py:600
  28.0 8.9 %shard_map.96 = (f32[2,4,2,128,128]{4,3,2,1,0:T(8,128)}, f32[2,8,2,128]{3,2,1,0:T(2,128)}) custom-call(f32[4,128,2048]{2,1,0:T(8,128)} %get-tuple-element.18.sums, bf16[8,128,2048]{2,1,0:T(8,128)(2,1)} %high.1, bf16[8,128,2048]{2,1,0:T(8,128)(2,1)} %high.1, bf16[128,2048]{1,0:T(8,128)(2,1)} %get-tuple-element.19.below, ...), custom_call_target="tpu_custom_call" | custom-call | flops 1 | bytes 1 | tf_op jit(solution)/shard_map/pallas_call | solution.py:614
  36.9 2.1 %slice_bitcast_fusion = (f32[4,2,128,128]{3,2,1,0:T(8,128)S(1)}, f32[4,2,128,128]{3,2,1,0:T(8,128)}) fusion(f32[2,4,2,128,128]{4,3,2,1,0:T(8,128)} %get-tuple-element.23), kind=kLoop, calls=%fused_computation | loop fusion | bytes 2097152 | tf_op jit(solution)/shard_map/squeeze | solution.py:634
  38.9 1.5 %collective-permute-start = (f32[4,2,128,128]{3,2,1,0:T(8,128)S(1)}, f32[4,2,128,128]{3,2,1,0:T(8,128)S(1)}, u32[]{:S(2)}, u32[]{:S(2)}) collective-permute-start(f32[4,2,128,128]{3,2,1,0:T(8,128)S(1)} %get-tuple-element.38), channel_id=1, source_target_pairs={{0,16},{16,0},{1,17},{17,1},{2,18},{18,2},{3,19},{19,3},{4,20},{20... | collective-permute-start | bytes 1572872 | tf_op jit(solution)/shard_map/ppermute | solution.py:592
  40.4 0.7 slice_bitcast_fusion.2
  41.2 0.0 collective-permute-start.1
  41.2 4.4 %collective-permute-start.2 = (f32[8,2,128]{2,1,0:T(2,128)S(1)}, f32[8,2,128]{2,1,0:T(2,128)S(1)}, u32[]{:S(2)}, u32[]{:S(2)}) collective-permute-start(f32[8,2,128]{2,1,0:T(2,128)S(1)} %get-tuple-element.40), channel_id=1, source_target_pairs={{1,0},{2,1},{3,2},{4,3},{5,4},{6,5},{7,6},{8,7},{9,8},{10,9},{11,1... | collective-permute-start | bytes 24584 | tf_op jit(solution)/shard_map/ppermute | solution.py:636
  45.6 1.3 %collective-permute-done.1 = f32[8,2,128]{2,1,0:T(2,128)S(1)} collective-permute-done((f32[8,2,128]{2,1,0:T(2,128)S(1)}, f32[8,2,128]{2,1,0:T(2,128)S(1)}, u32[]{:S(2)}, u32[]{:S(2)}) %collective-permute-start.1) | collective-permute-done | bytes 8224 | tf_op jit(solution)/shard_map/ppermute | solution.py:635
  46.9 0.0 collective-permute-done.2
  47.0 0.6 collective-permute-start.3
  47.5 3.1 %collective-permute-done.3 = f32[2,4,2,128]{3,2,1,0:T(2,128)S(1)} collective-permute-done((f32[2,4,2,128]{3,2,1,0:T(2,128)S(1)}, f32[2,4,2,128]{3,2,1,0:T(2,128)S(1)}, u32[]{:S(2)}, u32[]{:S(2)}) %collective-permute-start.3) | collective-permute-done | bytes 8224 | tf_op jit(solution)/shard_map/ppermute | solution.py:592
  50.7 0.6 fusion.2.refs_1_
  51.3 0.0 collective-permute-done.refs_0_
  51.3 0.0 copy-start
  51.3 0.8 copy-done
  52.1 4.2 %shard_map.97.source = s32[16,40,128]{2,1,0:T(8,128)} custom-call(s32[2]{0:T(128)} %pad_add_fusion.place, f32[4,2,128,128]{3,2,1,0:T(8,128)} %get-tuple-element.39.own, f32[4,2,128,128]{3,2,1,0:T(8,128)} %copy-done, f32[2,4,2,128]{3,2,1,0:T(2,128)} %fusion.2.refs_1_, f32[8,256,256]{2,1,0:T(8,128)} %constant.44.clone.refs_2_.table), custom_call_target="tpu_custom_call" | custom-call | flops 1 | bytes 1 | tf_op jit(solution)/shard_map/pallas_call | solution.py:647
  56.2 14.0 %shard_map.98.modes = s32[16,40,128]{2,1,0:T(8,128)} custom-call(s32[16,40,128]{2,1,0:T(8,128)} %shard_map.97.source), custom_call_target="tpu_custom_call" | custom-call | tf_op jit(solution)/shard_map/pallas_call | solution.py:531
  70.2 5.3 %shard_map.99 = (s32[16,40,128]{2,1,0:T(8,128)}, s32[16,40,128]{2,1,0:T(8,128)}) custom-call(s32[2]{0:T(128)} %pad_add_fusion.place, s32[16,40,128]{2,1,0:T(8,128)} %shard_map.98.modes, f32[256,256]{1,0:T(8,128)} %constant.45.clone.forward, f32[16,2,128]{2,1,0:T(2,128)} %constant.46.clone.twist), custom_call_target="tpu_custom_call" | custom-call | flops 1 | bytes 1 | tf_op jit(solution)/shard_map/pallas_call | solution.py:652
  75.5 13.1 %shard_map.100.modes = s32[16,40,128]{2,1,0:T(8,128)} custom-call(s32[16,40,128]{2,1,0:T(8,128)} %get-tuple-element.26.source), custom_call_target="tpu_custom_call" | custom-call | tf_op jit(solution)/shard_map/pallas_call | solution.py:531
  88.7 4.0 %shard_map.101 = (f32[128,1024]{1,0:T(8,128)}, s32[152,512]{1,0:T(8,128)}) custom-call(s32[2]{0:T(128)} %pad_add_fusion.place, s32[16,40,128]{2,1,0:T(8,128)} %shard_map.100.modes, f32[8,256,256]{2,1,0:T(8,128)} %constant.44.clone.refs_2_.table, f32[8,32]{1,0:T(8,128)} %constant.47.clone.mix), custom_call_target="tpu_custom_call" | custom-call | flops 1 | bytes 1 | tf_op jit(solution)/shard_map/pallas_call | solution.py:667
  92.6 13.6 %shard_map.103.modes = s32[16,40,128]{2,1,0:T(8,128)} custom-call(s32[16,40,128]{2,1,0:T(8,128)} %get-tuple-element.31.source), custom_call_target="tpu_custom_call" | custom-call | tf_op jit(solution)/shard_map/pallas_call | solution.py:531
  106.2 4.0 %shard_map.104 = (f32[128,1024]{1,0:T(8,128)}, s32[152,512]{1,0:T(8,128)}) custom-call(s32[2]{0:T(128)} %pad_add_fusion.place, s32[16,40,128]{2,1,0:T(8,128)} %shard_map.103.modes, f32[8,256,256]{2,1,0:T(8,128)} %constant.44.clone.refs_2_.table, f32[8,32]{1,0:T(8,128)} %constant.47.clone.mix), custom_call_target="tpu_custom_call" | custom-call | flops 1 | bytes 1 | tf_op jit(solution)/shard_map/pallas_call | solution.py:667
  110.2 0.3 collective-permute-start.5
  110.5 1.8 %collective-permute-start.4 = (s32[152,512]{1,0:T(8,128)}, s32[152,512]{1,0:T(8,128)S(1)}, u32[]{:S(2)}, u32[]{:S(2)}) collective-permute-start(s32[152,512]{1,0:T(8,128)} %get-tuple-element.30), channel_id=1, source_target_pairs={{0,16},{16,0},{1,17},{17,1},{2,18},{18,2},{3,19},{19,3},{4,20},{20... | collective-permute-start | bytes 933896 | tf_op jit(solution)/shard_map/ppermute | solution.py:592
  112.2 8.4 %collective-permute-done.5.refs_0_ = s32[152,512]{1,0:T(8,128)S(1)} collective-permute-done((s32[152,512]{1,0:T(8,128)}, s32[152,512]{1,0:T(8,128)S(1)}, u32[]{:S(2)}, u32[]{:S(2)}) %collective-permute-start.5) | collective-permute-done | bytes 311328 | tf_op jit(solution)/shard_map/ppermute | solution.py:592
  120.7 0.0 copy-start.2
  120.7 0.7 copy-done.2
  121.4 2.1 %shard_map.105 = f32[128,1024]{1,0:T(8,128)} custom-call(f32[128,1024]{1,0:T(8,128)} %get-tuple-element.32.own, s32[152,512]{1,0:T(8,128)} %copy-done.2), custom_call_target="tpu_custom_call" | custom-call | flops 1 | bytes 1 | tf_op jit(solution)/shard_map/pallas_call | solution.py:677
  123.4 2.9 %collective-permute-done.4.refs_0_ = s32[152,512]{1,0:T(8,128)S(1)} collective-permute-done((s32[152,512]{1,0:T(8,128)}, s32[152,512]{1,0:T(8,128)S(1)}, u32[]{:S(2)}, u32[]{:S(2)}) %collective-permute-start.4) | collective-permute-done | bytes 311328 | tf_op jit(solution)/shard_map/ppermute | solution.py:592
  126.3 0.0 copy-start.1
  126.3 0.7 copy-done.1
  127.0 2.1 %shard_map.102 = f32[128,1024]{1,0:T(8,128)} custom-call(f32[128,1024]{1,0:T(8,128)} %get-tuple-element.29.own, s32[152,512]{1,0:T(8,128)} %copy-done.1), custom_call_target="tpu_custom_call" | custom-call | flops 1 | bytes 1 | tf_op jit(solution)/shard_map/pallas_call | solution.py:677
  (1 shorter events, 0.0 us)
Async XLA Ops:
  3.3 3.3 %copy-start.3 = (f32[8]{0:T(128)}, f32[8]{0:T(128)S(1)}, u32[]{:S(2)}) copy-start(f32[8]{0:T(128)S(1)} %get-tuple-element.43.average) | copy-start | bytes 100
  38.9 12.3 %collective-permute-start = (f32[4,2,128,128]{3,2,1,0:T(8,128)S(1)}, f32[4,2,128,128]{3,2,1,0:T(8,128)S(1)}, u32[]{:S(2)}, u32[]{:S(2)}) collective-permute-start(f32[4,2,128,128]{3,2,1,0:T(8,128)S(1)} %get-tuple-element.38), channel_id=1, source_target_pairs={{0,16},{16,0},{1,17},{17,1},{2,18},{18,2},{3,19},{19,3},{4,20},{20... | collective-permute-start | bytes 1572872 | tf_op jit(solution)/shard_map/ppermute | solution.py:592
  41.2 5.8 %collective-permute-start.1 = (f32[8,2,128]{2,1,0:T(2,128)S(1)}, f32[8,2,128]{2,1,0:T(2,128)S(1)}, u32[]{:S(2)}, u32[]{:S(2)}) collective-permute-start(f32[8,2,128]{2,1,0:T(2,128)S(1)} %get-tuple-element.41), channel_id=1, source_target_pairs={{0,1},{1,2},{2,3},{3,4},{4,5},{5,6},{6,7},{7,8},{8,9},{9,10},{10,1... | collective-permute-start | bytes 24584 | tf_op jit(solution)/shard_map/ppermute | solution.py:635
  41.2 5.8 %collective-permute-start.2 = (f32[8,2,128]{2,1,0:T(2,128)S(1)}, f32[8,2,128]{2,1,0:T(2,128)S(1)}, u32[]{:S(2)}, u32[]{:S(2)}) collective-permute-start(f32[8,2,128]{2,1,0:T(2,128)S(1)} %get-tuple-element.40), channel_id=1, source_target_pairs={{1,0},{2,1},{3,2},{4,3},{5,4},{6,5},{7,6},{8,7},{9,8},{10,9},{11,1... | collective-permute-start | bytes 24584 | tf_op jit(solution)/shard_map/ppermute | solution.py:636
  47.0 3.7 %collective-permute-start.3 = (f32[2,4,2,128]{3,2,1,0:T(2,128)S(1)}, f32[2,4,2,128]{3,2,1,0:T(2,128)S(1)}, u32[]{:S(2)}, u32[]{:S(2)}) collective-permute-start(f32[2,4,2,128]{3,2,1,0:T(2,128)S(1)} %fusion), channel_id=1, source_target_pairs={{0,16},{16,0},{1,17},{17,1},{2,18},{18,2},{3,19},{19,3},{4,20},{20... | collective-permute-start | bytes 24584 | tf_op jit(solution)/shard_map/ppermute | solution.py:592
  51.3 0.8 copy-start
  110.2 10.4 %collective-permute-start.5 = (s32[152,512]{1,0:T(8,128)}, s32[152,512]{1,0:T(8,128)S(1)}, u32[]{:S(2)}, u32[]{:S(2)}) collective-permute-start(s32[152,512]{1,0:T(8,128)} %get-tuple-element.33), channel_id=1, source_target_pairs={{0,16},{16,0},{1,17},{17,1},{2,18},{18,2},{3,19},{19,3},{4,20},{20... | collective-permute-start | bytes 933896 | tf_op jit(solution)/shard_map/ppermute | solution.py:592
  110.5 15.9 %collective-permute-start.4 = (s32[152,512]{1,0:T(8,128)}, s32[152,512]{1,0:T(8,128)S(1)}, u32[]{:S(2)}, u32[]{:S(2)}) collective-permute-start(s32[152,512]{1,0:T(8,128)} %get-tuple-element.30), channel_id=1, source_target_pairs={{0,16},{16,0},{1,17},{17,1},{2,18},{18,2},{3,19},{19,3},{4,20},{20... | collective-permute-start | bytes 933896 | tf_op jit(solution)/shard_map/ppermute | solution.py:592
  120.7 0.7 copy-start.2
  126.3 0.7 copy-start.1
